TPU v7x, 32 devices: a whole 2x2x4 slice. The times are simulated.
32 devices in a mesh: groups: 2 (over y), seq: 4 (over z), tensor: 2 (over x), sub: 2 (over core).
Axes of the slice: x: 2, y: 2, z: 4, core: 2. Of those that a mesh axis runs over, the one named last changes fastest.
Arguments:
- activations: bfloat16 [4096, 4096], P(('groups', 'seq'), ('tensor', 'sub')), parts along dimension 0, may hold values from -18 to 18
- conv_weight: bfloat16 [512, 4096], P(None, ('tensor', 'sub')), may hold values from -0.25 to 0.25
- query_weight: bfloat16 [4096, 2048], P('seq', ('tensor', 'sub')), may hold values from -0.09375 to 0.09375
- key_weight: bfloat16 [4096, 2048], P('seq', ('tensor', 'sub')), may hold values from -0.09375 to 0.09375
- value_weight: bfloat16 [4096, 2048], P('seq', ('tensor', 'sub')), may hold values from -0.09375 to 0.09375
- segment_for_slot: int32 [16], P('groups'), parts along dimension 0, may hold values from 0 to 7, each once
- book_length: int32 [2], P('groups'), parts along dimension 0, may hold values from 1024 to 2048
Outputs:
- context: bfloat16 [4096, 2048], P(('groups', 'seq'), ('tensor', 'sub')), parts along dimension 0
There are 2 independent parts, one for each index of `groups`. A program takes and returns all parts, laid end to end along the dimension named above; an argument that names none is the same for every part. Nothing has to cross between parts.
Inputs may be any that keep to these rules, and one draw needn't show every extreme that they name: `segment_for_slot`: each segment appears in exactly one slot.
All inputs are finite; a program needn't handle non-finite values.
Results may differ from a plain program's by a relative error of at most 0.012.
The roundings to bfloat16 on the way count: a program that leaves them out, or rounds other values in their place, can miss the bound.
Values may be sent and summed in bfloat16 or wider, within the bound.
No kernel may reach another device: no remote copies, remote signals or barrier semaphores. Data moves between devices by JAX's collectives and lax.ppermute only.
A program may use at most 64 MiB of HBM per device.

v0:
```python
import jax
import jax.numpy as jnp
from jax import lax
from jax.sharding import PartitionSpec as P

HD = 128
CG = 128
RATE = 4
SLOTS = 2
SEG = 256
MEM = 64


def compress_rows(local_rows, conv_local):
    count_rows, channels = local_rows.shape
    groups = channels // CG
    shaped = local_rows.reshape(count_rows // RATE, RATE, groups, CG)
    kernel = conv_local.reshape(RATE, CG, groups, CG)
    mixed_out = jnp.einsum("mtgc,tcgo->mgo", shaped, kernel, preferred_element_type=jnp.float32)
    return mixed_out.reshape(count_rows // RATE, channels).astype(jnp.bfloat16)


def add_product(source, weight_rows):
    return jnp.dot(source, weight_rows, preferred_element_type=jnp.float32)


def local_attention(queries, keys_here, values_here):
    total_rows, head_count, head_dim = queries.shape
    slot_count = total_rows // SEG
    shaped_q = queries.reshape(slot_count, SEG, head_count, head_dim)
    shaped_k = keys_here.reshape(slot_count, SEG, head_count, head_dim)
    shaped_v = values_here.reshape(slot_count, SEG, head_count, head_dim)
    scores = jnp.einsum(
        "asnd,atnd->asnt", shaped_q, shaped_k, preferred_element_type=jnp.float32
    ) * HD ** (-0.5)
    causal = jnp.arange(SEG, dtype=jnp.int32)[:, None] >= jnp.arange(SEG, dtype=jnp.int32)[None, :]
    scores = jnp.where(causal[None, :, None, :], scores, -jnp.inf)
    row_best = jnp.max(scores, axis=3)
    weights = jnp.exp(scores - row_best[..., None])
    denominator = jnp.sum(weights, axis=3)
    weighted_numerator = jnp.einsum(
        "asnt,atnd->asnd",
        weights.astype(jnp.bfloat16),
        shaped_v,
        preferred_element_type=jnp.float32,
    )
    return (
        row_best.reshape(total_rows, head_count),
        denominator.reshape(total_rows, head_count),
        weighted_numerator.reshape(total_rows, head_count, head_dim),
    )


def memory_step(state, pieces, queries, row_segment, segment_for_slot):
    keys_in, values_in = pieces
    count_keys = keys_in.shape[0]
    total_rows, head_count, head_dim = queries.shape
    key_slot = jnp.arange(count_keys, dtype=jnp.int32) // MEM
    slot_ids = jnp.arange(segment_for_slot.shape[0], dtype=jnp.int32)
    key_segment = jnp.sum(
        jnp.where(key_slot[:, None] == slot_ids[None, :], segment_for_slot[None, :], 0), axis=1
    )
    row_best, denominator, weighted_numerator = state
    shaped_keys = keys_in.reshape(count_keys, head_count, head_dim)
    shaped_values = values_in.reshape(count_keys, head_count, head_dim)
    scores = jnp.einsum(
        "rnd,knd->rnk", queries, shaped_keys, preferred_element_type=jnp.float32
    ) * HD ** (-0.5)
    allowed = key_segment[None, None, :] < row_segment[:, None, None]
    scores = jnp.where(allowed, scores, -jnp.inf)
    new_best = jnp.maximum(row_best, jnp.max(scores, axis=2))
    weights = jnp.exp(scores - new_best[:, :, None])
    factor = jnp.exp(row_best - new_best)
    denominator = denominator * factor + jnp.sum(weights, axis=2)
    weighted_numerator = weighted_numerator * factor[:, :, None] + jnp.einsum(
        "rnk,knd->rnd",
        weights.astype(jnp.bfloat16),
        shaped_values,
        preferred_element_type=jnp.float32,
    )
    return (new_best, denominator, weighted_numerator)


def on_device(
    activations, conv_weight, query_weight, key_weight, value_weight, segment_for_slot, book_length
):
    compressed_local = compress_rows(activations, conv_weight)
    full_rows, full_compressed = (
        lax.all_gather(activations, ("tensor", "sub"), axis=1, tiled=True),
        lax.all_gather(compressed_local, ("tensor", "sub"), axis=1, tiled=True),
    )
    total_rows = full_rows.shape[0]
    local_width = query_weight.shape[1]
    head_count = local_width // HD
    shard_index = lax.axis_index("seq")
    my_segments = lax.dynamic_slice_in_dim(segment_for_slot, shard_index * SLOTS, SLOTS, 0)
    row_segment = jnp.repeat(my_segments, SEG, total_repeat_length=total_rows)
    query_rows = lax.all_gather(query_weight, "seq", axis=0, tiled=True)
    key_matrix_rows = lax.all_gather(key_weight, "seq", axis=0, tiled=True)
    value_rows = lax.all_gather(value_weight, "seq", axis=0, tiled=True)
    queries = add_product(full_rows, query_rows).astype(jnp.bfloat16)
    keys_here = add_product(full_rows, key_matrix_rows).astype(jnp.bfloat16)
    values_here = add_product(full_rows, value_rows).astype(jnp.bfloat16)
    keys_mem = add_product(full_compressed, key_matrix_rows).astype(jnp.bfloat16)
    values_mem = add_product(full_compressed, value_rows).astype(jnp.bfloat16)
    shaped_q = queries.reshape(total_rows, head_count, HD)
    state = local_attention(
        shaped_q,
        keys_here.reshape(total_rows, head_count, HD),
        values_here.reshape(total_rows, head_count, HD),
    )
    state = memory_step(
        state,
        (
            lax.all_gather(keys_mem, "seq", axis=0, tiled=True),
            lax.all_gather(values_mem, "seq", axis=0, tiled=True),
        ),
        shaped_q,
        row_segment,
        segment_for_slot,
    )
    row_best, denominator, weighted_numerator = state
    result = (weighted_numerator / denominator[:, :, None]).reshape(total_rows, local_width)
    position = row_segment * SEG + jnp.arange(total_rows, dtype=jnp.int32) % SEG
    result = jnp.where((position < book_length[0])[:, None], result, 0.0)
    return result.astype(jnp.bfloat16)


def solution(mesh):
    placed = (
        P(("groups", "seq"), ("tensor", "sub")),
        P(None, ("tensor", "sub")),
        P("seq", ("tensor", "sub")),
        P("seq", ("tensor", "sub")),
        P("seq", ("tensor", "sub")),
        P("groups"),
        P("groups"),
    )
    return jax.shard_map(
        on_device,
        mesh=mesh,
        in_specs=placed,
        out_specs=P(("groups", "seq"), ("tensor", "sub")),
        check_vma=False,
    )
```

profile of v0, /device:TPU:0, one launch (start us, length us, event | category | flops | bytes accessed | tf_op | source)
XLA Modules:
  0.0 350.5 jit_solution(3054702752094949203)
XLA Ops:
  6.5 0.0 copy-start
  6.5 0.0 all-gather.6.cloned.1.call-start
  6.5 0.7 all-gather.6.cloned.1.call-update
  7.3 0.0 all-gather.10.cloned.1.call-start
  7.3 0.7 all-gather.10.cloned.1.call-update
  8.0 0.0 all-gather.12.cloned.1.call-start
  8.1 0.7 all-gather.12.cloned.1.call-update
  8.7 0.0 all-gather.14.cloned.1.call-start
  8.8 0.0 copy-start.5
  8.8 0.0 copy-start.4
  8.8 1.5 copy.64
  10.3 0.0 copy-done
  10.3 0.3 copy.65
  10.6 1.7 fusion.17
  12.3 0.0 all-gather.14.cloned.1.call-update
  12.3 0.0 all-gather.8.cloned.1.call-start
  12.4 0.5 all-gather.8.cloned.1.call-update
  13.5 0.0 copy-done.5
  13.6 0.1 dynamic_slice.3
  13.6 0.6 fusion.41
  14.2 0.1 select_reduce_fusion
  14.3 0.0 copy-done.4
  14.3 1.3 fusion.32
  15.6 1.3 broadcast_select_fusion
  16.9 0.2 broadcast_compare_fusion
  17.1 29.0 %all-gather.6.cloned.1.call-done = bf16[512,4096]{1,0:T(8,128)(2,1)} async-done(((bf16[512,1024]{1,0:T(8,128)(2,1)}), bf16[512,4096]{1,0:T(8,128)(2,1)}) %all-gather.6.cloned.1.call-update) | async-done | bytes 4194320 | tf_op jit(solution)/shard_map/all_gather | solution.py:89
  46.1 82.4 %all-gather.10.cloned.1.call-done = bf16[4096,512]{1,0:T(8,128)(2,1)} async-done(((bf16[1024,512]{1,0:T(8,128)(2,1)}), bf16[4096,512]{1,0:T(8,128)(2,1)}) %all-gather.10.cloned.1.call-update) | async-done | bytes 4194320 | tf_op jit(solution)/shard_map/all_gather | solution.py:99
  128.5 5.8 %convolution_convert_fusion.1 = bf16[512,512]{1,0:T(8,128)(2,1)S(1)} fusion(bf16[512,4096]{1,0:T(8,128)(2,1)} %all-gather.6.cloned.1.call-done, bf16[4096,512]{1,0:T(8,128)(2,1)} %all-gather.10.cloned.1.call-done), kind=kOutput, calls=%fused_computation.18 | convolution fusion | flops 2147745792 | bytes 8912896 | tf_op jit(solution)/shard_map/dot_general | solution.py:24
  134.3 0.1 reshape_reshape.10
  134.4 75.0 %all-gather.12.cloned.1.call-done = bf16[4096,512]{1,0:T(8,128)(2,1)} async-done(((bf16[1024,512]{1,0:T(8,128)(2,1)}), bf16[4096,512]{1,0:T(8,128)(2,1)}) %all-gather.12.cloned.1.call-update) | async-done | bytes 4194320 | tf_op jit(solution)/shard_map/all_gather | solution.py:98
  209.4 5.8 %convolution_convert_fusion = bf16[512,512]{0,1:T(8,128)(2,1)S(1)} fusion(bf16[512,4096]{1,0:T(8,128)(2,1)} %all-gather.6.cloned.1.call-done, bf16[4096,512]{1,0:T(8,128)(2,1)} %all-gather.12.cloned.1.call-done), kind=kOutput, calls=%fused_computation.17 | convolution fusion | flops 2147745792 | bytes 8912896 | tf_op jit(solution)/shard_map/dot_general | solution.py:24
  215.2 0.0 copy-start.3
  215.3 0.1 reshape_reshape.11
  215.4 10.7 %all-gather.14.cloned.1.call-done = bf16[128,4096]{0,1:T(8,128)(2,1)} async-done(((bf16[128,1024]{0,1:T(8,128)(2,1)}), bf16[128,4096]{0,1:T(8,128)(2,1)}) %all-gather.14.cloned.1.call-update) | async-done | bytes 1048592 | tf_op jit(solution)/shard_map/all_gather | solution.py:90
  226.1 3.3 convolution_convert_fusion.4
  229.4 21.4 %all_gather.26 = bf16[512,512]{1,0:T(8,128)(2,1)} all-gather(bf16[128,512]{1,0:T(8,128)(2,1)S(1)} %convolution_convert_fusion.4), channel_id=1, replica_groups=mesh['groups'=2,'seq'=4,'tensor'=2,'sub'=2] {'seq'}, dimensions={0}, use_global_device_ids=true | all-gather | bytes 655360 | tf_op jit(solution)/shard_map/all_gather | solution.py:115
  250.8 61.4 %all-gather.8.cloned.1.call-done = bf16[4096,512]{1,0:T(8,128)(2,1)} async-done(((bf16[1024,512]{1,0:T(8,128)(2,1)}), bf16[4096,512]{1,0:T(8,128)(2,1)}) %all-gather.8.cloned.1.call-update) | async-done | bytes 4194320 | tf_op jit(solution)/shard_map/all_gather | solution.py:100
  312.2 0.0 copy-done.3
  312.2 5.8 %convolution_convert_fusion.2 = bf16[512,512]{1,0:T(8,128)(2,1)S(1)} fusion(bf16[512,4096]{1,0:T(8,128)(2,1)} %all-gather.6.cloned.1.call-done, bf16[4096,512]{1,0:T(8,128)(2,1)} %all-gather.8.cloned.1.call-done), kind=kOutput, calls=%fused_computation.19 | convolution fusion | flops 2147745792 | bytes 8912896 | tf_op jit(solution)/shard_map/dot_general | solution.py:24
  318.0 0.1 reshape_reshape.9
  318.1 0.5 fusion.42
  318.6 0.3 fusion.9
  318.9 0.0 copy-start.1
  318.9 0.5 convolution_bitcast_fusion
  319.4 0.3 copy.49
  319.7 0.3 copy.54
  320.1 0.0 copy-done.1
  320.1 0.0 copy-start.2
  320.1 3.0 convolution_convert_fusion.3
  323.1 15.2 %all_gather.27 = bf16[512,512]{1,0:T(8,128)(2,1)S(1)} all-gather(bf16[128,512]{1,0:T(8,128)(2,1)S(1)} %convolution_convert_fusion.3), channel_id=1, replica_groups=mesh['groups'=2,'seq'=4,'tensor'=2,'sub'=2] {'seq'}, dimensions={0}, use_global_device_ids=true | all-gather | bytes 655360 | tf_op jit(solution)/shard_map/all_gather | solution.py:116
  338.4 0.2 copy.62
  338.6 0.0 copy-done.2
  338.6 1.9 fusion.2
  340.5 0.9 fusion
  341.4 1.4 fusion.22
  342.8 0.2 copy.57
  343.0 1.0 select_convert_fusion
  (4 shorter events, 0.0 us)
Async XLA Ops:
  6.5 3.8 %copy-start = (bf16[512,1024]{1,0:T(8,128)(2,1)S(1)}, bf16[512,1024]{1,0:T(8,128)(2,1)}, u32[]{:S(2)}) copy-start(bf16[512,1024]{1,0:T(8,128)(2,1)} %param.9) | copy-start | bytes 3145732
  6.5 39.6 %all-gather.6.cloned.1.call-start = ((), (), s32[]{:S(2)}) async-start(), calls=%async_computation | async-start | bytes 5242880 | tf_op jit(solution)/shard_map/all_gather | solution.py:89
  7.3 121.2 %all-gather.10.cloned.1.call-start = ((), (), s32[]{:S(2)}) async-start(), calls=%async_computation.2 | async-start | bytes 5242880 | tf_op jit(solution)/shard_map/all_gather | solution.py:99
  8.0 201.4 %all-gather.12.cloned.1.call-start = ((), (), s32[]{:S(2)}) async-start(), calls=%async_computation.3 | async-start | bytes 5242880 | tf_op jit(solution)/shard_map/all_gather | solution.py:98
  8.7 217.4 %all-gather.14.cloned.1.call-start = ((), (), s32[]{:S(2)}) async-start(), calls=%async_computation.4 | async-start | bytes 1310720 | tf_op jit(solution)/shard_map/all_gather | solution.py:90
  8.8 4.8 %copy-start.5 = (s32[8]{0:T(128)S(1)}, s32[8]{0:T(128)}, u32[]{:S(2)}) copy-start(s32[8]{0:T(128)} %param.14) | copy-start | bytes 100
  8.8 5.5 %copy-start.4 = (pred[512]{0:T(512)(128)(4,1)S(1)}, pred[512]{0:T(512)(128)(4,1)}, u32[]{:S(2)}) copy-start(pred[512]{0:T(512)(128)(4,1)} %constant.157) | copy-start | bytes 1540
  12.3 299.9 %all-gather.8.cloned.1.call-start = ((), (), s32[]{:S(2)}) async-start(), calls=%async_computation.1 | async-start | bytes 5242880 | tf_op jit(solution)/shard_map/all_gather | solution.py:100
  215.2 96.9 %copy-start.3 = (bf16[512,512]{0,1:T(8,128)(2,1)}, bf16[512,512]{0,1:T(8,128)(2,1)S(1)}, u32[]{:S(2)}) copy-start(bf16[512,512]{0,1:T(8,128)(2,1)S(1)} %convolution_convert_fusion) | copy-start | bytes 1572868
  318.9 1.2 copy-start.1
  320.1 18.4 %copy-start.2 = (bf16[512,512]{1,0:T(8,128)(2,1)S(1)}, bf16[512,512]{1,0:T(8,128)(2,1)}, u32[]{:S(2)}) copy-start(bf16[512,512]{1,0:T(8,128)(2,1)} %all_gather.26) | copy-start | bytes 1572868
Sparse Core Ops, SparseCore 0:
  8.9 37.1 all-gather.5
  47.7 80.7 all-gather.9
  130.1 79.2 all-gather.11
  210.8 15.2 all-gather.13
  227.5 84.6 all-gather.7
where the time goes:
time: 351 us
  waiting for transfers between devices  261 us (74%)
  blocking collectives  36.6 us (10%)
  matrix products  29.6 us (8%)
  between operations  14 us (4%)
  other arithmetic  5.11 us (1%)
  local copies, waits for them, and re-layouts  3.95 us (1%)
    all_gather x1, waiting for transfers between devices, on_device(): key_matrix_rows = lax.all_gather(key_weight, 'seq', axis=0, tiled=True)  82.4 us
    all_gather x1, waiting for transfers between devices, on_device(): query_rows = lax.all_gather(query_weight, 'seq', axis=0, tiled=True)  75 us
    all_gather x1, waiting for transfers between devices, on_device(): value_rows = lax.all_gather(value_weight, 'seq', axis=0, tiled=True)  61.4 us
    all_gather x1, waiting for transfers between devices, on_device(): lax.all_gather(activations, ('tensor', 'sub'), axis=1, tiled=True)  29 us
    dot_general x5, matrix products, add_product(): return jnp.dot(source, weight_rows, preferred_element_type=jnp.float32)  23.6 us
    all_gather x1, blocking collectives, on_device(): lax.all_gather(keys_mem, 'seq', axis=0, tiled=True)  21.4 us
    all_gather x1, blocking collectives, on_device(): lax.all_gather(values_mem, 'seq', axis=0, tiled=True)  15.2 us
    all_gather x1, waiting for transfers between devices, on_device(): lax.all_gather(compressed_local, ('tensor', 'sub'), axis=1, tiled=True)  10.7 us
  transfers between devices with their start and end apart: 5, of which 5 were waited for; matrix products, arithmetic and copies ran while one was open for 6% of the time, Pallas kernels for 0%

commit v1 on v0

v1 whole, which is shorter than its diff:
```python
import jax
import jax.numpy as jnp
from jax import lax
from jax.sharding import PartitionSpec as P

HD = 128
CG = 128
RATE = 4
SEG = 256
MEM = 64
BF = jnp.bfloat16


def swap(value, axis, distance):
    size = lax.axis_size(axis)
    return lax.ppermute(value, axis, [(i, i ^ distance) for i in range(size)])


def after(value, *others):
    return lax.optimization_barrier((value,) + others)[0]


def compress_rows(local_rows, conv_local):
    count_rows, channels = local_rows.shape
    groups = channels // CG
    shaped = local_rows.reshape(count_rows // RATE, RATE, groups, CG)
    kernel = conv_local.reshape(RATE, CG, groups, CG)
    mixed_out = jnp.einsum("mtgc,tcgo->mgo", shaped, kernel, preferred_element_type=jnp.float32)
    return mixed_out.reshape(count_rows // RATE, channels).astype(BF)


def gather_channels(block):
    tensor_size, sub_size = lax.axis_size("tensor"), lax.axis_size("sub")
    tensor_index, sub_index = lax.axis_index("tensor"), lax.axis_index("sub")
    rows, width = block.shape
    whole = jnp.zeros((rows, width * tensor_size * sub_size), block.dtype)
    for kt in range(tensor_size):
        here = swap(block, "tensor", kt) if kt else block
        for ku in range(sub_size):
            piece = swap(here, "sub", ku) if ku else here
            owner = (tensor_index ^ kt) * sub_size + (sub_index ^ ku)
            whole = lax.dynamic_update_slice(whole, piece, (0, owner * width))
    return whole


def attention(queries, keys, values, mem_keys, mem_values, row_segments, mem_segments, length):
    total_rows, width = queries.shape
    heads, slots = width // HD, total_rows // SEG
    shaped_q = queries.reshape(slots, SEG, heads, HD)
    shaped_k = keys.reshape(slots, SEG, heads, HD)
    shaped_v = values.reshape(slots, SEG, heads, HD)
    local = jnp.einsum("asnd,atnd->anst", shaped_q, shaped_k, preferred_element_type=jnp.float32)
    local = local * HD ** (-0.5)
    index = jnp.arange(SEG, dtype=jnp.int32)
    local = jnp.where(index[:, None] >= index[None, :], local, -jnp.inf)
    mk = mem_keys.reshape(-1, heads, HD)
    mv = mem_values.reshape(-1, heads, HD)
    far = jnp.einsum("asnd,knd->ansk", shaped_q, mk, preferred_element_type=jnp.float32)
    far = far * HD ** (-0.5)
    key_segments = jnp.repeat(mem_segments, MEM, total_repeat_length=mk.shape[0])
    allowed = key_segments[None, :] < row_segments[:, None]
    far = jnp.where(allowed[:, None, None, :], far, -jnp.inf)
    best = jnp.maximum(jnp.max(local, axis=3), jnp.max(far, axis=3))[..., None]
    local, far = jnp.exp(local - best), jnp.exp(far - best)
    denominator = jnp.sum(local, axis=3) + jnp.sum(far, axis=3)
    numerator = jnp.einsum(
        "ansk,aknd->ansd", local.astype(BF), shaped_v, preferred_element_type=jnp.float32
    ) + jnp.einsum("ansk,knd->ansd", far.astype(BF), mv, preferred_element_type=jnp.float32)
    result = numerator / denominator[..., None]
    position = row_segments[:, None] * SEG + index[None, :]
    result = jnp.where((position < length)[:, None, :, None], result, 0.0).astype(BF)
    return result.transpose(0, 2, 1, 3).reshape(total_rows, width)


def on_device(
    activations, conv_weight, query_weight, key_weight, value_weight, segment_for_slot, book_length
):
    planes = lax.axis_size("seq")
    plane, group = lax.axis_index("seq"), lax.axis_index("groups")
    parity = plane & 1
    rows, _ = activations.shape
    slots = rows // SEG
    depth, columns = key_weight.shape
    half_depth, half_columns = depth // 2, columns // 2

    partner_rows = swap(activations, "seq", 1)

    def outgoing(weight, target_parity):
        start = (group * half_depth, target_parity * half_columns)
        return lax.dynamic_slice(weight, start, (half_depth, half_columns))

    weights = (key_weight, value_weight, query_weight)
    arrived = [[None] * planes for _ in weights]
    last = {1: partner_rows}
    for which, weight in enumerate(weights):
        pieces = (outgoing(weight, parity), outgoing(weight, 1 - parity))
        for distance in range(1, planes):
            piece = pieces[distance & 1]
            if distance in last:
                piece = after(piece, last[distance])
            near = swap(piece, "seq", distance)
            last[distance] = near
            arrived[which][distance] = (near, swap(near, "groups", 1))

    def whole_weight(which):
        own = lax.dynamic_slice(weights[which], (0, parity * half_columns), (depth, half_columns))
        whole = jnp.zeros((depth * planes, half_columns), BF)
        whole = lax.dynamic_update_slice(whole, own, (plane * depth, 0))
        for distance in range(1, planes):
            start = (plane ^ distance) * depth
            near, far = arrived[which][distance]
            whole = lax.dynamic_update_slice(whole, near, (start + group * half_depth, 0))
            whole = lax.dynamic_update_slice(whole, far, (start + (1 - group) * half_depth, 0))
        return whole

    own_block = jnp.concatenate([activations, compress_rows(activations, conv_weight)], axis=0)
    partner_block = jnp.concatenate([partner_rows, compress_rows(partner_rows, conv_weight)], axis=0)
    own_all, partner_all = gather_channels(own_block), gather_channels(partner_block)

    def product(which, source):
        return jnp.dot(source, whole[which], preferred_element_type=jnp.float32).astype(BF)

    whole = [whole_weight(which) for which in range(3)]
    k_own, k_partner = product(0, own_all), product(0, partner_all)
    v_own, v_partner = product(1, own_all), product(1, partner_all)
    q_own, q_partner = product(2, own_all[:rows]), product(2, partner_all[:rows])

    mem = [jnp.concatenate([a[rows:], b[rows:]], axis=0) for a, b in ((k_own, k_partner), (v_own, v_partner))]
    mem_keys = jnp.concatenate([mem[0]] + [swap(mem[0], "seq", d) for d in range(2, planes, 2)], axis=0)
    mem_values = jnp.concatenate([mem[1]] + [swap(mem[1], "seq", d) for d in range(2, planes, 2)], axis=0)
    by_plane = segment_for_slot.reshape(planes, slots)
    mem_segments = jnp.concatenate([lax.dynamic_index_in_dim(by_plane, plane ^ d, 0, keepdims=False) for d in range(planes)])
    context = attention(
        jnp.concatenate([q_own, q_partner], axis=0),
        jnp.concatenate([k_own[:rows], k_partner[:rows]], axis=0),
        jnp.concatenate([v_own[:rows], v_partner[:rows]], axis=0),
        mem_keys,
        mem_values,
        mem_segments[: 2 * slots],
        mem_segments,
        book_length[0],
    )
    mine, theirs = context[:rows], swap(context[rows:], "seq", 1)
    return jnp.where(
        parity == 0,
        jnp.concatenate([mine, theirs], axis=1),
        jnp.concatenate([theirs, mine], axis=1),
    )


def solution(mesh):
    placed = (
        P(("groups", "seq"), ("tensor", "sub")),
        P(None, ("tensor", "sub")),
        P("seq", ("tensor", "sub")),
        P("seq", ("tensor", "sub")),
        P("seq", ("tensor", "sub")),
        P("groups"),
        P("groups"),
    )
    return jax.shard_map(
        on_device,
        mesh=mesh,
        in_specs=placed,
        out_specs=P(("groups", "seq"), ("tensor", "sub")),
        check_vma=False,
    )
```

time: 351 us -> 183 us (0.52)
  waiting for transfers between devices: 261 us -> 68.1 us
  starting transfers between devices: 0.16 us -> 39 us
  blocking collectives: 36.6 us -> 0 us
  local copies, waits for them, and re-layouts: 3.95 us -> 37.7 us
  between operations: 14 us -> 1.43 us
  other arithmetic: 5.11 us -> 13.9 us
  matrix products: 29.6 us -> 22.2 us
    all_gather x5 -> x0, waiting for transfers between devices: 258 us -> none  [the longest x1 82.4 us: on_device(): key_matrix_rows = lax.all_gather(key_weight, 'seq', axis=0, tiled=True)]
    ppermute x0 -> x28, waiting for transfers between devices: none -> 68.1 us  [swap(): return lax.ppermute(value, axis, [(i, i ^ distance) for i in range(size)])]
    ppermute x0 -> x28, starting transfers between devices: none -> 39 us  [swap(): return lax.ppermute(value, axis, [(i, i ^ distance) for i in range(size)])]
    all_gather x2 -> x0, blocking collectives: 36.6 us -> none  [the longest x1 21.4 us: on_device(): lax.all_gather(keys_mem, 'seq', axis=0, tiled=True)]
    dynamic_update_slice x0 -> x27, local copies, waits for them, and re-layouts: none -> 14 us  [the longest x6 6.87 us: gather_channels(): whole = lax.dynamic_update_slice(whole, piece, (0, owner * width))]
    dot_general x9 -> x10, matrix products: 27.9 us -> 20.4 us  [the longest x6 16.1 us: product(): jnp.dot(source, whole[which], preferred_element_type=jnp.float32).astype(BF)]
    unnamed x14 -> x55, local copies, waits for them, and re-layouts: 1.83 us -> 7.26 us
    concatenate x0 -> x9, other arithmetic: none -> 5.42 us  [the longest x1 1.94 us: on_device(): jnp.concatenate([activations, compress_rows(activations, conv_weight)], a...]
  transfers between devices with their start and end apart: 5 -> 28, of which waited for: 5 -> 13; matrix products, arithmetic and copies ran while one was open for 6% -> 30% of each run, Pallas kernels for 0% -> 0%
where the time goes in v1:
time: 183 us; the launch traced here: 182 us
  waiting for transfers between devices  68.1 us (37%)
  starting transfers between devices  39 us (21%)
  local copies, waits for them, and re-layouts  37.7 us (21%)
  matrix products  22.2 us (12%)
  other arithmetic  13.9 us (8%)
    ppermute x28, waiting for transfers between devices, swap(): return lax.ppermute(value, axis, [(i, i ^ distance) for i in range(size)])  68.1 us
    ppermute x28, starting transfers between devices, swap(): return lax.ppermute(value, axis, [(i, i ^ distance) for i in range(size)])  39 us
    dot_general x6, matrix products, product(): jnp.dot(source, whole[which], preferred_element_type=jnp.float32).astype(BF)  16.1 us
    unnamed x55, local copies, waits for them, and re-layouts  7.26 us
    dynamic_update_slice x6, local copies, waits for them, and re-layouts, gather_channels(): whole = lax.dynamic_update_slice(whole, piece, (0, owner * width))  6.87 us
    dynamic_update_slice x9, local copies, waits for them, and re-layouts, whole_weight(): lax.dynamic_update_slice(whole, near, (start + group * half_depth, 0))  4.97 us
    gather x2, other arithmetic, attention(): jnp.repeat(mem_segments, MEM, total_repeat_length=mk.shape[0])  4.35 us
    another operation x5, local copies, waits for them, and re-layouts  4.02 us
  transfers between devices with their start and end apart: 28, of which 13 were waited for; matrix products, arithmetic and copies ran while one was open for 30% of the time, Pallas kernels for 0%

profile of v1, /device:TPU:0, one launch (start us, length us, event | category | flops | bytes accessed | tf_op | source)
XLA Modules:
  0.0 182.3 jit_solution(9419649413337846951)
XLA Ops:
  0.0 3.0 %collective-permute-start.3 = (bf16[512,1024]{1,0:T(8,128)(2,1)}, bf16[512,1024]{1,0:T(8,128)(2,1)S(1)}, u32[]{:S(2)}, u32[]{:S(2)}) collective-permute-start(bf16[512,1024]{1,0:T(8,128)(2,1)} %param.9), channel_id=1, source_target_pairs={{0,4},{4,0},{8,12},{12,8},{1,5},{5,1},{9,13},{13,9},{2,6},{6,2},{1... | collective-permute-start | bytes 3145736 | tf_op jit(solution)/shard_map/ppermute | solution.py:16
  3.0 1.6 copy.110
  4.6 1.5 copy.80
  6.4 0.9 copy-done.9
  8.0 3.0 %broadcast.148.clone.1 = bf16[640,4096]{1,0:T(8,128)(2,1)} broadcast(bf16[]{:T(256)} %constant.125.clone.1), dimensions={} | broadcast | bytes 5242882 | tf_op jit(solution)/shard_map/broadcast.13
  11.0 1.9 %pad_maximum_fusion = (bf16[640,1024]{1,0:T(8,128)(2,1)}, bf16[640,4096]{1,0:T(8,128)(2,1)}) fusion(bf16[128,1024]{1,0:T(8,128)(2,1)S(1)} %copy.82, bf16[512,1024]{1,0:T(8,128)(2,1)S(1)} %copy-done, bf16[640,4096]{1,0:T(8,128)(2,1)} %broadcast.148.clone.1, s32[]{:T(128)S(6)} %select_n.139), kind=kLoop, calls=%fused_computation.19 | loop fusion | flops 2621440 | bytes 3932164 | tf_op jit(solution)/shard_map/concatenate | solution.py:116
  13.0 1.4 collective-permute-start.1
  14.4 1.8 %fusion.54 = (bf16[512,256]{1,0:T(8,128)(2,1)}, bf16[512,256]{1,0:T(8,128)(2,1)}) fusion(bf16[1024,512]{1,0:T(8,128)(2,1)} %param.12, s32[]{:T(128)S(6)} %select_n.145, s32[]{:T(128)S(6)} %select_n.143, s32[]{:T(128)S(6)} %select_n.146), kind=kLoop, calls=%fused_computation.115 | loop fusion | bytes 1048588 | tf_op jit(solution)/shard_map/dynamic_slice | solution.py:90
  16.3 2.6 %collective-permute-start.8 = (bf16[512,256]{1,0:T(8,128)(2,1)}, bf16[512,256]{1,0:T(8,128)(2,1)}, u32[]{:S(2)}, u32[]{:S(2)}) collective-permute-start(bf16[512,256]{1,0:T(8,128)(2,1)} %get-tuple-element.43), channel_id=1, source_target_pairs={{0,8},{4,12},{8,0},{12,4},{1,9},{5,13},{9,1},{13,5},{2,10},{6,14},... | collective-permute-start | bytes 786440 | tf_op jit(solution)/shard_map/ppermute | solution.py:16
  19.8 0.8 fusion.53
  22.9 4.3 %compare_select_fusion.1 = s32[512,1]{0,1:T(1,128)S(1)} fusion(s32[]{:T(128)} %bitcast.16, s32[]{:T(128)} %bitcast.17, s32[]{:T(128)} %bitcast.18, s32[]{:T(128)} %bitcast.19, s32[]{:T(128)} %bitcast.20, s32[]{:T(128)} %bitcast.22, s32[]{:T(128)} %bitcast.21, s32[512,1]{0,1:T(1,128)S(1)} %bitcast.113, s32[512,1]{0,1:T(1,128)S(1)} %bitcast.111), kind=kLoop, calls=%fused_computation.96 | loop fusion | flops 7168 | bytes 6172 | tf_op jit(solution)/shard_map/jit(_take)/gather | solution.py:60
  27.6 1.6 copy-done.6
  29.4 1.7 copy-done.8
  31.8 0.8 collective-permute-done.8
  32.6 7.5 %collective-permute-done.12 = bf16[512,256]{1,0:T(8,128)(2,1)} collective-permute-done((bf16[512,256]{1,0:T(8,128)(2,1)}, bf16[512,256]{1,0:T(8,128)(2,1)}, u32[]{:S(2)}, u32[]{:S(2)}) %collective-permute-start.12) | collective-permute-done | bytes 262176 | tf_op jit(solution)/shard_map/ppermute | solution.py:16
  40.0 1.4 collective-permute-start.13
  41.5 11.5 %collective-permute-start.9 = (bf16[512,256]{1,0:T(8,128)(2,1)}, bf16[512,256]{1,0:T(8,128)(2,1)}, u32[]{:S(2)}, u32[]{:S(2)}) collective-permute-start(bf16[512,256]{1,0:T(8,128)(2,1)} %get-tuple-element.27), channel_id=1, source_target_pairs={{0,8},{4,12},{8,0},{12,4},{1,9},{5,13},{9,1},{13,5},{2,10},{6,14},... | collective-permute-start | bytes 786440 | tf_op jit(solution)/shard_map/ppermute | solution.py:16
  53.7 1.5 collective-permute-start.20
  55.3 10.6 %collective-permute-done.9 = bf16[512,256]{1,0:T(8,128)(2,1)} collective-permute-done((bf16[512,256]{1,0:T(8,128)(2,1)}, bf16[512,256]{1,0:T(8,128)(2,1)}, u32[]{:S(2)}, u32[]{:S(2)}) %collective-permute-start.9) | collective-permute-done | bytes 262176 | tf_op jit(solution)/shard_map/ppermute | solution.py:16
  65.9 1.5 collective-permute-start.21
  67.7 1.3 fusion.28
  69.0 1.1 copy.85
  71.0 7.3 %collective-permute-done.4 = bf16[512,256]{1,0:T(8,128)(2,1)} collective-permute-done((bf16[512,256]{1,0:T(8,128)(2,1)}, bf16[512,256]{1,0:T(8,128)(2,1)}, u32[]{:S(2)}, u32[]{:S(2)}) %collective-permute-start.4) | collective-permute-done | bytes 262176 | tf_op jit(solution)/shard_map/ppermute | solution.py:16
  78.2 1.0 collective-permute-start.14
  79.3 2.6 %constant_dynamic-update-slice_fusion.24 = bf16[640,4096]{1,0:T(8,128)(2,1)} fusion(bf16[640,4096]{1,0:T(8,128)(2,1)} %get-tuple-element.36, bf16[640,1024]{1,0:T(8,128)(2,1)} %collective-permute-done, s32[]{:T(128)S(6)} %select_n.140), kind=kLoop, calls=%fused_computation.88 | loop fusion | bytes 2621444 | tf_op jit(solution)/shard_map/dynamic_update_slice | solution.py:42
  81.9 2.5 %constant_dynamic-update-slice_fusion.23 = bf16[640,4096]{1,0:T(8,128)(2,1)} fusion(bf16[640,4096]{1,0:T(8,128)(2,1)} %constant_dynamic-update-slice_fusion.24, bf16[640,1024]{1,0:T(8,128)(2,1)} %collective-permute-done.1, s32[]{:T(128)S(6)} %select_n.141), kind=kLoop, calls=%fused_computation.87 | loop fusion | bytes 2621444 | tf_op jit(solution)/shard_map/dynamic_update_slice | solution.py:42
  84.4 1.0 constant_dynamic-update-slice_fusion.10
  85.4 3.1 %collective-permute-done.19 = bf16[512,256]{1,0:T(8,128)(2,1)S(1)} collective-permute-done((bf16[512,256]{1,0:T(8,128)(2,1)}, bf16[512,256]{1,0:T(8,128)(2,1)S(1)}, u32[]{:S(2)}, u32[]{:S(2)}) %collective-permute-start.19) | collective-permute-done | bytes 262176 | tf_op jit(solution)/shard_map/ppermute | solution.py:16
  88.5 1.0 constant_dynamic-update-slice_fusion.8
  89.6 2.1 %collective-permute-start.23 = (bf16[512,256]{1,0:T(8,128)(2,1)S(1)}, bf16[512,256]{1,0:T(8,128)(2,1)S(1)}, u32[]{:S(2)}, u32[]{:S(2)}) collective-permute-start(bf16[512,256]{1,0:T(8,128)(2,1)S(1)} %collective-permute-done.5), channel_id=1, source_target_pairs={{0,16},{16,0},{1,17},{17,1},{2,18},{18,2},{3,19},{19,3},{4,20},{20... | collective-permute-start | bytes 786440 | tf_op jit(solution)/shard_map/ppermute | solution.py:16
  91.7 1.0 constant_dynamic-update-slice_fusion.7
  92.7 1.0 constant_dynamic-update-slice_fusion.6
  93.8 2.1 %collective-permute-start.6 = (bf16[512,256]{1,0:T(8,128)(2,1)S(1)}, bf16[512,256]{1,0:T(8,128)(2,1)S(1)}, u32[]{:S(2)}, u32[]{:S(2)}) collective-permute-start(bf16[512,256]{1,0:T(8,128)(2,1)S(1)} %copy-done.18), channel_id=1, source_target_pairs={{0,4},{4,0},{8,12},{12,8},{1,5},{5,1},{9,13},{13,9},{2,6},{6,2},{1... | collective-permute-start | bytes 786440 | tf_op jit(solution)/shard_map/ppermute | solution.py:16
  95.8 1.0 constant_dynamic-update-slice_fusion.5
  96.8 3.9 %collective-permute-done.23 = bf16[512,256]{1,0:T(8,128)(2,1)S(1)} collective-permute-done((bf16[512,256]{1,0:T(8,128)(2,1)S(1)}, bf16[512,256]{1,0:T(8,128)(2,1)S(1)}, u32[]{:S(2)}, u32[]{:S(2)}) %collective-permute-start.23) | collective-permute-done | bytes 262176 | tf_op jit(solution)/shard_map/ppermute | solution.py:16
  100.7 1.0 constant_dynamic-update-slice_fusion.2
  101.7 3.4 %collective-permute-start.10 = (bf16[512,256]{1,0:T(8,128)(2,1)S(1)}, bf16[512,256]{1,0:T(8,128)(2,1)S(1)}, u32[]{:S(2)}, u32[]{:S(2)}) collective-permute-start(bf16[512,256]{1,0:T(8,128)(2,1)S(1)} %copy-done.17), channel_id=1, source_target_pairs={{0,8},{4,12},{8,0},{12,4},{1,9},{5,13},{9,1},{13,5},{2,10},{6,14},... | collective-permute-start | bytes 786440 | tf_op jit(solution)/shard_map/ppermute | solution.py:16
  105.2 2.1 %collective-permute-done.24 = bf16[512,256]{1,0:T(8,128)(2,1)S(1)} collective-permute-done((bf16[512,256]{1,0:T(8,128)(2,1)}, bf16[512,256]{1,0:T(8,128)(2,1)S(1)}, u32[]{:S(2)}, u32[]{:S(2)}) %collective-permute-start.24) | collective-permute-done | bytes 262176 | tf_op jit(solution)/shard_map/ppermute | solution.py:16
  107.3 1.7 collective-permute-start.7
  109.0 1.0 constant_dynamic-update-slice_fusion
  110.0 6.8 %collective-permute-done.10 = bf16[512,256]{1,0:T(8,128)(2,1)S(1)} collective-permute-done((bf16[512,256]{1,0:T(8,128)(2,1)S(1)}, bf16[512,256]{1,0:T(8,128)(2,1)S(1)}, u32[]{:S(2)}, u32[]{:S(2)}) %collective-permute-start.10) | collective-permute-done | bytes 262176 | tf_op jit(solution)/shard_map/ppermute | solution.py:16
  117.2 1.8 collective-permute-start.15
  119.0 7.1 %collective-permute-done.11 = bf16[512,256]{1,0:T(8,128)(2,1)S(1)} collective-permute-done((bf16[512,256]{1,0:T(8,128)(2,1)S(1)}, bf16[512,256]{1,0:T(8,128)(2,1)S(1)}, u32[]{:S(2)}, u32[]{:S(2)}) %collective-permute-start.11) | collective-permute-done | bytes 262176 | tf_op jit(solution)/shard_map/ppermute | solution.py:16
  126.2 3.8 %collective-permute-done.15 = bf16[512,256]{1,0:T(8,128)(2,1)S(1)} collective-permute-done((bf16[512,256]{1,0:T(8,128)(2,1)S(1)}, bf16[512,256]{1,0:T(8,128)(2,1)S(1)}, u32[]{:S(2)}, u32[]{:S(2)}) %collective-permute-start.15) | collective-permute-done | bytes 262176 | tf_op jit(solution)/shard_map/ppermute | solution.py:16
  130.4 1.2 constant_dynamic-update-slice_fusion.22
  131.7 4.0 %convolution_convert_fusion.3 = bf16[640,256]{1,0:T(8,128)(2,1)S(1)} fusion(bf16[640,4096]{1,0:T(8,128)(2,1)} %constant_dynamic-update-slice_fusion.22, bf16[4096,256]{1,0:T(8,128)(2,1)S(1)} %constant_dynamic-update-slice_fusion.5), kind=kOutput, calls=%fused_computation.29 | convolution fusion | flops 1342341120 | bytes 7667712 | tf_op jit(solution)/shard_map/dot_general | solution.py:121
  136.4 4.0 %convolution_convert_fusion.1 = bf16[640,256]{1,0:T(8,128)(2,1)S(1)} fusion(bf16[640,4096]{1,0:T(8,128)(2,1)} %constant_dynamic-update-slice_fusion.22, bf16[4096,256]{1,0:T(8,128)(2,1)S(1)} %constant_dynamic-update-slice_fusion.21), kind=kOutput, calls=%fused_computation.27 | convolution fusion | flops 1342341120 | bytes 7667712 | tf_op jit(solution)/shard_map/dot_general | solution.py:121
  140.4 3.6 %fusion.29 = bf16[512,256]{1,0:T(8,128)(2,1)S(1)} fusion(bf16[4096,256]{1,0:T(8,128)(2,1)S(1)} %constant_dynamic-update-slice_fusion.15, bf16[640,4096]{1,0:T(8,128)(2,1)} %constant_dynamic-update-slice_fusion.22), kind=kOutput, calls=%fused_computation.32 | convolution fusion | flops 1073872896 | bytes 6553600 | tf_op jit(solution)/shard_map/dot_general | solution.py:121
  144.2 1.3 fusion.32
  145.5 1.7 convolution_convert_fusion
  147.2 1.5 convolution_convert_fusion.2
  149.8 0.9 reshape.191
  152.0 2.9 %collective-permute-start.26 = (bf16[256,256]{1,0:T(8,128)(2,1)}, bf16[256,256]{1,0:T(8,128)(2,1)}, u32[]{:S(2)}, u32[]{:S(2)}) collective-permute-start(bf16[256,256]{1,0:T(8,128)(2,1)} %pad_maximum_fusion.8), channel_id=1, source_target_pairs={{0,8},{4,12},{8,0},{12,4},{1,9},{5,13},{9,1},{13,5},{2,10},{6,14},... | collective-permute-start | bytes 393224 | tf_op jit(solution)/shard_map/ppermute | solution.py:16
  154.9 1.5 fusion.9
  156.6 0.9 reshape.193
  157.5 5.5 %collective-permute-done.22 = bf16[256,256]{1,0:T(8,128)(2,1)} collective-permute-done((bf16[256,256]{1,0:T(8,128)(2,1)}, bf16[256,256]{1,0:T(8,128)(2,1)}, u32[]{:S(2)}, u32[]{:S(2)}) %collective-permute-start.22) | collective-permute-done | bytes 131104 | tf_op jit(solution)/shard_map/ppermute | solution.py:16
  163.0 0.9 pad_maximum_fusion.5
  164.0 1.8 collective-permute-done.26
  165.7 0.9 pad_maximum_fusion.6
  166.7 0.8 copy.108
  168.3 1.1 fusion.4
  171.5 1.2 fusion.24
  173.5 7.9 %collective-permute-done.27 = bf16[512,256]{1,0:T(8,128)(2,1)S(1)} collective-permute-done((bf16[512,256]{1,0:T(8,128)(2,1)S(1)}, bf16[512,256]{1,0:T(8,128)(2,1)S(1)}, u32[]{:S(2)}, u32[]{:S(2)}) %collective-permute-start.27) | collective-permute-done | bytes 262176 | tf_op jit(solution)/shard_map/ppermute | solution.py:16
  181.4 0.9 maximum_select_fusion
  (143 shorter events, 14.4 us)
Async XLA Ops:
  0.0 67.4 %collective-permute-start.3 = (bf16[512,1024]{1,0:T(8,128)(2,1)}, bf16[512,1024]{1,0:T(8,128)(2,1)S(1)}, u32[]{:S(2)}, u32[]{:S(2)}) collective-permute-start(bf16[512,1024]{1,0:T(8,128)(2,1)} %param.9), channel_id=1, source_target_pairs={{0,4},{4,0},{8,12},{12,8},{1,5},{5,1},{9,13},{13,9},{2,6},{6,2},{1... | collective-permute-start | bytes 3145736 | tf_op jit(solution)/shard_map/ppermute | solution.py:16
  3.0 3.1 %copy-start = (bf16[512,1024]{1,0:T(8,128)(2,1)S(1)}, bf16[512,1024]{1,0:T(8,128)(2,1)}, u32[]{:S(2)}) copy-start(bf16[512,1024]{1,0:T(8,128)(2,1)} %param.9) | copy-start | bytes 3145732
  6.1 1.2 copy-start.9
  11.0 8.7 %copy-start.24 = (s32[8]{0:T(128)S(1)}, s32[8]{0:T(128)}, u32[]{:S(2)}) copy-start(s32[8]{0:T(128)} %param.14) | copy-start | bytes 100
  11.0 8.8 %copy-start.5 = (bf16[1024,512]{1,0:T(8,128)(2,1)S(1)}, bf16[1024,512]{1,0:T(8,128)(2,1)}, u32[]{:S(2)}) copy-start(bf16[1024,512]{1,0:T(8,128)(2,1)} %param.11) | copy-start | bytes 3145732
  13.0 7.7 %copy-start.7 = (bf16[1024,512]{1,0:T(8,128)(2,1)S(1)}, bf16[1024,512]{1,0:T(8,128)(2,1)}, u32[]{:S(2)}) copy-start(bf16[1024,512]{1,0:T(8,128)(2,1)} %param.13) | copy-start | bytes 3145732
  13.0 9.9 %copy-start.23 = (s32[4,128]{1,0:T(4,128)S(1)}, s32[4,128]{1,0:T(4,128)}, u32[]{:S(2)}) copy-start(s32[4,128]{1,0:T(4,128)} %constant.135.clone.1) | copy-start | bytes 6148
  13.0 66.3 %collective-permute-start = (bf16[640,1024]{1,0:T(8,128)(2,1)}, bf16[640,1024]{1,0:T(8,128)(2,1)}, u32[]{:S(2)}, u32[]{:S(2)}) collective-permute-start(bf16[640,1024]{1,0:T(8,128)(2,1)} %get-tuple-element.35), channel_id=1, source_target_pairs={{0,1},{1,0},{2,3},{3,2},{4,5},{5,4},{6,7},{7,6},{8,9},{9,8},{10,11... | collective-permute-start | bytes 3932168 | tf_op jit(solution)/shard_map/ppermute | solution.py:16
  13.0 68.9 %collective-permute-start.1 = (bf16[640,1024]{1,0:T(8,128)(2,1)}, bf16[640,1024]{1,0:T(8,128)(2,1)}, u32[]{:S(2)}, u32[]{:S(2)}) collective-permute-start(bf16[640,1024]{1,0:T(8,128)(2,1)} %get-tuple-element.35), channel_id=1, source_target_pairs={{0,2},{2,0},{1,3},{3,1},{4,6},{6,4},{5,7},{7,5},{8,10},{10,8},{9,1... | collective-permute-start | bytes 3932168 | tf_op jit(solution)/shard_map/ppermute | solution.py:16
  16.3 16.3 %collective-permute-start.8 = (bf16[512,256]{1,0:T(8,128)(2,1)}, bf16[512,256]{1,0:T(8,128)(2,1)}, u32[]{:S(2)}, u32[]{:S(2)}) collective-permute-start(bf16[512,256]{1,0:T(8,128)(2,1)} %get-tuple-element.43), channel_id=1, source_target_pairs={{0,8},{4,12},{8,0},{12,4},{1,9},{5,13},{9,1},{13,5},{2,10},{6,14},... | collective-permute-start | bytes 786440 | tf_op jit(solution)/shard_map/ppermute | solution.py:16
  18.9 21.2 %collective-permute-start.12 = (bf16[512,256]{1,0:T(8,128)(2,1)}, bf16[512,256]{1,0:T(8,128)(2,1)}, u32[]{:S(2)}, u32[]{:S(2)}) collective-permute-start(bf16[512,256]{1,0:T(8,128)(2,1)} %get-tuple-element.24), channel_id=1, source_target_pairs={{0,12},{4,8},{8,4},{12,0},{1,13},{5,9},{9,5},{13,1},{2,14},{6,10},... | collective-permute-start | bytes 786440 | tf_op jit(solution)/shard_map/ppermute | solution.py:16
  21.4 18.6 %copy-start.19 = (bf16[512,256]{1,0:T(8,128)(2,1)}, bf16[512,256]{1,0:T(8,128)(2,1)S(1)}, u32[]{:S(2)}) copy-start(bf16[512,256]{1,0:T(8,128)(2,1)S(1)} %get-tuple-element.29) | copy-start | bytes 786436
  27.4 1.8 copy-start.6
  27.5 2.0 %copy-start.1 = (bf16[4096,256]{1,0:T(8,128)(2,1)}, bf16[4096,256]{1,0:T(8,128)(2,1)S(1)}, u32[]{:S(2)}) copy-start(bf16[4096,256]{1,0:T(8,128)(2,1)S(1)} %dynamic-slice_dynamic-update-slice_fusion.2) | copy-start | bytes 6291460
  29.2 1.9 %copy-start.8 = (bf16[1024,512]{1,0:T(8,128)(2,1)S(1)}, bf16[1024,512]{1,0:T(8,128)(2,1)}, u32[]{:S(2)}) copy-start(bf16[1024,512]{1,0:T(8,128)(2,1)} %param.13) | copy-start | bytes 3145732
  29.3 1.9 %copy-start.3 = (bf16[4096,256]{1,0:T(8,128)(2,1)}, bf16[4096,256]{1,0:T(8,128)(2,1)S(1)}, u32[]{:S(2)}) copy-start(bf16[4096,256]{1,0:T(8,128)(2,1)S(1)} %dynamic-slice_dynamic-update-slice_fusion.1) | copy-start | bytes 6291460
  40.0 13.7 %collective-permute-start.13 = (bf16[512,256]{1,0:T(8,128)(2,1)S(1)}, bf16[512,256]{1,0:T(8,128)(2,1)}, u32[]{:S(2)}, u32[]{:S(2)}) collective-permute-start(bf16[512,256]{1,0:T(8,128)(2,1)S(1)} %get-tuple-element.29), channel_id=1, source_target_pairs={{0,12},{4,8},{8,4},{12,0},{1,13},{5,9},{9,5},{13,1},{2,14},{6,10},... | collective-permute-start | bytes 786440 | tf_op jit(solution)/shard_map/ppermute | solution.py:16
  41.5 24.4 %collective-permute-start.9 = (bf16[512,256]{1,0:T(8,128)(2,1)}, bf16[512,256]{1,0:T(8,128)(2,1)}, u32[]{:S(2)}, u32[]{:S(2)}) collective-permute-start(bf16[512,256]{1,0:T(8,128)(2,1)} %get-tuple-element.27), channel_id=1, source_target_pairs={{0,8},{4,12},{8,0},{12,4},{1,9},{5,13},{9,1},{13,5},{2,10},{6,14},... | collective-permute-start | bytes 786440 | tf_op jit(solution)/shard_map/ppermute | solution.py:16
  53.7 14.0 %copy-start.10 = (bf16[4,128,8,128]{1,3,0,2:T(8,128)(2,1)S(1)}, bf16[4,128,8,128]{1,3,0,2:T(8,128)(2,1)}, u32[]{:S(2)}) copy-start(bf16[4,128,8,128]{1,3,0,2:T(8,128)(2,1)} %copy.80) | copy-start | bytes 3145732
  53.7 35.9 %collective-permute-start.20 = (bf16[512,256]{1,0:T(8,128)(2,1)}, bf16[512,256]{1,0:T(8,128)(2,1)}, u32[]{:S(2)}, u32[]{:S(2)}) collective-permute-start(bf16[512,256]{1,0:T(8,128)(2,1)} %collective-permute-done.8), channel_id=1, source_target_pairs={{0,16},{16,0},{1,17},{17,1},{2,18},{18,2},{3,19},{19,3},{4,20},{20... | collective-permute-start | bytes 786440 | tf_op jit(solution)/shard_map/ppermute | solution.py:16
  65.9 27.8 %collective-permute-start.21 = (bf16[512,256]{1,0:T(8,128)(2,1)}, bf16[512,256]{1,0:T(8,128)(2,1)}, u32[]{:S(2)}, u32[]{:S(2)}) collective-permute-start(bf16[512,256]{1,0:T(8,128)(2,1)} %collective-permute-done.12), channel_id=1, source_target_pairs={{0,16},{16,0},{1,17},{17,1},{2,18},{18,2},{3,19},{19,3},{4,20},{20... | collective-permute-start | bytes 786440 | tf_op jit(solution)/shard_map/ppermute | solution.py:16
  67.4 10.8 %collective-permute-start.4 = (bf16[512,256]{1,0:T(8,128)(2,1)}, bf16[512,256]{1,0:T(8,128)(2,1)}, u32[]{:S(2)}, u32[]{:S(2)}) collective-permute-start(bf16[512,256]{1,0:T(8,128)(2,1)} %get-tuple-element.24), channel_id=1, source_target_pairs={{0,4},{4,0},{8,12},{12,8},{1,5},{5,1},{9,13},{13,9},{2,6},{6,2},{1... | collective-permute-start | bytes 786440 | tf_op jit(solution)/shard_map/ppermute | solution.py:16
  70.7 7.5 %copy-start.18 = (bf16[512,256]{1,0:T(8,128)(2,1)S(1)}, bf16[512,256]{1,0:T(8,128)(2,1)}, u32[]{:S(2)}) copy-start(bf16[512,256]{1,0:T(8,128)(2,1)} %get-tuple-element.30) | copy-start | bytes 786436
  70.7 8.5 %copy-start.20 = (bf16[512,256]{1,0:T(8,128)(2,1)S(1)}, bf16[512,256]{1,0:T(8,128)(2,1)}, u32[]{:S(2)}) copy-start(bf16[512,256]{1,0:T(8,128)(2,1)} %copy-done.19) | copy-start | bytes 786436
  78.2 15.5 %collective-permute-start.14 = (bf16[512,256]{1,0:T(8,128)(2,1)S(1)}, bf16[512,256]{1,0:T(8,128)(2,1)S(1)}, u32[]{:S(2)}, u32[]{:S(2)}) collective-permute-start(bf16[512,256]{1,0:T(8,128)(2,1)S(1)} %copy-done.18), channel_id=1, source_target_pairs={{0,12},{4,8},{8,4},{12,0},{1,13},{5,9},{9,5},{13,1},{2,14},{6,10},... | collective-permute-start | bytes 786440 | tf_op jit(solution)/shard_map/ppermute | solution.py:16
  79.2 10.3 %collective-permute-start.5 = (bf16[512,256]{1,0:T(8,128)(2,1)S(1)}, bf16[512,256]{1,0:T(8,128)(2,1)S(1)}, u32[]{:S(2)}, u32[]{:S(2)}) collective-permute-start(bf16[512,256]{1,0:T(8,128)(2,1)S(1)} %copy-done.20), channel_id=1, source_target_pairs={{0,4},{4,0},{8,12},{12,8},{1,5},{5,1},{9,13},{13,9},{2,6},{6,2},{1... | collective-permute-start | bytes 786440 | tf_op jit(solution)/shard_map/ppermute | solution.py:16
  79.2 5.2 %copy-start.4 = (bf16[4096,256]{1,0:T(8,128)(2,1)S(1)}, bf16[4096,256]{1,0:T(8,128)(2,1)}, u32[]{:S(2)}) copy-start(bf16[4096,256]{1,0:T(8,128)(2,1)} %copy-done.3) | copy-start | bytes 6291460
  81.9 6.6 %collective-permute-start.19 = (bf16[512,256]{1,0:T(8,128)(2,1)}, bf16[512,256]{1,0:T(8,128)(2,1)S(1)}, u32[]{:S(2)}, u32[]{:S(2)}) collective-permute-start(bf16[512,256]{1,0:T(8,128)(2,1)} %collective-permute-done.4), channel_id=1, source_target_pairs={{0,16},{16,0},{1,17},{17,1},{2,18},{18,2},{3,19},{19,3},{4,20},{20... | collective-permute-start | bytes 786440 | tf_op jit(solution)/shard_map/ppermute | solution.py:16
  85.4 16.3 %copy-start.17 = (bf16[512,256]{1,0:T(8,128)(2,1)S(1)}, bf16[512,256]{1,0:T(8,128)(2,1)}, u32[]{:S(2)}) copy-start(bf16[512,256]{1,0:T(8,128)(2,1)} %get-tuple-element.28) | copy-start | bytes 786436
  85.4 19.8 %copy-start.2 = (bf16[4096,256]{1,0:T(8,128)(2,1)S(1)}, bf16[4096,256]{1,0:T(8,128)(2,1)}, u32[]{:S(2)}) copy-start(bf16[4096,256]{1,0:T(8,128)(2,1)} %copy-done.1) | copy-start | bytes 6291460
  88.5 13.2 %collective-permute-start.25 = (bf16[512,256]{1,0:T(8,128)(2,1)}, bf16[512,256]{1,0:T(8,128)(2,1)S(1)}, u32[]{:S(2)}, u32[]{:S(2)}) collective-permute-start(bf16[512,256]{1,0:T(8,128)(2,1)} %collective-permute-done.13), channel_id=1, source_target_pairs={{0,16},{16,0},{1,17},{17,1},{2,18},{18,2},{3,19},{19,3},{4,20},{20... | collective-permute-start | bytes 786440 | tf_op jit(solution)/shard_map/ppermute | solution.py:16
  89.5 40.6 %collective-permute-start.16 = (bf16[640,1024]{1,0:T(8,128)(2,1)S(1)}, bf16[640,1024]{1,0:T(8,128)(2,1)S(1)}, u32[]{:S(2)}, u32[]{:S(2)}) collective-permute-start(bf16[640,1024]{1,0:T(8,128)(2,1)S(1)} %get-tuple-element.37), channel_id=1, source_target_pairs={{0,1},{1,0},{2,3},{3,2},{4,5},{5,4},{6,7},{7,6},{8,9},{9,8},{10,11... | collective-permute-start | bytes 3932168 | tf_op jit(solution)/shard_map/ppermute | solution.py:16
  89.6 11.1 %collective-permute-start.23 = (bf16[512,256]{1,0:T(8,128)(2,1)S(1)}, bf16[512,256]{1,0:T(8,128)(2,1)S(1)}, u32[]{:S(2)}, u32[]{:S(2)}) collective-permute-start(bf16[512,256]{1,0:T(8,128)(2,1)S(1)} %collective-permute-done.5), channel_id=1, source_target_pairs={{0,16},{16,0},{1,17},{17,1},{2,18},{18,2},{3,19},{19,3},{4,20},{20... | collective-permute-start | bytes 786440 | tf_op jit(solution)/shard_map/ppermute | solution.py:16
  93.7 36.3 %collective-permute-start.17 = (bf16[640,1024]{1,0:T(8,128)(2,1)S(1)}, bf16[640,1024]{1,0:T(8,128)(2,1)S(1)}, u32[]{:S(2)}, u32[]{:S(2)}) collective-permute-start(bf16[640,1024]{1,0:T(8,128)(2,1)S(1)} %get-tuple-element.37), channel_id=1, source_target_pairs={{0,2},{2,0},{1,3},{3,1},{4,6},{6,4},{5,7},{7,5},{8,10},{10,8},{9,1... | collective-permute-start | bytes 3932168 | tf_op jit(solution)/shard_map/ppermute | solution.py:16
  93.8 11.4 %collective-permute-start.6 = (bf16[512,256]{1,0:T(8,128)(2,1)S(1)}, bf16[512,256]{1,0:T(8,128)(2,1)S(1)}, u32[]{:S(2)}, u32[]{:S(2)}) collective-permute-start(bf16[512,256]{1,0:T(8,128)(2,1)S(1)} %copy-done.18), channel_id=1, source_target_pairs={{0,4},{4,0},{8,12},{12,8},{1,5},{5,1},{9,13},{13,9},{2,6},{6,2},{1... | collective-permute-start | bytes 786440 | tf_op jit(solution)/shard_map/ppermute | solution.py:16
  100.7 6.6 %collective-permute-start.24 = (bf16[512,256]{1,0:T(8,128)(2,1)}, bf16[512,256]{1,0:T(8,128)(2,1)S(1)}, u32[]{:S(2)}, u32[]{:S(2)}) collective-permute-start(bf16[512,256]{1,0:T(8,128)(2,1)} %collective-permute-done.9), channel_id=1, source_target_pairs={{0,16},{16,0},{1,17},{17,1},{2,18},{18,2},{3,19},{19,3},{4,20},{20... | collective-permute-start | bytes 786440 | tf_op jit(solution)/shard_map/ppermute | solution.py:16
  101.7 15.1 %collective-permute-start.10 = (bf16[512,256]{1,0:T(8,128)(2,1)S(1)}, bf16[512,256]{1,0:T(8,128)(2,1)S(1)}, u32[]{:S(2)}, u32[]{:S(2)}) collective-permute-start(bf16[512,256]{1,0:T(8,128)(2,1)S(1)} %copy-done.17), channel_id=1, source_target_pairs={{0,8},{4,12},{8,0},{12,4},{1,9},{5,13},{9,1},{13,5},{2,10},{6,14},... | collective-permute-start | bytes 786440 | tf_op jit(solution)/shard_map/ppermute | solution.py:16
  105.1 25.3 %collective-permute-start.2 = (bf16[640,1024]{1,0:T(8,128)(2,1)}, bf16[640,1024]{1,0:T(8,128)(2,1)S(1)}, u32[]{:S(2)}, u32[]{:S(2)}) collective-permute-start(bf16[640,1024]{1,0:T(8,128)(2,1)} %collective-permute-done.1), channel_id=1, source_target_pairs={{0,1},{1,0},{2,3},{3,2},{4,5},{5,4},{6,7},{7,6},{8,9},{9,8},{10,11... | collective-permute-start | bytes 3932168 | tf_op jit(solution)/shard_map/ppermute | solution.py:16
  107.3 9.9 %collective-permute-start.7 = (bf16[512,256]{1,0:T(8,128)(2,1)S(1)}, bf16[512,256]{1,0:T(8,128)(2,1)S(1)}, u32[]{:S(2)}, u32[]{:S(2)}) collective-permute-start(bf16[512,256]{1,0:T(8,128)(2,1)S(1)} %collective-permute-done.6), channel_id=1, source_target_pairs={{0,16},{16,0},{1,17},{17,1},{2,18},{18,2},{3,19},{19,3},{4,20},{20... | collective-permute-start | bytes 786440 | tf_op jit(solution)/shard_map/ppermute | solution.py:16
  116.9 9.2 %collective-permute-start.11 = (bf16[512,256]{1,0:T(8,128)(2,1)S(1)}, bf16[512,256]{1,0:T(8,128)(2,1)S(1)}, u32[]{:S(2)}, u32[]{:S(2)}) collective-permute-start(bf16[512,256]{1,0:T(8,128)(2,1)S(1)} %collective-permute-done.10), channel_id=1, source_target_pairs={{0,16},{16,0},{1,17},{17,1},{2,18},{18,2},{3,19},{19,3},{4,20},{20... | collective-permute-start | bytes 786440 | tf_op jit(solution)/shard_map/ppermute | solution.py:16
  117.2 12.8 %collective-permute-start.15 = (bf16[512,256]{1,0:T(8,128)(2,1)S(1)}, bf16[512,256]{1,0:T(8,128)(2,1)S(1)}, u32[]{:S(2)}, u32[]{:S(2)}) collective-permute-start(bf16[512,256]{1,0:T(8,128)(2,1)S(1)} %collective-permute-done.14), channel_id=1, source_target_pairs={{0,16},{16,0},{1,17},{17,1},{2,18},{18,2},{3,19},{19,3},{4,20},{20... | collective-permute-start | bytes 786440 | tf_op jit(solution)/shard_map/ppermute | solution.py:16
  130.0 14.0 %collective-permute-start.18 = (bf16[640,1024]{1,0:T(8,128)(2,1)S(1)}, bf16[640,1024]{1,0:T(8,128)(2,1)S(1)}, u32[]{:S(2)}, u32[]{:S(2)}) collective-permute-start(bf16[640,1024]{1,0:T(8,128)(2,1)S(1)} %collective-permute-done.17), channel_id=1, source_target_pairs={{0,1},{1,0},{2,3},{3,2},{4,5},{5,4},{6,7},{7,6},{8,9},{9,8},{10,11... | collective-permute-start | bytes 3932168 | tf_op jit(solution)/shard_map/ppermute | solution.py:16
  135.7 4.7 %copy-start.12 = (bf16[640,256]{1,0:T(8,128)(2,1)}, bf16[640,256]{1,0:T(8,128)(2,1)S(1)}, u32[]{:S(2)}) copy-start(bf16[640,256]{1,0:T(8,128)(2,1)S(1)} %convolution_convert_fusion.3) | copy-start | bytes 983044
  140.4 3.6 %copy-start.11 = (bf16[640,256]{1,0:T(8,128)(2,1)}, bf16[640,256]{1,0:T(8,128)(2,1)S(1)}, u32[]{:S(2)}) copy-start(bf16[640,256]{1,0:T(8,128)(2,1)S(1)} %convolution_convert_fusion.1) | copy-start | bytes 983044
  147.2 1.6 copy-start.15
  148.8 1.0 slice-start.1
  148.9 1.8 %copy-start.13 = (bf16[128,256]{1,0:T(8,128)(2,1)S(1)}, bf16[128,256]{1,0:T(8,128)(2,1)}, u32[]{:S(2)}) copy-start(bf16[128,256]{1,0:T(8,128)(2,1)} %slice.105) | copy-start | bytes 196612
  148.9 6.0 %copy-start.21 = (pred[256,256]{0,1:T(8,128)(4,1)S(1)}, pred[256,256]{0,1:T(8,128)(4,1)}, u32[]{:S(2)}) copy-start(pred[256,256]{0,1:T(8,128)(4,1)} %iota_compare_fusion) | copy-start | bytes 196612
  150.7 5.8 %copy-start.16 = (bf16[640,256]{1,0:T(8,128)(2,1)S(1)}, bf16[640,256]{1,0:T(8,128)(2,1)}, u32[]{:S(2)}) copy-start(bf16[640,256]{1,0:T(8,128)(2,1)} %copy-done.15) | copy-start | bytes 983044
  151.4 5.2 %slice-start = ((bf16[640,256]{1,0:T(8,128)(2,1)}), bf16[512,256]{1,0:T(8,128)(2,1)S(1)}, s32[]{:S(2)}) async-start(bf16[640,256]{1,0:T(8,128)(2,1)} %copy-done.11), calls=%async_computation | async-start | bytes 524288 | tf_op jit(solution)/shard_map/slice | solution.py:136
  151.4 11.6 %collective-permute-start.22 = (bf16[256,256]{1,0:T(8,128)(2,1)}, bf16[256,256]{1,0:T(8,128)(2,1)}, u32[]{:S(2)}, u32[]{:S(2)}) collective-permute-start(bf16[256,256]{1,0:T(8,128)(2,1)} %pad_maximum_fusion.7), channel_id=1, source_target_pairs={{0,8},{4,12},{8,0},{12,4},{1,9},{5,13},{9,1},{13,5},{2,10},{6,14},... | collective-permute-start | bytes 393224 | tf_op jit(solution)/shard_map/ppermute | solution.py:16
  152.0 13.7 %collective-permute-start.26 = (bf16[256,256]{1,0:T(8,128)(2,1)}, bf16[256,256]{1,0:T(8,128)(2,1)}, u32[]{:S(2)}, u32[]{:S(2)}) collective-permute-start(bf16[256,256]{1,0:T(8,128)(2,1)} %pad_maximum_fusion.8), channel_id=1, source_target_pairs={{0,8},{4,12},{8,0},{12,4},{1,9},{5,13},{9,1},{13,5},{2,10},{6,14},... | collective-permute-start | bytes 393224 | tf_op jit(solution)/shard_map/ppermute | solution.py:16
  169.5 1.0 copy-start.14
  170.5 0.9 copy-start.22
  173.0 8.3 %collective-permute-start.27 = (bf16[512,256]{1,0:T(8,128)(2,1)S(1)}, bf16[512,256]{1,0:T(8,128)(2,1)S(1)}, u32[]{:S(2)}, u32[]{:S(2)}) collective-permute-start(bf16[512,256]{1,0:T(8,128)(2,1)S(1)} %bitcast.108), channel_id=1, source_target_pairs={{0,4},{4,0},{8,12},{12,8},{1,5},{5,1},{9,13},{13,9},{2,6},{6,2},{1... | collective-permute-start | bytes 786440 | tf_op jit(solution)/shard_map/ppermute | solution.py:16

commit v2 on v0

v2 whole, which is shorter than its diff:
```python
import functools
import math

import jax
import jax.numpy as jnp
from jax import lax
from jax.experimental import pallas as pl
from jax.experimental.pallas import tpu as pltpu
from jax.sharding import PartitionSpec as P

HD = 128
CG = 128
RATE = 4
SEG = 256
MEM = 64
BF = jnp.bfloat16


def cost(microseconds):
    return pl.CostEstimate(flops=int(microseconds * 1.0e9), bytes_accessed=1000, transcendentals=0)
F32 = jnp.float32
ANY = pl.BlockSpec(memory_space=pl.ANY)
SMEM = pl.BlockSpec(memory_space=pltpu.SMEM)
VMEM = pl.BlockSpec(memory_space=pltpu.VMEM)


EARLY = 2


def swap(value, axis, distance, label):
    size = lax.axis_size(axis)
    with jax.named_scope("L_" + label):
        return lax.ppermute(value, axis, [(i, i ^ distance) for i in range(size)])


def after(value, *others):
    return lax.optimization_barrier((value,) + others)[0]


def run_copies(copies):
    for copy in copies:
        copy.start()
    for copy in copies:
        copy.wait()


def aligned(index, size):
    return pl.ds(pl.multiple_of(index * size, size), size)


def split_kernel(wk, wv, wq, kv_same, kv_other, q_same, q_other, sems):
    group, parity = lax.axis_index("groups"), lax.axis_index("seq") & 1
    half, width = q_same.shape
    rows = aligned(group, half)
    copies = []
    for target, kv, q in ((parity, kv_same, q_same), (1 - parity, kv_other, q_other)):
        columns = aligned(target, width)
        for source, dest in (
            (wk, kv.at[:, 0:width]),
            (wv, kv.at[:, width : 2 * width]),
            (wq, q),
        ):
            copies.append(pltpu.make_async_copy(source.at[rows, columns], dest, sems.at[len(copies)]))
    run_copies(copies)


def split_weights(wk, wv, wq):
    depth, columns = wk.shape
    half, width = depth // 2, columns // 2
    shapes = [(half, 2 * width), (half, 2 * width), (half, width), (half, width)]
    return pl.pallas_call(
        split_kernel,
        out_shape=[jax.ShapeDtypeStruct(s, BF) for s in shapes],
        in_specs=[ANY] * 3,
        out_specs=[VMEM] * 4,
        scratch_shapes=[pltpu.SemaphoreType.DMA((6,))],
        cost_estimate=cost(2),
        name="split_weights",
    )(wk, wv, wq)


def compress_kernel(own_ref, partner_ref, w_ref, out_ref):
    rows, channels = own_ref.shape
    count = rows // RATE
    row = lax.broadcasted_iota(jnp.int32, (count, rows), 0)
    column = lax.broadcasted_iota(jnp.int32, (count, rows), 1)
    taps = []
    for t in range(RATE):
        pick = (column == row * RATE + t).astype(BF)
        pair = [jnp.dot(pick, ref[...], preferred_element_type=F32).astype(BF) for ref in (own_ref, partner_ref)]
        taps.append(jnp.concatenate(pair, axis=0))
    for g in range(channels // CG):
        columns = slice(g * CG, (g + 1) * CG)
        total = jnp.zeros((2 * count, CG), F32)
        for t in range(RATE):
            weight = w_ref[t * CG : (t + 1) * CG, columns]
            total += jnp.dot(taps[t][:, columns], weight, preferred_element_type=F32)
        out_ref[:, columns] = total.astype(BF)


def compress(own, partner, conv_weight):
    count, channels = own.shape
    return pl.pallas_call(
        compress_kernel,
        out_shape=jax.ShapeDtypeStruct((2 * count // RATE, channels), BF),
        in_specs=[VMEM, VMEM, VMEM],
        out_specs=VMEM,
        cost_estimate=cost(5),
        name="compress",
    )(own, partner, conv_weight)


def weight_copies(planes, buffer, sems, owns, nears, fars):
    plane, group = lax.axis_index("seq"), lax.axis_index("groups")
    depth = owns[0][0].shape[0]
    half = depth // 2
    copies = []
    for ref, columns, place in owns:
        dest = buffer.at[aligned(plane, depth), place]
        copies.append(pltpu.make_async_copy(ref.at[:, columns], dest, sems.at[len(copies)]))
    for distance in range(1, planes):
        first = (plane ^ distance) * 2
        for ref, side in ((nears[distance - 1], group), (fars[distance - 1], 1 - group)):
            dest = buffer.at[aligned(first + side, half), :]
            copies.append(pltpu.make_async_copy(ref, dest, sems.at[len(copies)]))
    return copies


def block_owner(index, tensor_size, sub_size):
    tensor, sub = lax.axis_index("tensor"), lax.axis_index("sub")
    return (tensor ^ (index // sub_size)) * sub_size + (sub ^ (index % sub_size))


def project_kernel(planes, tensor_size, sub_size, counts, *refs):
    blocks, others = tensor_size * sub_size, planes - 1
    wk, wv = refs[:2]
    nears, fars, refs = refs[2 : 2 + others], refs[2 + others : 2 + 2 * others], refs[2 + 2 * others :]
    groups = [refs[i * blocks : (i + 1) * blocks] for i in range(len(counts))]
    out, xbuf, wbuf, acc, xsem, wsem = refs[len(counts) * blocks :]
    width = wbuf.shape[1] // 2
    columns = aligned(lax.axis_index("seq") & 1, width)
    owns = [(wk, columns, slice(0, width)), (wv, columns, slice(width, 2 * width))]
    wcopies = weight_copies(planes, wbuf, wsem, owns, nears, fars)
    for copy in wcopies:
        copy.start()
    xcopies = []
    for j in range(blocks):
        row = 0
        for i, count in enumerate(counts):
            dest = xbuf.at[j, row : row + count, :]
            xcopies.append(pltpu.make_async_copy(groups[i][j], dest, xsem.at[len(xcopies)]))
            xcopies[-1].start()
            row += count
    for copy in wcopies:
        copy.wait()
    product_loop(tensor_size, sub_size, counts, xcopies, xbuf, wbuf, acc, out)


def product_loop(tensor_size, sub_size, counts, xcopies, xbuf, wbuf, acc, out):
    blocks, chunk = xbuf.shape[0], xbuf.shape[2]
    for j in range(blocks):
        weight = aligned(block_owner(j, tensor_size, sub_size), chunk)
        row = 0
        for i, count in enumerate(counts):
            rows = slice(row, row + count)
            row += count
            xcopies[j * len(counts) + i].wait()
            part = jnp.dot(xbuf[j, rows, :], wbuf[weight, :], preferred_element_type=F32)
            if j:
                part += acc[rows, :]
            if j < blocks - 1:
                acc[rows, :] = part
            else:
                out[rows, :] = part.astype(BF)


def project(planes, tensor_size, sub_size, wk, wv, nears, fars, groups, name):
    depth, columns = wk.shape
    blocks = tensor_size * sub_size
    counts = [g[0].shape[0] for g in groups]
    chunk, total = groups[0][0].shape[1], sum(counts)
    operands = [wk, wv, *nears, *fars] + [block for g in groups for block in g]
    return pl.pallas_call(
        functools.partial(project_kernel, planes, tensor_size, sub_size, counts),
        out_shape=jax.ShapeDtypeStruct((total, columns), BF),
        in_specs=[ANY] * len(operands),
        out_specs=VMEM,
        scratch_shapes=[
            pltpu.VMEM((blocks, total, chunk), BF),
            pltpu.VMEM((depth * planes, columns), BF),
            pltpu.VMEM((total, columns), F32),
            pltpu.SemaphoreType.DMA((len(groups) * blocks,)),
            pltpu.SemaphoreType.DMA((2 + 2 * (planes - 1),)),
        ],
        compiler_params=pltpu.CompilerParams(vmem_limit_bytes=62 << 20),
        cost_estimate=cost(2 + total // 128),
        name=name,
    )(*operands)


def attend_kernel(side, planes, tensor_size, sub_size, *refs):
    blocks, others = tensor_size * sub_size, planes - 1
    segments, length, wq = refs[:3]
    refs = refs[3:]
    nears, fars, refs = refs[:others], refs[others : 2 * others], refs[2 * others :]
    xs, refs = refs[:blocks], refs[blocks:]
    kv_tok, refs = refs[0], refs[1:]
    mems, refs = refs[: planes // 2], refs[planes // 2 :]
    out, xbuf, wbuf, acc, qbuf, kvbuf, membuf, xsem, wsem, ksem = refs
    plane = lax.axis_index("seq")
    width = wbuf.shape[1]
    rows_here = out.shape[0]
    slots = rows_here // SEG
    owns = [(wq, aligned(plane & 1, width), slice(0, width))]
    wcopies = weight_copies(planes, wbuf, wsem, owns, nears, fars)
    xcopies = [pltpu.make_async_copy(xs[j], xbuf.at[j], xsem.at[j]) for j in range(blocks)]
    kcopies = [pltpu.make_async_copy(kv_tok.at[pl.ds(side * rows_here, rows_here), :], kvbuf, ksem.at[0])]
    count = mems[0].shape[0]
    for i, mem in enumerate(mems):
        kcopies.append(pltpu.make_async_copy(mem, membuf.at[pl.ds(i * count, count), :], ksem.at[1 + i]))
    for copy in wcopies + xcopies + kcopies:
        copy.start()
    per_plane = count // 2
    mem_total = membuf.shape[0]
    column = lax.broadcasted_iota(jnp.int32, (1, mem_total), 1)
    owner = jnp.zeros((1, mem_total), jnp.int32)
    for distance in range(planes):
        for i in range(slots):
            start = distance * per_plane + i * MEM
            here = (column >= start) & (column < start + MEM)
            owner = jnp.where(here, segments[(plane ^ distance) * slots + i], owner)
    row = lax.broadcasted_iota(jnp.int32, (SEG, SEG), 0)
    causal = row >= lax.broadcasted_iota(jnp.int32, (SEG, SEG), 1)
    position = lax.broadcasted_iota(jnp.int32, (SEG, HD), 0)
    contract = (((1,), (1,)), ((), ()))
    scale = HD ** (-0.5) * math.log2(math.e)
    for copy in wcopies:
        copy.wait()
    product_loop(tensor_size, sub_size, [rows_here], xcopies, xbuf, wbuf, acc, qbuf)
    for copy in kcopies:
        copy.wait()
    for a in range(slots):
        rows = slice(a * SEG, (a + 1) * SEG)
        segment = segments[(plane ^ side) * slots + a]
        allowed = owner < segment
        valid = position + segment * SEG < length[0]
        for h in range(width // HD):
            ks, vs = slice(h * HD, (h + 1) * HD), slice(width + h * HD, width + (h + 1) * HD)
            query = qbuf[rows, ks]
            near = lax.dot_general(query, kvbuf[rows, ks], contract, preferred_element_type=F32)
            far = lax.dot_general(query, membuf[:, ks], contract, preferred_element_type=F32)
            near = jnp.where(causal, near * scale, -jnp.inf)
            far = jnp.where(allowed, far * scale, -jnp.inf)
            best = jnp.maximum(
                jnp.max(near, axis=1, keepdims=True), jnp.max(far, axis=1, keepdims=True)
            )
            near, far = jnp.exp2(near - best), jnp.exp2(far - best)
            denominator = jnp.sum(near, axis=1, keepdims=True) + jnp.sum(far, axis=1, keepdims=True)
            numerator = jnp.dot(near.astype(BF), kvbuf[rows, vs], preferred_element_type=F32)
            numerator += jnp.dot(far.astype(BF), membuf[:, vs], preferred_element_type=F32)
            out[rows, ks] = jnp.where(valid, numerator / denominator, 0.0).astype(BF)


def attend(side, planes, tensor_size, sub_size, segments, length, wq, nears, fars, xs, kv_tok, mems):
    depth, columns = wq.shape
    width = columns // 2
    rows, chunk = xs[0].shape
    blocks = tensor_size * sub_size
    mem_total = len(mems) * mems[0].shape[0]
    operands = [segments, length, wq, *nears, *fars, *xs, kv_tok, *mems]
    return pl.pallas_call(
        functools.partial(attend_kernel, side, planes, tensor_size, sub_size),
        out_shape=jax.ShapeDtypeStruct((rows, width), BF),
        in_specs=[SMEM, SMEM] + [ANY] * (len(operands) - 2),
        out_specs=VMEM,
        scratch_shapes=[
            pltpu.VMEM((blocks, rows, chunk), BF),
            pltpu.VMEM((depth * planes, width), BF),
            pltpu.VMEM((rows, width), F32),
            pltpu.VMEM((rows, width), BF),
            pltpu.VMEM((rows, 2 * width), BF),
            pltpu.VMEM((mem_total, 2 * width), BF),
            pltpu.SemaphoreType.DMA((blocks,)),
            pltpu.SemaphoreType.DMA((1 + 2 * (planes - 1),)),
            pltpu.SemaphoreType.DMA((1 + len(mems),)),
        ],
        compiler_params=pltpu.CompilerParams(vmem_limit_bytes=62 << 20),
        cost_estimate=cost(8),
        name="attend",
    )(*operands)


def on_device(
    activations, conv_weight, query_weight, key_weight, value_weight, segment_for_slot, book_length
):
    planes, tensor_size, sub_size = (lax.axis_size(name) for name in ("seq", "tensor", "sub"))
    parity = lax.axis_index("seq") & 1

    kv_same, kv_other, q_same, q_other = split_weights(key_weight, value_weight, query_weight)

    def across(block, label):
        return {f"{label}x{k}": (block, "tensor", k) for k in range(1, tensor_size)}

    def within(block, label):
        return {f"{label}c{k}": (block, "sub", k) for k in range(1, sub_size)}

    def distant(distances, name):
        same, other = {"kv": (kv_same, kv_other), "q": (q_same, q_other)}[name]
        return {f"{name}{d}": (other if d & 1 else same, "seq", d) for d in distances}

    def relayed(distances, name):
        return {f"y{name}{d}": (got[f"{name}{d}"], "groups", 1) for d in distances}

    got = {}

    def stage(sends, *computed):
        held = tuple(got[key] for key in fresh)
        new = {}
        for key, (value, axis, distance) in sends.items():
            new[key] = swap(after(value, *held), axis, distance, key)
        ended = lax.optimization_barrier(tuple(new.values()) + computed)
        got.update(zip(new, ended))
        fresh[:] = list(new)
        return ended[len(new) :]

    fresh = []
    every = range(1, planes)
    first = [2] if planes > 2 else []
    second = [d for d in every if d not in first]
    stage(
        {"Xz": (activations, "seq", 1)}
        | across(activations, "A")
        | within(activations, "A0")
        | distant(first, "kv")
    )
    partner = got["Xz"]
    sends = across(partner, "B") | within(partner, "B0") | distant(second, "kv") | relayed(first, "kv")
    for k in range(1, tensor_size):
        sends |= within(got[f"Ax{k}"], f"A{k}")
    (both,) = stage(sends, compress(activations, partner, conv_weight))
    sends = across(both, "C") | within(both, "C0") | distant(every, "q") | relayed(second, "kv")
    for k in range(1, tensor_size):
        sends |= within(got[f"Bx{k}"], f"B{k}")
    stage(sends)
    sends = relayed(every, "q")
    for k in range(1, tensor_size):
        sends |= within(got[f"Cx{k}"], f"C{k}")
    held = tuple(got[key] for key in fresh)
    for key, (value, axis, distance) in sends.items():
        got[key] = swap(after(value, *held), axis, distance, key)

    def pieces(block, label):
        whole = []
        for k in range(tensor_size):
            whole.append(got[f"{label}x{k}"] if k else block)
            whole += [got[f"{label}{k}c{u}"] for u in range(1, sub_size)]
        return whole

    own_pieces, partner_pieces = pieces(activations, "A"), pieces(partner, "B")
    compressed_pieces = pieces(both, "C")
    near_kv, far_kv = ({d: got[f"{y}kv{d}"] for d in every} for y in ("", "y"))
    near_q, far_q = ({d: got[f"{y}q{d}"] for d in every} for y in ("", "y"))

    distances = range(1, planes)
    sizes = (planes, tensor_size, sub_size)
    kv_parts = ([near_kv[d] for d in distances], [far_kv[d] for d in distances])
    kv_mem = project(*sizes, key_weight, value_weight, *kv_parts, (compressed_pieces,), "project_memory")
    mems = [kv_mem] + [swap(kv_mem, "seq", d, f"m{d}") for d in range(2, planes, 2)]
    kv_tok = project(
        *sizes, after(key_weight, kv_mem), value_weight, *kv_parts, (own_pieces, partner_pieces), "project_tokens"
    )
    shared = (
        query_weight,
        [near_q[d] for d in distances],
        [far_q[d] for d in distances],
    )
    theirs = attend(1, *sizes, segment_for_slot, book_length, *shared, partner_pieces, kv_tok, mems)
    returned = swap(theirs, "seq", 1, "ctx")
    mine = attend(0, *sizes, segment_for_slot, book_length, *shared, own_pieces, kv_tok, mems)
    width = mine.shape[1]
    result = jnp.concatenate([mine, mine], axis=1)
    return lax.dynamic_update_slice(result, returned, (0, (1 - parity) * width))


def solution(mesh):
    placed = (
        P(("groups", "seq"), ("tensor", "sub")),
        P(None, ("tensor", "sub")),
        P("seq", ("tensor", "sub")),
        P("seq", ("tensor", "sub")),
        P("seq", ("tensor", "sub")),
        P("groups"),
        P("groups"),
    )
    return jax.shard_map(
        on_device,
        mesh=mesh,
        in_specs=placed,
        out_specs=P(("groups", "seq"), ("tensor", "sub")),
        check_vma=False,
    )
```

time: 351 us -> 142 us (0.40)
  waiting for transfers between devices: 261 us -> 67.9 us
  Pallas kernels: 0 us -> 39.9 us
  blocking collectives: 36.6 us -> 0 us
  matrix products: 29.6 us -> 0 us
  starting transfers between devices: 0.16 us -> 29.5 us
  between operations: 14 us -> 0.81 us
    all_gather x5 -> x0, waiting for transfers between devices: 258 us -> none  [the longest x1 82.4 us: on_device(): key_matrix_rows = lax.all_gather(key_weight, 'seq', axis=0, tiled=True)]
    ppermute x0 -> x24, waiting for transfers between devices: none -> 67.9 us  [swap(): return lax.ppermute(value, axis, [(i, i ^ distance) for i in range(size)])]
    pallas_call x0 -> x6, Pallas kernels: none -> 39.9 us  [the longest x2 17.7 us: attend(): pl.pallas_call(functools.partial(attend_kernel, side, planes, tensor_size...]
    all_gather x2 -> x0, blocking collectives: 36.6 us -> none  [the longest x1 21.4 us: on_device(): lax.all_gather(keys_mem, 'seq', axis=0, tiled=True)]
    dot_general x10 -> x0, matrix products: 29.6 us -> none  [the longest x5 23.6 us: add_product(): return jnp.dot(source, weight_rows, preferred_element_type=jnp.float32)]
    ppermute x0 -> x24, starting transfers between devices: none -> 29.5 us  [swap(): return lax.ppermute(value, axis, [(i, i ^ distance) for i in range(size)])]
  transfers between devices with their start and end apart: 5 -> 24, of which waited for: 5 -> 11; matrix products, arithmetic and copies ran while one was open for 6% -> 1% of each run, Pallas kernels for 0% -> 22%
where the time goes in v2:
time: 142 us
  waiting for transfers between devices  67.9 us (48%)
  Pallas kernels  39.9 us (28%)
  starting transfers between devices  29.5 us (21%)
  local copies, waits for them, and re-layouts  2.14 us (2%)
  other arithmetic  1.86 us (1%)
    ppermute x24, waiting for transfers between devices, swap(): return lax.ppermute(value, axis, [(i, i ^ distance) for i in range(size)])  67.9 us
    ppermute x24, starting transfers between devices, swap(): return lax.ppermute(value, axis, [(i, i ^ distance) for i in range(size)])  29.5 us
    pallas_call x2, Pallas kernels, attend(): pl.pallas_call(functools.partial(attend_kernel, side, planes, tensor_size...  17.7 us
    pallas_call x2, Pallas kernels, project(): pl.pallas_call(functools.partial(project_kernel, planes, tensor_size, sub...  15.2 us
    pallas_call x1, Pallas kernels, compress(): pl.pallas_call(compress_kernel, out_shape=jax.ShapeDtypeStruct((2 * count...  4.48 us
  transfers between devices with their start and end apart: 24, of which 11 were waited for; matrix products, arithmetic and copies ran while one was open for 1% of the time, Pallas kernels for 22%

profile of v2, /device:TPU:0, one launch (start us, length us, event | category | flops | bytes accessed | tf_op | source)
XLA Modules:
  0.0 142.1 jit_solution(1002582237019812475)
XLA Ops:
  0.0 3.0 %collective-permute-start = (bf16[512,1024]{1,0:T(8,128)(2,1)}, bf16[512,1024]{1,0:T(8,128)(2,1)}, u32[]{:S(2)}, u32[]{:S(2)}) collective-permute-start(bf16[512,1024]{1,0:T(8,128)(2,1)} %refs_9_.1), channel_id=1, source_target_pairs={{0,4},{4,0},{8,12},{12,8},{1,5},{5,1},{9,13},{13,9},{2,6},{6,2},{1... | collective-permute-start | bytes 3145736 | tf_op jit(solution)/shard_map/L_Xz/ppermute | solution.py:33
  3.0 1.5 %collective-permute-start.1 = (bf16[512,1024]{1,0:T(8,128)(2,1)}, bf16[512,1024]{1,0:T(8,128)(2,1)S(1)}, u32[]{:S(2)}, u32[]{:S(2)}) collective-permute-start(bf16[512,1024]{1,0:T(8,128)(2,1)} %refs_9_.1), channel_id=1, source_target_pairs={{0,2},{2,0},{1,3},{3,1},{4,6},{6,4},{5,7},{7,5},{8,10},{10,8},{9,1... | collective-permute-start | bytes 3145736 | tf_op jit(solution)/shard_map/L_Ax1/ppermute | solution.py:33
  4.5 0.0 collective-permute-start.2
  4.5 2.5 %split_weights.1 = (bf16[512,512]{1,0:T(8,128)(2,1)}, bf16[512,512]{1,0:T(8,128)(2,1)}, bf16[512,256]{1,0:T(8,128)(2,1)}, bf16[512,256]{1,0:T(8,128)(2,1)}) custom-call(bf16[1024,512]{1,0:T(8,128)(2,1)} %refs_0_.4, bf16[1024,512]{1,0:T(8,128)(2,1)} %refs_1_.5, bf16[1024,512]{1,0:T(8,128)(2,1)} %refs_2_.3), custom_call_target="tpu_custom_call" | custom-call | flops 2000000000 | bytes 1000 | tf_op jit(solution)/shard_map/split_weights/pallas_call | solution.py:71
  7.1 2.7 %collective-permute-start.3 = (bf16[512,512]{1,0:T(8,128)(2,1)}, bf16[512,512]{1,0:T(8,128)(2,1)S(1)}, u32[]{:S(2)}, u32[]{:S(2)}) collective-permute-start(bf16[512,512]{1,0:T(8,128)(2,1)} %get-tuple-element.43), channel_id=1, source_target_pairs={{0,8},{4,12},{8,0},{12,4},{1,9},{5,13},{9,1},{13,5},{2,10},{6,14},... | collective-permute-start | bytes 1572872 | tf_op jit(solution)/shard_map/L_kv2/ppermute | solution.py:33
  9.7 27.3 %collective-permute-done.3.refs_3_ = bf16[512,512]{1,0:T(8,128)(2,1)S(1)} collective-permute-done((bf16[512,512]{1,0:T(8,128)(2,1)}, bf16[512,512]{1,0:T(8,128)(2,1)S(1)}, u32[]{:S(2)}, u32[]{:S(2)}) %collective-permute-start.3) | collective-permute-done | bytes 524320 | tf_op jit(solution)/shard_map/L_kv2/ppermute | solution.py:33
  37.0 0.7 collective-permute-done.partner_ref.refs_12_.refs_9_
  37.7 0.0 collective-permute-done.1.refs_10_.refs_11_
  37.7 0.0 collective-permute-done.2.refs_9_.refs_10_
  37.7 0.0 copy-start.1
  37.8 2.7 %collective-permute-start.6 = (bf16[512,512]{1,0:T(8,128)(2,1)}, bf16[512,512]{1,0:T(8,128)(2,1)S(1)}, u32[]{:S(2)}, u32[]{:S(2)}) collective-permute-start(bf16[512,512]{1,0:T(8,128)(2,1)} %get-tuple-element.50), channel_id=1, source_target_pairs={{0,4},{4,0},{8,12},{12,8},{1,5},{5,1},{9,13},{13,9},{2,6},{6,2},{1... | collective-permute-start | bytes 1572872 | tf_op jit(solution)/shard_map/L_kv1/ppermute | solution.py:33
  40.5 1.5 %collective-permute-start.4 = (bf16[512,1024]{1,0:T(8,128)(2,1)}, bf16[512,1024]{1,0:T(8,128)(2,1)}, u32[]{:S(2)}, u32[]{:S(2)}) collective-permute-start(bf16[512,1024]{1,0:T(8,128)(2,1)} %collective-permute-done.partner_ref.refs_12_.refs_9_), channel_id=1, source_target_pairs={{0,2},{2,0},{1,3},{3,1},{4,6},{6,4},{5,7},{7,5},{8,10},{10,8},{9,1... | collective-permute-start | bytes 3145736 | tf_op jit(solution)/shard_map/L_Bx1/ppermute | solution.py:33
  42.0 0.0 collective-permute-start.5
  42.0 0.5 collective-permute-start.9
  42.5 1.3 collective-permute-start.7
  43.8 9.3 %collective-permute-done.6.refs_2_ = bf16[512,512]{1,0:T(8,128)(2,1)S(1)} collective-permute-done((bf16[512,512]{1,0:T(8,128)(2,1)}, bf16[512,512]{1,0:T(8,128)(2,1)S(1)}, u32[]{:S(2)}, u32[]{:S(2)}) %collective-permute-start.6) | collective-permute-done | bytes 524320 | tf_op jit(solution)/shard_map/L_kv1/ppermute | solution.py:33
  53.2 1.5 %collective-permute-start.8 = (bf16[512,512]{1,0:T(8,128)(2,1)S(1)}, bf16[512,512]{1,0:T(8,128)(2,1)}, u32[]{:S(2)}, u32[]{:S(2)}) collective-permute-start(bf16[512,512]{1,0:T(8,128)(2,1)S(1)} %collective-permute-done.3.refs_3_), channel_id=1, source_target_pairs={{0,16},{16,0},{1,17},{17,1},{2,18},{18,2},{3,19},{19,3},{4,20},{20... | collective-permute-start | bytes 1572872 | tf_op jit(solution)/shard_map/L_ykv2/ppermute | solution.py:33
  54.7 4.5 %compress.1.refs_8_ = bf16[256,1024]{1,0:T(8,128)(2,1)} custom-call(bf16[512,1024]{1,0:T(8,128)(2,1)} %refs_9_.1, bf16[512,1024]{1,0:T(8,128)(2,1)} %collective-permute-done.partner_ref.refs_12_.refs_9_, bf16[512,1024]{1,0:T(8,128)(2,1)} %w_ref.1), custom_call_target="tpu_custom_call" | custom-call | flops 5000000000 | bytes 1000 | tf_op jit(solution)/shard_map/compress/pallas_call | solution.py:103
  59.2 0.0 copy-done.3
  59.2 0.0 copy-done
  59.2 0.0 copy-done.1
  59.2 5.1 %collective-permute-done.7.refs_4_ = bf16[512,512]{1,0:T(8,128)(2,1)} collective-permute-done((bf16[512,512]{1,0:T(8,128)(2,1)}, bf16[512,512]{1,0:T(8,128)(2,1)}, u32[]{:S(2)}, u32[]{:S(2)}) %collective-permute-start.7) | collective-permute-done | bytes 524320 | tf_op jit(solution)/shard_map/L_kv3/ppermute | solution.py:33
  64.3 0.0 collective-permute-done.8.refs_6_
  64.3 0.3 collective-permute-done.4.refs_14_.refs_11_
  64.6 0.0 collective-permute-done.5.refs_13_.refs_10_
  64.6 0.0 collective-permute-done.9.refs_11_.refs_12_
  64.6 0.0 collective-permute-start.17
  64.6 5.1 %collective-permute-start.13 = (bf16[512,256]{1,0:T(8,128)(2,1)}, bf16[512,256]{1,0:T(8,128)(2,1)S(1)}, u32[]{:S(2)}, u32[]{:S(2)}) collective-permute-start(bf16[512,256]{1,0:T(8,128)(2,1)} %get-tuple-element.64), channel_id=1, source_target_pairs={{0,8},{4,12},{8,0},{12,4},{1,9},{5,13},{9,1},{13,5},{2,10},{6,14},... | collective-permute-start | bytes 786440 | tf_op jit(solution)/shard_map/L_q2/ppermute | solution.py:33
  69.7 0.0 collective-permute-start.12
  69.7 1.6 %collective-permute-start.14 = (bf16[512,256]{1,0:T(8,128)(2,1)}, bf16[512,256]{1,0:T(8,128)(2,1)}, u32[]{:S(2)}, u32[]{:S(2)}) collective-permute-start(bf16[512,256]{1,0:T(8,128)(2,1)} %get-tuple-element.62), channel_id=1, source_target_pairs={{0,12},{4,8},{8,4},{12,0},{1,13},{5,9},{9,5},{13,1},{2,14},{6,10},... | collective-permute-start | bytes 786440 | tf_op jit(solution)/shard_map/L_q3/ppermute | solution.py:33
  71.3 1.5 %collective-permute-start.16 = (bf16[512,512]{1,0:T(8,128)(2,1)}, bf16[512,512]{1,0:T(8,128)(2,1)S(1)}, u32[]{:S(2)}, u32[]{:S(2)}) collective-permute-start(bf16[512,512]{1,0:T(8,128)(2,1)} %collective-permute-done.7.refs_4_), channel_id=1, source_target_pairs={{0,16},{16,0},{1,17},{17,1},{2,18},{18,2},{3,19},{19,3},{4,20},{20... | collective-permute-start | bytes 1572872 | tf_op jit(solution)/shard_map/L_ykv3/ppermute | solution.py:33
  72.8 10.0 %collective-permute-done.13.refs_4_ = bf16[512,256]{1,0:T(8,128)(2,1)S(1)} collective-permute-done((bf16[512,256]{1,0:T(8,128)(2,1)}, bf16[512,256]{1,0:T(8,128)(2,1)S(1)}, u32[]{:S(2)}, u32[]{:S(2)}) %collective-permute-start.13) | collective-permute-done | bytes 262176 | tf_op jit(solution)/shard_map/L_q2/ppermute | solution.py:33
  82.7 0.0 copy-done.4
  82.7 1.5 %collective-permute-start.15 = (bf16[512,512]{1,0:T(8,128)(2,1)S(1)}, bf16[512,512]{1,0:T(8,128)(2,1)S(1)}, u32[]{:S(2)}, u32[]{:S(2)}) collective-permute-start(bf16[512,512]{1,0:T(8,128)(2,1)S(1)} %collective-permute-done.6.refs_2_), channel_id=1, source_target_pairs={{0,16},{16,0},{1,17},{17,1},{2,18},{18,2},{3,19},{19,3},{4,20},{20... | collective-permute-start | bytes 1572872 | tf_op jit(solution)/shard_map/L_ykv1/ppermute | solution.py:33
  84.3 0.0 collective-permute-done.12.refs_3_
  84.3 0.5 collective-permute-start.10
  84.8 4.4 %collective-permute-done.14.refs_5_ = bf16[512,256]{1,0:T(8,128)(2,1)} collective-permute-done((bf16[512,256]{1,0:T(8,128)(2,1)}, bf16[512,256]{1,0:T(8,128)(2,1)}, u32[]{:S(2)}, u32[]{:S(2)}) %collective-permute-start.14) | collective-permute-done | bytes 262176 | tf_op jit(solution)/shard_map/L_q3/ppermute | solution.py:33
  89.2 0.0 collective-permute-start.11
  89.2 0.0 collective-permute-done.16.refs_7_
  89.2 7.1 %collective-permute-done.15.refs_5_ = bf16[512,512]{1,0:T(8,128)(2,1)S(1)} collective-permute-done((bf16[512,512]{1,0:T(8,128)(2,1)S(1)}, bf16[512,512]{1,0:T(8,128)(2,1)S(1)}, u32[]{:S(2)}, u32[]{:S(2)}) %collective-permute-start.15) | collective-permute-done | bytes 524320 | tf_op jit(solution)/shard_map/L_ykv1/ppermute | solution.py:33
  96.3 1.4 collective-permute-done.10.refs_10_
  97.7 0.0 collective-permute-done.11.refs_9_
  97.7 0.0 collective-permute-done.17.refs_15_.refs_12_
  97.7 0.0 copy-done.6
  97.8 0.1 collective-permute-start.21
  97.8 0.7 copy-done.7
  99.2 0.6 collective-permute-start.20
  99.7 1.5 %collective-permute-start.19 = (bf16[512,256]{1,0:T(8,128)(2,1)S(1)}, bf16[512,256]{1,0:T(8,128)(2,1)}, u32[]{:S(2)}, u32[]{:S(2)}) collective-permute-start(bf16[512,256]{1,0:T(8,128)(2,1)S(1)} %collective-permute-done.13.refs_4_), channel_id=1, source_target_pairs={{0,16},{16,0},{1,17},{17,1},{2,18},{18,2},{3,19},{19,3},{4,20},{20... | collective-permute-start | bytes 786440 | tf_op jit(solution)/shard_map/L_yq2/ppermute | solution.py:33
  101.3 0.5 collective-permute-start.18
  101.8 0.0 collective-permute-done.21.refs_11_
  101.8 4.8 %project_memory.1.refs_14_ = bf16[256,512]{1,0:T(8,128)(2,1)} custom-call(bf16[1024,512]{1,0:T(8,128)(2,1)} %refs_0_.4, bf16[1024,512]{1,0:T(8,128)(2,1)} %refs_1_.5, bf16[512,512]{1,0:T(8,128)(2,1)} %copy-done.4, bf16[512,512]{1,0:T(8,128)(2,1)} %copy-done.3, bf16[512,512]{1,0:T(8,128)(2,1)} %collective-permute-done.7.refs_4_, bf16[512,512]{1,0:T(8,128)(2,1)} %copy-done.6, ...), custom_call_target="tpu_custom_call" | custom-call | flops 4000000000 | bytes 1000 | tf_op jit(solution)/shard_map/project_memory/pallas_call | solution.py:183
  106.6 1.7 %collective-permute-start.22 = (bf16[256,512]{1,0:T(8,128)(2,1)}, bf16[256,512]{1,0:T(8,128)(2,1)S(1)}, u32[]{:S(2)}, u32[]{:S(2)}) collective-permute-start(bf16[256,512]{1,0:T(8,128)(2,1)} %project_memory.1.refs_14_), channel_id=1, source_target_pairs={{0,8},{4,12},{8,0},{12,4},{1,9},{5,13},{9,1},{13,5},{2,10},{6,14},... | collective-permute-start | bytes 786440 | tf_op jit(solution)/shard_map/L_m2/ppermute | solution.py:33
  108.3 10.3 %project_tokens.1.refs_13_ = bf16[1024,512]{1,0:T(8,128)(2,1)} custom-call(bf16[1024,512]{1,0:T(8,128)(2,1)} %refs_0_.4, bf16[1024,512]{1,0:T(8,128)(2,1)} %refs_1_.5, bf16[512,512]{1,0:T(8,128)(2,1)} %copy-done.4, bf16[512,512]{1,0:T(8,128)(2,1)} %copy-done.3, bf16[512,512]{1,0:T(8,128)(2,1)} %collective-permute-done.7.refs_4_, bf16[512,512]{1,0:T(8,128)(2,1)} %copy-done.6, ...), custom_call_target="tpu_custom_call" | custom-call | flops 10000000000 | bytes 1000 | tf_op jit(solution)/shard_map/project_tokens/pallas_call | solution.py:183
  118.6 0.0 collective-permute-done.20.refs_8_
  118.7 0.0 collective-permute-done.19.refs_7_
  118.7 0.2 collective-permute-done.18.refs_6_
  118.8 2.1 %collective-permute-done.22.refs_15_ = bf16[256,512]{1,0:T(8,128)(2,1)S(1)} collective-permute-done((bf16[256,512]{1,0:T(8,128)(2,1)}, bf16[256,512]{1,0:T(8,128)(2,1)S(1)}, u32[]{:S(2)}, u32[]{:S(2)}) %collective-permute-start.22) | collective-permute-done | bytes 262176 | tf_op jit(solution)/shard_map/L_m2/ppermute | solution.py:33
  120.9 0.7 copy-done.9
  121.6 8.9 %attend.3 = bf16[512,256]{1,0:T(8,128)(2,1)} custom-call(s32[8]{0:T(128)} %refs_0_.6, s32[1]{0:T(128)S(6)} %copy.9.refs_1_, bf16[1024,512]{1,0:T(8,128)(2,1)} %refs_2_.3, bf16[512,256]{1,0:T(8,128)(2,1)} %collective-permute-done.12.refs_3_, bf16[512,256]{1,0:T(8,128)(2,1)} %copy-done.8, bf16[512,256]{1,0:T(8,128)(2,1)} %collective-permute-done.14.refs_5_, ...), custom_call_target="tpu_custom_call" | custom-call | flops 8000000000 | bytes 1000 | tf_op jit(solution)/shard_map/attend/pallas_call | solution.py:271
  130.5 0.1 collective-permute-start.23
  130.6 8.9 %attend.2 = bf16[512,256]{1,0:T(8,128)(2,1)} custom-call(s32[8]{0:T(128)} %refs_0_.6, s32[1]{0:T(128)S(6)} %copy.9.refs_1_, bf16[1024,512]{1,0:T(8,128)(2,1)} %refs_2_.3, bf16[512,256]{1,0:T(8,128)(2,1)} %collective-permute-done.12.refs_3_, bf16[512,256]{1,0:T(8,128)(2,1)} %copy-done.8, bf16[512,256]{1,0:T(8,128)(2,1)} %collective-permute-done.14.refs_5_, ...), custom_call_target="tpu_custom_call" | custom-call | flops 8000000000 | bytes 1000 | tf_op jit(solution)/shard_map/attend/pallas_call | solution.py:271
  139.5 1.9 %pad_maximum_fusion = bf16[512,512]{1,0:T(8,128)(2,1)} fusion(bf16[512,256]{1,0:T(8,128)(2,1)} %attend.2), kind=kLoop, calls=%fused_computation | loop fusion | flops 1048576 | bytes 786432 | tf_op jit(solution)/shard_map/concatenate | solution.py:381
  141.3 0.0 collective-permute-done.23
  141.4 0.7 constant_dynamic-update-slice_fusion
  (12 shorter events, 0.0 us)
Async XLA Ops:
  0.0 37.7 %collective-permute-start = (bf16[512,1024]{1,0:T(8,128)(2,1)}, bf16[512,1024]{1,0:T(8,128)(2,1)}, u32[]{:S(2)}, u32[]{:S(2)}) collective-permute-start(bf16[512,1024]{1,0:T(8,128)(2,1)} %refs_9_.1), channel_id=1, source_target_pairs={{0,4},{4,0},{8,12},{12,8},{1,5},{5,1},{9,13},{13,9},{2,6},{6,2},{1... | collective-permute-start | bytes 3145736 | tf_op jit(solution)/shard_map/L_Xz/ppermute | solution.py:33
  3.0 34.7 %collective-permute-start.1 = (bf16[512,1024]{1,0:T(8,128)(2,1)}, bf16[512,1024]{1,0:T(8,128)(2,1)S(1)}, u32[]{:S(2)}, u32[]{:S(2)}) collective-permute-start(bf16[512,1024]{1,0:T(8,128)(2,1)} %refs_9_.1), channel_id=1, source_target_pairs={{0,2},{2,0},{1,3},{3,1},{4,6},{6,4},{5,7},{7,5},{8,10},{10,8},{9,1... | collective-permute-start | bytes 3145736 | tf_op jit(solution)/shard_map/L_Ax1/ppermute | solution.py:33
  4.5 33.2 %collective-permute-start.2 = (bf16[512,1024]{1,0:T(8,128)(2,1)}, bf16[512,1024]{1,0:T(8,128)(2,1)S(1)}, u32[]{:S(2)}, u32[]{:S(2)}) collective-permute-start(bf16[512,1024]{1,0:T(8,128)(2,1)} %refs_9_.1), channel_id=1, source_target_pairs={{0,1},{1,0},{2,3},{3,2},{4,5},{5,4},{6,7},{7,6},{8,9},{9,8},{10,11... | collective-permute-start | bytes 3145736 | tf_op jit(solution)/shard_map/L_A0c1/ppermute | solution.py:33
  7.1 29.9 %collective-permute-start.3 = (bf16[512,512]{1,0:T(8,128)(2,1)}, bf16[512,512]{1,0:T(8,128)(2,1)S(1)}, u32[]{:S(2)}, u32[]{:S(2)}) collective-permute-start(bf16[512,512]{1,0:T(8,128)(2,1)} %get-tuple-element.43), channel_id=1, source_target_pairs={{0,8},{4,12},{8,0},{12,4},{1,9},{5,13},{9,1},{13,5},{2,10},{6,14},... | collective-permute-start | bytes 1572872 | tf_op jit(solution)/shard_map/L_kv2/ppermute | solution.py:33
  37.0 22.2 %copy-start.3 = (bf16[512,512]{1,0:T(8,128)(2,1)}, bf16[512,512]{1,0:T(8,128)(2,1)S(1)}, u32[]{:S(2)}) copy-start(bf16[512,512]{1,0:T(8,128)(2,1)S(1)} %collective-permute-done.3.refs_3_) | copy-start | bytes 1572868
  37.7 21.5 %copy-start = (bf16[512,1024]{1,0:T(8,128)(2,1)}, bf16[512,1024]{1,0:T(8,128)(2,1)S(1)}, u32[]{:S(2)}) copy-start(bf16[512,1024]{1,0:T(8,128)(2,1)S(1)} %collective-permute-done.1.refs_10_.refs_11_) | copy-start | bytes 3145732
  37.7 21.5 %copy-start.1 = (bf16[512,1024]{1,0:T(8,128)(2,1)}, bf16[512,1024]{1,0:T(8,128)(2,1)S(1)}, u32[]{:S(2)}) copy-start(bf16[512,1024]{1,0:T(8,128)(2,1)S(1)} %collective-permute-done.2.refs_9_.refs_10_) | copy-start | bytes 3145732
  37.8 15.4 %collective-permute-start.6 = (bf16[512,512]{1,0:T(8,128)(2,1)}, bf16[512,512]{1,0:T(8,128)(2,1)S(1)}, u32[]{:S(2)}, u32[]{:S(2)}) collective-permute-start(bf16[512,512]{1,0:T(8,128)(2,1)} %get-tuple-element.50), channel_id=1, source_target_pairs={{0,4},{4,0},{8,12},{12,8},{1,5},{5,1},{9,13},{13,9},{2,6},{6,2},{1... | collective-permute-start | bytes 1572872 | tf_op jit(solution)/shard_map/L_kv1/ppermute | solution.py:33
  40.5 24.1 %collective-permute-start.4 = (bf16[512,1024]{1,0:T(8,128)(2,1)}, bf16[512,1024]{1,0:T(8,128)(2,1)}, u32[]{:S(2)}, u32[]{:S(2)}) collective-permute-start(bf16[512,1024]{1,0:T(8,128)(2,1)} %collective-permute-done.partner_ref.refs_12_.refs_9_), channel_id=1, source_target_pairs={{0,2},{2,0},{1,3},{3,1},{4,6},{6,4},{5,7},{7,5},{8,10},{10,8},{9,1... | collective-permute-start | bytes 3145736 | tf_op jit(solution)/shard_map/L_Bx1/ppermute | solution.py:33
  42.0 22.6 %collective-permute-start.5 = (bf16[512,1024]{1,0:T(8,128)(2,1)}, bf16[512,1024]{1,0:T(8,128)(2,1)}, u32[]{:S(2)}, u32[]{:S(2)}) collective-permute-start(bf16[512,1024]{1,0:T(8,128)(2,1)} %collective-permute-done.partner_ref.refs_12_.refs_9_), channel_id=1, source_target_pairs={{0,1},{1,0},{2,3},{3,2},{4,5},{5,4},{6,7},{7,6},{8,9},{9,8},{10,11... | collective-permute-start | bytes 3145736 | tf_op jit(solution)/shard_map/L_B0c1/ppermute | solution.py:33
  42.0 22.6 %collective-permute-start.9 = (bf16[512,1024]{1,0:T(8,128)(2,1)S(1)}, bf16[512,1024]{1,0:T(8,128)(2,1)}, u32[]{:S(2)}, u32[]{:S(2)}) collective-permute-start(bf16[512,1024]{1,0:T(8,128)(2,1)S(1)} %collective-permute-done.1.refs_10_.refs_11_), channel_id=1, source_target_pairs={{0,1},{1,0},{2,3},{3,2},{4,5},{5,4},{6,7},{7,6},{8,9},{9,8},{10,11... | collective-permute-start | bytes 3145736 | tf_op jit(solution)/shard_map/L_A1c1/ppermute | solution.py:33
  42.5 21.8 %collective-permute-start.7 = (bf16[512,512]{1,0:T(8,128)(2,1)}, bf16[512,512]{1,0:T(8,128)(2,1)}, u32[]{:S(2)}, u32[]{:S(2)}) collective-permute-start(bf16[512,512]{1,0:T(8,128)(2,1)} %get-tuple-element.50), channel_id=1, source_target_pairs={{0,12},{4,8},{8,4},{12,0},{1,13},{5,9},{9,5},{13,1},{2,14},{6,10},... | collective-permute-start | bytes 1572872 | tf_op jit(solution)/shard_map/L_kv3/ppermute | solution.py:33
  53.2 29.6 %copy-start.4 = (bf16[512,512]{1,0:T(8,128)(2,1)}, bf16[512,512]{1,0:T(8,128)(2,1)S(1)}, u32[]{:S(2)}) copy-start(bf16[512,512]{1,0:T(8,128)(2,1)S(1)} %collective-permute-done.6.refs_2_) | copy-start | bytes 1572868
  53.2 11.1 %collective-permute-start.8 = (bf16[512,512]{1,0:T(8,128)(2,1)S(1)}, bf16[512,512]{1,0:T(8,128)(2,1)}, u32[]{:S(2)}, u32[]{:S(2)}) collective-permute-start(bf16[512,512]{1,0:T(8,128)(2,1)S(1)} %collective-permute-done.3.refs_3_), channel_id=1, source_target_pairs={{0,16},{16,0},{1,17},{17,1},{2,18},{18,2},{3,19},{19,3},{4,20},{20... | collective-permute-start | bytes 1572872 | tf_op jit(solution)/shard_map/L_ykv2/ppermute | solution.py:33
  64.6 33.2 %collective-permute-start.17 = (bf16[512,1024]{1,0:T(8,128)(2,1)}, bf16[512,1024]{1,0:T(8,128)(2,1)S(1)}, u32[]{:S(2)}, u32[]{:S(2)}) collective-permute-start(bf16[512,1024]{1,0:T(8,128)(2,1)} %collective-permute-done.4.refs_14_.refs_11_), channel_id=1, source_target_pairs={{0,1},{1,0},{2,3},{3,2},{4,5},{5,4},{6,7},{7,6},{8,9},{9,8},{10,11... | collective-permute-start | bytes 3145736 | tf_op jit(solution)/shard_map/L_B1c1/ppermute | solution.py:33
  64.6 18.2 %collective-permute-start.13 = (bf16[512,256]{1,0:T(8,128)(2,1)}, bf16[512,256]{1,0:T(8,128)(2,1)S(1)}, u32[]{:S(2)}, u32[]{:S(2)}) collective-permute-start(bf16[512,256]{1,0:T(8,128)(2,1)} %get-tuple-element.64), channel_id=1, source_target_pairs={{0,8},{4,12},{8,0},{12,4},{1,9},{5,13},{9,1},{13,5},{2,10},{6,14},... | collective-permute-start | bytes 786440 | tf_op jit(solution)/shard_map/L_q2/ppermute | solution.py:33
  69.7 14.6 %collective-permute-start.12 = (bf16[512,256]{1,0:T(8,128)(2,1)}, bf16[512,256]{1,0:T(8,128)(2,1)}, u32[]{:S(2)}, u32[]{:S(2)}) collective-permute-start(bf16[512,256]{1,0:T(8,128)(2,1)} %get-tuple-element.62), channel_id=1, source_target_pairs={{0,4},{4,0},{8,12},{12,8},{1,5},{5,1},{9,13},{13,9},{2,6},{6,2},{1... | collective-permute-start | bytes 786440 | tf_op jit(solution)/shard_map/L_q1/ppermute | solution.py:33
  69.7 19.5 %collective-permute-start.14 = (bf16[512,256]{1,0:T(8,128)(2,1)}, bf16[512,256]{1,0:T(8,128)(2,1)}, u32[]{:S(2)}, u32[]{:S(2)}) collective-permute-start(bf16[512,256]{1,0:T(8,128)(2,1)} %get-tuple-element.62), channel_id=1, source_target_pairs={{0,12},{4,8},{8,4},{12,0},{1,13},{5,9},{9,5},{13,1},{2,14},{6,10},... | collective-permute-start | bytes 786440 | tf_op jit(solution)/shard_map/L_q3/ppermute | solution.py:33
  71.3 18.0 %collective-permute-start.16 = (bf16[512,512]{1,0:T(8,128)(2,1)}, bf16[512,512]{1,0:T(8,128)(2,1)S(1)}, u32[]{:S(2)}, u32[]{:S(2)}) collective-permute-start(bf16[512,512]{1,0:T(8,128)(2,1)} %collective-permute-done.7.refs_4_), channel_id=1, source_target_pairs={{0,16},{16,0},{1,17},{17,1},{2,18},{18,2},{3,19},{19,3},{4,20},{20... | collective-permute-start | bytes 1572872 | tf_op jit(solution)/shard_map/L_ykv3/ppermute | solution.py:33
  82.7 23.9 %copy-start.8 = (bf16[512,256]{1,0:T(8,128)(2,1)}, bf16[512,256]{1,0:T(8,128)(2,1)S(1)}, u32[]{:S(2)}) copy-start(bf16[512,256]{1,0:T(8,128)(2,1)S(1)} %collective-permute-done.13.refs_4_) | copy-start | bytes 786436
  82.7 13.6 %collective-permute-start.15 = (bf16[512,512]{1,0:T(8,128)(2,1)S(1)}, bf16[512,512]{1,0:T(8,128)(2,1)S(1)}, u32[]{:S(2)}, u32[]{:S(2)}) collective-permute-start(bf16[512,512]{1,0:T(8,128)(2,1)S(1)} %collective-permute-done.6.refs_2_), channel_id=1, source_target_pairs={{0,16},{16,0},{1,17},{17,1},{2,18},{18,2},{3,19},{19,3},{4,20},{20... | collective-permute-start | bytes 1572872 | tf_op jit(solution)/shard_map/L_ykv1/ppermute | solution.py:33
  84.3 13.5 %collective-permute-start.10 = (bf16[256,1024]{1,0:T(8,128)(2,1)}, bf16[256,1024]{1,0:T(8,128)(2,1)}, u32[]{:S(2)}, u32[]{:S(2)}) collective-permute-start(bf16[256,1024]{1,0:T(8,128)(2,1)} %compress.1.refs_8_), channel_id=1, source_target_pairs={{0,2},{2,0},{1,3},{3,1},{4,6},{6,4},{5,7},{7,5},{8,10},{10,8},{9,1... | collective-permute-start | bytes 1572872 | tf_op jit(solution)/shard_map/L_Cx1/ppermute | solution.py:33
  89.2 8.5 %collective-permute-start.11 = (bf16[256,1024]{1,0:T(8,128)(2,1)}, bf16[256,1024]{1,0:T(8,128)(2,1)S(1)}, u32[]{:S(2)}, u32[]{:S(2)}) collective-permute-start(bf16[256,1024]{1,0:T(8,128)(2,1)} %compress.1.refs_8_), channel_id=1, source_target_pairs={{0,1},{1,0},{2,3},{3,2},{4,5},{5,4},{6,7},{7,6},{8,9},{9,8},{10,11... | collective-permute-start | bytes 1572872 | tf_op jit(solution)/shard_map/L_C0c1/ppermute | solution.py:33
  89.2 12.6 %copy-start.5 = (bf16[512,512]{1,0:T(8,128)(2,1)}, bf16[512,512]{1,0:T(8,128)(2,1)S(1)}, u32[]{:S(2)}) copy-start(bf16[512,512]{1,0:T(8,128)(2,1)S(1)} %collective-permute-done.16.refs_7_) | copy-start | bytes 1572868
  96.3 1.4 copy-start.6
  97.7 0.8 copy-start.7
  97.7 8.9 %copy-start.2 = (bf16[512,1024]{1,0:T(8,128)(2,1)}, bf16[512,1024]{1,0:T(8,128)(2,1)S(1)}, u32[]{:S(2)}) copy-start(bf16[512,1024]{1,0:T(8,128)(2,1)S(1)} %collective-permute-done.17.refs_15_.refs_12_) | copy-start | bytes 3145732
  97.8 4.0 %collective-permute-start.21 = (bf16[256,1024]{1,0:T(8,128)(2,1)}, bf16[256,1024]{1,0:T(8,128)(2,1)}, u32[]{:S(2)}, u32[]{:S(2)}) collective-permute-start(bf16[256,1024]{1,0:T(8,128)(2,1)} %collective-permute-done.10.refs_10_), channel_id=1, source_target_pairs={{0,1},{1,0},{2,3},{3,2},{4,5},{5,4},{6,7},{7,6},{8,9},{9,8},{10,11... | collective-permute-start | bytes 1572872 | tf_op jit(solution)/shard_map/L_C1c1/ppermute | solution.py:33
  99.2 19.5 %collective-permute-start.20 = (bf16[512,256]{1,0:T(8,128)(2,1)}, bf16[512,256]{1,0:T(8,128)(2,1)}, u32[]{:S(2)}, u32[]{:S(2)}) collective-permute-start(bf16[512,256]{1,0:T(8,128)(2,1)} %collective-permute-done.14.refs_5_), channel_id=1, source_target_pairs={{0,16},{16,0},{1,17},{17,1},{2,18},{18,2},{3,19},{19,3},{4,20},{20... | collective-permute-start | bytes 786440 | tf_op jit(solution)/shard_map/L_yq3/ppermute | solution.py:33
  99.7 18.9 %collective-permute-start.19 = (bf16[512,256]{1,0:T(8,128)(2,1)S(1)}, bf16[512,256]{1,0:T(8,128)(2,1)}, u32[]{:S(2)}, u32[]{:S(2)}) collective-permute-start(bf16[512,256]{1,0:T(8,128)(2,1)S(1)} %collective-permute-done.13.refs_4_), channel_id=1, source_target_pairs={{0,16},{16,0},{1,17},{17,1},{2,18},{18,2},{3,19},{19,3},{4,20},{20... | collective-permute-start | bytes 786440 | tf_op jit(solution)/shard_map/L_yq2/ppermute | solution.py:33
  101.3 17.5 %collective-permute-start.18 = (bf16[512,256]{1,0:T(8,128)(2,1)}, bf16[512,256]{1,0:T(8,128)(2,1)}, u32[]{:S(2)}, u32[]{:S(2)}) collective-permute-start(bf16[512,256]{1,0:T(8,128)(2,1)} %collective-permute-done.12.refs_3_), channel_id=1, source_target_pairs={{0,16},{16,0},{1,17},{17,1},{2,18},{18,2},{3,19},{19,3},{4,20},{20... | collective-permute-start | bytes 786440 | tf_op jit(solution)/shard_map/L_yq1/ppermute | solution.py:33
  106.6 14.3 %collective-permute-start.22 = (bf16[256,512]{1,0:T(8,128)(2,1)}, bf16[256,512]{1,0:T(8,128)(2,1)S(1)}, u32[]{:S(2)}, u32[]{:S(2)}) collective-permute-start(bf16[256,512]{1,0:T(8,128)(2,1)} %project_memory.1.refs_14_), channel_id=1, source_target_pairs={{0,8},{4,12},{8,0},{12,4},{1,9},{5,13},{9,1},{13,5},{2,10},{6,14},... | collective-permute-start | bytes 786440 | tf_op jit(solution)/shard_map/L_m2/ppermute | solution.py:33
  120.9 0.7 copy-start.9
  130.5 10.8 %collective-permute-start.23 = (bf16[512,256]{1,0:T(8,128)(2,1)}, bf16[512,256]{1,0:T(8,128)(2,1)S(1)}, u32[]{:S(2)}, u32[]{:S(2)}) collective-permute-start(bf16[512,256]{1,0:T(8,128)(2,1)} %attend.3), channel_id=1, source_target_pairs={{0,4},{4,0},{8,12},{12,8},{1,5},{5,1},{9,13},{13,9},{2,6},{6,2},{1... | collective-permute-start | bytes 786440 | tf_op jit(solution)/shard_map/L_ctx/ppermute | solution.py:33

commit v3 on v2

v3 whole, which is shorter than its diff:
```python
import functools
import math

import jax
import jax.numpy as jnp
from jax import lax
from jax.experimental import pallas as pl
from jax.experimental.pallas import tpu as pltpu
from jax.sharding import PartitionSpec as P

HD = 128
CG = 128
RATE = 4
SEG = 256
MEM = 64
BF = jnp.bfloat16


def cost(microseconds):
    return pl.CostEstimate(flops=int(microseconds * 1.0e9), bytes_accessed=1000, transcendentals=0)
F32 = jnp.float32
ANY = pl.BlockSpec(memory_space=pl.ANY)
MEMORY_LIMIT, TOKENS_LIMIT, VMEM_LIMIT = 58 << 20, 40 << 20, 40 << 20
SMEM = pl.BlockSpec(memory_space=pltpu.SMEM)
VMEM = pl.BlockSpec(memory_space=pltpu.VMEM)


EARLY = 2


def swap(value, axis, distance, label):
    size = lax.axis_size(axis)
    with jax.named_scope("L_" + label):
        return lax.ppermute(value, axis, [(i, i ^ distance) for i in range(size)])


def after(value, *others):
    return lax.optimization_barrier((value,) + others)[0]


def resident(value):
    return pltpu.with_memory_space_constraint(value, pltpu.VMEM)


def run_copies(copies):
    for copy in copies:
        copy.start()
    for copy in copies:
        copy.wait()


def aligned(index, size):
    return pl.ds(pl.multiple_of(index * size, size), size)


def split_kernel(wk, wv, wq, kv_same, kv_other, q_same, q_other, q_whole, sems):
    group, parity = lax.axis_index("groups"), lax.axis_index("seq") & 1
    half, width = q_same.shape
    rows = aligned(group, half)
    copies = []
    for target, kv, q in ((parity, kv_same, q_same), (1 - parity, kv_other, q_other)):
        columns = aligned(target, width)
        for source, dest in ((wk, kv.at[:, 0:width]), (wv, kv.at[:, width : 2 * width]), (wq, q)):
            copies.append(pltpu.make_async_copy(source.at[rows, columns], dest, sems.at[len(copies)]))
    source = wq.at[:, aligned(1 - parity, width)]
    copies.append(pltpu.make_async_copy(source, q_whole, sems.at[len(copies)]))
    run_copies(copies)


def split_weights(wk, wv, wq):
    depth, columns = wk.shape
    half, width = depth // 2, columns // 2
    shapes = [(half, 2 * width), (half, 2 * width), (half, width), (half, width), (depth, width)]
    return pl.pallas_call(
        split_kernel,
        out_shape=[jax.ShapeDtypeStruct(s, BF) for s in shapes],
        in_specs=[ANY] * 3,
        out_specs=[VMEM] * 5,
        scratch_shapes=[pltpu.SemaphoreType.DMA((7,))],
        cost_estimate=cost(2),
        name="split_weights",
    )(wk, wv, wq)


def compress_kernel(own_ref, partner_ref, w_ref, out_ref):
    rows, channels = own_ref.shape
    count = rows // RATE
    row = lax.broadcasted_iota(jnp.int32, (count, rows), 0)
    column = lax.broadcasted_iota(jnp.int32, (count, rows), 1)
    taps = []
    for t in range(RATE):
        pick = (column == row * RATE + t).astype(BF)
        pair = [jnp.dot(pick, ref[...], preferred_element_type=F32).astype(BF) for ref in (own_ref, partner_ref)]
        taps.append(jnp.concatenate(pair, axis=0))
    for g in range(channels // CG):
        columns = slice(g * CG, (g + 1) * CG)
        total = jnp.zeros((2 * count, CG), F32)
        for t in range(RATE):
            weight = w_ref[t * CG : (t + 1) * CG, columns]
            total += jnp.dot(taps[t][:, columns], weight, preferred_element_type=F32)
        out_ref[:, columns] = total.astype(BF)


def compress(own, partner, conv_weight):
    count, channels = own.shape
    return pl.pallas_call(
        compress_kernel,
        out_shape=jax.ShapeDtypeStruct((2 * count // RATE, channels), BF),
        in_specs=[VMEM, VMEM, VMEM],
        out_specs=VMEM,
        cost_estimate=cost(5),
        name="compress",
    )(own, partner, conv_weight)


def weight_copies(planes, buffer, sems, owns, nears, fars):
    plane, group = lax.axis_index("seq"), lax.axis_index("groups")
    depth = owns[0][0].shape[0]
    half = depth // 2
    pieces = [(ref.at[:, columns], aligned(plane, depth), place) for ref, columns, place in owns]
    fars = iter(fars)
    for distance, near in enumerate(nears, 1):
        if near.shape[0] == depth:
            pieces.append((near, aligned(plane ^ distance, depth), slice(None)))
        else:
            first = (plane ^ distance) * 2
            pieces.append((near, aligned(first + group, half), slice(None)))
            pieces.append((next(fars), aligned(first + 1 - group, half), slice(None)))
    copies = []
    for ref, rows, place in pieces:
        copies.append(pltpu.make_async_copy(ref, buffer.at[rows, place], sems.at[len(copies)]))
    return copies


def block_owner(index, tensor_size, sub_size):
    tensor, sub = lax.axis_index("tensor"), lax.axis_index("sub")
    return (tensor ^ (index // sub_size)) * sub_size + (sub ^ (index % sub_size))


def memory_kernel(planes, tensor_size, sub_size, *refs):
    blocks, others = tensor_size * sub_size, planes - 1
    wk, wv = refs[:2]
    nears, fars, refs = refs[2 : 2 + others], refs[2 + others : 2 + 2 * others], refs[2 + 2 * others :]
    pieces, (out, wbuf, xbuf, acc, xsem, wsem) = refs[:blocks], refs[blocks:]
    width = wbuf.shape[1] // 2
    columns = aligned(lax.axis_index("seq") & 1, width)
    owns = [(wk, columns, slice(0, width)), (wv, columns, slice(width, 2 * width))]
    wcopies = weight_copies(planes, wbuf, wsem, owns, nears, fars)
    xcopies = [pltpu.make_async_copy(pieces[j], xbuf.at[j], xsem.at[j]) for j in range(blocks)]
    run_copies(wcopies + xcopies)
    product_loop(tensor_size, sub_size, xbuf, pl.ds(0, out.shape[0]), wbuf, acc, out)


def product_loop(tensor_size, sub_size, xbuf, rows, wbuf, acc, out):
    blocks, chunk = xbuf.shape[0], xbuf.shape[2]
    for j in range(blocks):
        weight = aligned(block_owner(j, tensor_size, sub_size), chunk)
        part = jnp.dot(xbuf[j, rows, :], wbuf[weight, :], preferred_element_type=F32)
        if j:
            part += acc[...]
        if j < blocks - 1:
            acc[...] = part
        else:
            out[...] = part.astype(BF)


def project_memory(planes, tensor_size, sub_size, wk, wv, nears, fars, pieces):
    depth, columns = wk.shape
    blocks, (rows, chunk) = len(pieces), pieces[0].shape
    operands = [wk, wv, *nears, *fars, *pieces]
    return pl.pallas_call(
        functools.partial(memory_kernel, planes, tensor_size, sub_size),
        out_shape=[jax.ShapeDtypeStruct((rows, columns), BF), pltpu.VMEM((depth * planes, columns), BF)],
        in_specs=[ANY] * len(operands),
        out_specs=[VMEM, VMEM],
        scratch_shapes=[
            pltpu.VMEM((blocks, rows, chunk), BF),
            pltpu.VMEM((rows, columns), F32),
            pltpu.SemaphoreType.DMA((blocks,)),
            pltpu.SemaphoreType.DMA((2 + 2 * (planes - 1),)),
        ],
        compiler_params=pltpu.CompilerParams(vmem_limit_bytes=MEMORY_LIMIT),
        cost_estimate=cost(4),
        name="project_memory",
    )(*operands)


def tokens_kernel(tensor_size, sub_size, *refs):
    blocks = tensor_size * sub_size
    pieces, (wbuf, out, xbuf, acc, sems) = refs[: 2 * blocks], refs[2 * blocks :]
    rows, chunk = pieces[0].shape
    copies = []
    for j in range(blocks):
        for side in range(2):
            dest = xbuf.at[j, pl.ds(side * rows, rows), :]
            copies.append(pltpu.make_async_copy(pieces[side * blocks + j], dest, sems.at[len(copies)]))
    for copy in copies:
        copy.start()
    for j in range(blocks):
        weight = aligned(block_owner(j, tensor_size, sub_size), chunk)
        for side in range(2):
            copies[2 * j + side].wait()
            here = slice(side * rows, (side + 1) * rows)
            part = jnp.dot(xbuf[j, here, :], wbuf[weight, :], preferred_element_type=F32)
            if j:
                part += acc[here, :]
            if j < blocks - 1:
                acc[here, :] = part
            else:
                out[here, :] = part.astype(BF)


def project_tokens(tensor_size, sub_size, own, partner, weights):
    blocks, (rows, chunk), columns = len(own), own[0].shape, weights.shape[1]
    return pl.pallas_call(
        functools.partial(tokens_kernel, tensor_size, sub_size),
        out_shape=[pltpu.VMEM((2 * rows, columns), BF), pltpu.VMEM((blocks, 2 * rows, chunk), BF)],
        in_specs=[ANY] * (2 * blocks) + [VMEM],
        out_specs=[VMEM, VMEM],
        scratch_shapes=[pltpu.VMEM((2 * rows, columns), F32), pltpu.SemaphoreType.DMA((2 * blocks,))],
        compiler_params=pltpu.CompilerParams(vmem_limit_bytes=TOKENS_LIMIT),
        cost_estimate=cost(6),
        name="project_tokens",
    )(*own, *partner, resident(weights))


def attend_kernel(side, planes, tensor_size, sub_size, halves, *refs):
    segments, length, wq = refs[:3]
    refs = refs[3:]
    nears, fars, refs = refs[: planes - 1], refs[planes - 1 : planes - 1 + halves], refs[planes - 1 + halves :]
    xbuf, kvbuf, refs = refs[0], refs[1], refs[2:]
    mems, refs = refs[: planes // 2], refs[planes // 2 :]
    out, wbuf, acc, qbuf, membuf, obuf, wsem, ksem = refs
    plane = lax.axis_index("seq")
    rows_here, width = qbuf.shape
    slots = rows_here // SEG
    owns = [(wq, aligned(plane & 1, width), slice(0, width))]
    wcopies = weight_copies(planes, wbuf, wsem, owns, nears, fars)
    count = mems[0].shape[0]
    kcopies = []
    for i, mem in enumerate(mems):
        kcopies.append(pltpu.make_async_copy(mem, membuf.at[pl.ds(i * count, count), :], ksem.at[1 + i]))
    for copy in wcopies + kcopies:
        copy.start()
    per_plane = count // 2
    mem_total = membuf.shape[0]
    column = lax.broadcasted_iota(jnp.int32, (1, mem_total), 1)
    owner = jnp.zeros((1, mem_total), jnp.int32)
    for distance in range(planes):
        for i in range(slots):
            start = distance * per_plane + i * MEM
            inside = (column >= start) & (column < start + MEM)
            owner = jnp.where(inside, segments[(plane ^ distance) * slots + i], owner)
    row = lax.broadcasted_iota(jnp.int32, (SEG, SEG), 0)
    causal = row >= lax.broadcasted_iota(jnp.int32, (SEG, SEG), 1)
    position = lax.broadcasted_iota(jnp.int32, (SEG, HD), 0)
    contract = (((1,), (1,)), ((), ()))
    scale = HD ** (-0.5) * math.log2(math.e)
    for copy in wcopies:
        copy.wait()
    product_loop(tensor_size, sub_size, xbuf, pl.ds(side * rows_here, rows_here), wbuf, acc, qbuf)
    for copy in kcopies:
        copy.wait()
    for a in range(slots):
        rows = slice(a * SEG, (a + 1) * SEG)
        kvrows = slice(side * rows_here + a * SEG, side * rows_here + (a + 1) * SEG)
        segment = segments[(plane ^ side) * slots + a]
        allowed = owner < segment
        valid = position + segment * SEG < length[0]
        for h in range(width // HD):
            ks, vs = slice(h * HD, (h + 1) * HD), slice(width + h * HD, width + (h + 1) * HD)
            query = qbuf[rows, ks]
            near = lax.dot_general(query, kvbuf[kvrows, ks], contract, preferred_element_type=F32)
            far = lax.dot_general(query, membuf[:, ks], contract, preferred_element_type=F32)
            near = jnp.where(causal, near * scale, -jnp.inf)
            far = jnp.where(allowed, far * scale, -jnp.inf)
            best = jnp.maximum(
                jnp.max(near, axis=1, keepdims=True), jnp.max(far, axis=1, keepdims=True)
            )
            near, far = jnp.exp2(near - best), jnp.exp2(far - best)
            denominator = jnp.sum(near, axis=1, keepdims=True) + jnp.sum(far, axis=1, keepdims=True)
            numerator = jnp.dot(near.astype(BF), kvbuf[kvrows, vs], preferred_element_type=F32)
            numerator += jnp.dot(far.astype(BF), membuf[:, vs], preferred_element_type=F32)
            obuf[rows, ks] = jnp.where(valid, numerator / denominator, 0.0).astype(BF)
    dest = out if side else out.at[:, aligned(plane & 1, width)]
    copy = pltpu.make_async_copy(obuf, dest, ksem.at[0])
    copy.start()
    copy.wait()


def attend(side, planes, tensor_size, sub_size, segments, length, wq, nears, fars, held, kv_tok, mems):
    depth, columns = wq.shape
    rows, width = held.shape[1] // 2, columns // 2
    mem_total = len(mems) * mems[0].shape[0]
    operands = [segments, length, wq, *nears, *fars, resident(held), resident(kv_tok), *mems]
    return pl.pallas_call(
        functools.partial(attend_kernel, side, planes, tensor_size, sub_size, len(fars)),
        out_shape=jax.ShapeDtypeStruct((rows, width if side else 2 * width), BF),
        in_specs=[SMEM, SMEM] + [ANY] * (len(operands) - 4 - len(mems)) + [VMEM] * 2 + [ANY] * len(mems),
        out_specs=ANY,
        scratch_shapes=[
            pltpu.VMEM((depth * planes, width), BF),
            pltpu.VMEM((rows, width), F32),
            pltpu.VMEM((rows, width), BF),
            pltpu.VMEM((mem_total, 2 * width), BF),
            pltpu.VMEM((rows, width), BF),
            pltpu.SemaphoreType.DMA((1 + len(nears) + len(fars),)),
            pltpu.SemaphoreType.DMA((1 + len(mems),)),
        ],
        compiler_params=pltpu.CompilerParams(vmem_limit_bytes=VMEM_LIMIT),
        cost_estimate=cost(6),
        name="attend",
    )(*operands)


def on_device(
    activations, conv_weight, query_weight, key_weight, value_weight, segment_for_slot, book_length
):
    planes, tensor_size, sub_size = (lax.axis_size(name) for name in ("seq", "tensor", "sub"))
    parity = lax.axis_index("seq") & 1

    kv_same, kv_other, q_same, q_other, q_whole = split_weights(key_weight, value_weight, query_weight)

    def across(block, label):
        return {f"{label}x{k}": (block, "tensor", k) for k in range(1, tensor_size)}

    def within(block, label):
        return {f"{label}c{k}": (block, "sub", k) for k in range(1, sub_size)}

    def distant(distances, name):
        same, other = {"kv": (kv_same, kv_other), "q": (q_same, q_other)}[name]
        return {f"{name}{d}": (other if d & 1 else same, "seq", d) for d in distances}

    def relayed(distances, name):
        return {f"y{name}{d}": (got[f"{name}{d}"], "groups", 1) for d in distances}

    got = {}

    def stage(sends, *computed):
        held = tuple(got[key] for key in fresh)
        new = {}
        for key, (value, axis, distance) in sends.items():
            new[key] = swap(after(value, *held), axis, distance, key)
        ended = lax.optimization_barrier(tuple(new.values()) + computed)
        got.update(zip(new, ended))
        fresh[:] = list(new)
        return ended[len(new) :]

    fresh = []
    every = range(1, planes)
    first = [2] if planes > 2 else []
    second = [d for d in every if d not in first]
    stage(
        {"Xz": (activations, "seq", 1)}
        | across(activations, "A")
        | within(activations, "A0")
        | distant(first, "kv")
    )
    partner = got["Xz"]
    sends = across(partner, "B") | within(partner, "B0") | distant(second, "kv") | relayed(first, "kv")
    for k in range(1, tensor_size):
        sends |= within(got[f"Ax{k}"], f"A{k}")
    (both,) = stage(sends, compress(activations, partner, conv_weight))
    far_planes = range(2, planes)
    stage(distant(far_planes, "q") | relayed(second, "kv") | across(both, "C"))
    sends = within(both, "C0") | {"q1": (q_whole, "seq", 1)} | relayed(far_planes, "q")
    for label in ("C", "B"):
        for k in range(1, tensor_size):
            sends |= within(got[f"{label}x{k}"], f"{label}{k}")
    before = tuple(got[key] for key in fresh)
    for key, (value, axis, distance) in sends.items():
        got[key] = swap(after(value, *before), axis, distance, key)

    def pieces(block, label):
        whole = []
        for k in range(tensor_size):
            whole.append(got[f"{label}x{k}"] if k else block)
            whole += [got[f"{label}{k}c{u}"] for u in range(1, sub_size)]
        return whole

    own_pieces, partner_pieces = pieces(activations, "A"), pieces(partner, "B")
    compressed_pieces = pieces(both, "C")
    sizes = (planes, tensor_size, sub_size)
    kv_parts = ([got[f"kv{d}"] for d in every], [got[f"ykv{d}"] for d in every])
    kv_mem, kv_held = project_memory(*sizes, key_weight, value_weight, *kv_parts, compressed_pieces)
    mems = [kv_mem] + [swap(kv_mem, "seq", d, f"m{d}") for d in range(2, planes, 2)]
    kv_tok, held = project_tokens(tensor_size, sub_size, own_pieces, partner_pieces, kv_held)
    q_parts = ([got[f"q{d}"] for d in every], [got[f"yq{d}"] for d in far_planes])
    shared = (book_length, query_weight, *q_parts, held, kv_tok, mems)
    theirs = attend(1, *sizes, segment_for_slot, *shared)
    returned = swap(theirs, "seq", 1, "ctx")
    mine = attend(0, *sizes, after(segment_for_slot, theirs), *shared)
    return lax.dynamic_update_slice(mine, returned, (0, (1 - parity) * theirs.shape[1]))


def solution(mesh):
    placed = (
        P(("groups", "seq"), ("tensor", "sub")),
        P(None, ("tensor", "sub")),
        P("seq", ("tensor", "sub")),
        P("seq", ("tensor", "sub")),
        P("seq", ("tensor", "sub")),
        P("groups"),
        P("groups"),
    )
    return jax.shard_map(
        on_device,
        mesh=mesh,
        in_specs=placed,
        out_specs=P(("groups", "seq"), ("tensor", "sub")),
        check_vma=False,
    )
```

time: 142 us -> 132 us (0.930)
  Pallas kernels: 39.9 us -> 30.2 us
  starting transfers between devices: 29.5 us -> 32.3 us
  other arithmetic: 1.86 us -> 0 us
    pallas_call x2, Pallas kernels: 17.7 us -> 11.6 us  [attend(): pl.pallas_call(functools.partial(attend_kernel, side, planes, tensor_size...]
    pallas_call x2, Pallas kernels: 15.2 us -> 11.2 us  [the longest x1 6.38 us: project_tokens(): pl.pallas_call(functools.partial(tokens_kernel, tensor_size, sub_size), o...]
    ppermute x24 -> x23, starting transfers between devices: 29.5 us -> 32.3 us  [swap(): return lax.ppermute(value, axis, [(i, i ^ distance) for i in range(size)])]
    concatenate x1 -> x0, other arithmetic: 1.86 us -> none  [on_device(): result = jnp.concatenate([mine, mine], axis=1)]
    ppermute x24 -> x23, waiting for transfers between devices: 67.9 us -> 67.3 us  [swap(): return lax.ppermute(value, axis, [(i, i ^ distance) for i in range(size)])]
  transfers between devices with their start and end apart: 24 -> 23, of which waited for: 11 -> 8; matrix products, arithmetic and copies ran while one was open for 1% -> 0% of each run, Pallas kernels for 22% -> 19%
where the time goes in v3:
time: 132 us
  waiting for transfers between devices  67.3 us (51%)
  starting transfers between devices  32.3 us (24%)
  Pallas kernels  30.2 us (23%)
    ppermute x23, waiting for transfers between devices, swap(): return lax.ppermute(value, axis, [(i, i ^ distance) for i in range(size)])  67.3 us
    ppermute x23, starting transfers between devices, swap(): return lax.ppermute(value, axis, [(i, i ^ distance) for i in range(size)])  32.3 us
    pallas_call x2, Pallas kernels, attend(): pl.pallas_call(functools.partial(attend_kernel, side, planes, tensor_size...  11.6 us
    pallas_call x1, Pallas kernels, project_tokens(): pl.pallas_call(functools.partial(tokens_kernel, tensor_size, sub_size), o...  6.38 us
    pallas_call x1, Pallas kernels, project_memory(): pl.pallas_call(functools.partial(memory_kernel, planes, tensor_size, sub_...  4.84 us
    pallas_call x1, Pallas kernels, compress(): pl.pallas_call(compress_kernel, out_shape=jax.ShapeDtypeStruct((2 * count...  4.47 us
    pallas_call x1, Pallas kernels, split_weights(): pl.pallas_call(split_kernel, out_shape=[jax.ShapeDtypeStruct(s, BF) for s...  2.93 us
  transfers between devices with their start and end apart: 23, of which 8 were waited for; matrix products, arithmetic and copies ran while one was open for 0% of the time, Pallas kernels for 19%

profile of v3, /device:TPU:0, one launch (start us, length us, event | category | flops | bytes accessed | tf_op | source)
XLA Modules:
  0.0 131.6 jit_solution(10105282210847112701)
XLA Ops:
  0.0 3.0 %collective-permute-start = (bf16[512,1024]{1,0:T(8,128)(2,1)}, bf16[512,1024]{1,0:T(8,128)(2,1)S(1)}, u32[]{:S(2)}, u32[]{:S(2)}) collective-permute-start(bf16[512,1024]{1,0:T(8,128)(2,1)} %refs_0_.4), channel_id=1, source_target_pairs={{0,4},{4,0},{8,12},{12,8},{1,5},{5,1},{9,13},{13,9},{2,6},{6,2},{1... | collective-permute-start | bytes 3145736 | tf_op jit(solution)/shard_map/L_Xz/ppermute | solution.py:34
  3.0 1.5 %collective-permute-start.1 = (bf16[512,1024]{1,0:T(8,128)(2,1)}, bf16[512,1024]{1,0:T(8,128)(2,1)S(1)}, u32[]{:S(2)}, u32[]{:S(2)}) collective-permute-start(bf16[512,1024]{1,0:T(8,128)(2,1)} %refs_0_.4), channel_id=1, source_target_pairs={{0,2},{2,0},{1,3},{3,1},{4,6},{6,4},{5,7},{7,5},{8,10},{10,8},{9,1... | collective-permute-start | bytes 3145736 | tf_op jit(solution)/shard_map/L_Ax1/ppermute | solution.py:34
  4.5 0.0 collective-permute-start.2
  4.5 2.9 %split_weights.1 = (bf16[512,512]{1,0:T(8,128)(2,1)}, bf16[512,512]{1,0:T(8,128)(2,1)}, bf16[512,256]{1,0:T(8,128)(2,1)}, bf16[512,256]{1,0:T(8,128)(2,1)}, bf16[1024,256]{1,0:T(8,128)(2,1)}) custom-call(bf16[1024,512]{1,0:T(8,128)(2,1)} %refs_0_.3, bf16[1024,512]{1,0:T(8,128)(2,1)} %refs_1_.3, bf16[1024,512]{1,0:T(8,128)(2,1)} %refs_2_.3), custom_call_target="tpu_custom_call" | custom-call | flops 2000000000 | bytes 1000 | tf_op jit(solution)/shard_map/split_weights/pallas_call | solution.py:74
  7.5 2.7 %collective-permute-start.3 = (bf16[512,512]{1,0:T(8,128)(2,1)}, bf16[512,512]{1,0:T(8,128)(2,1)}, u32[]{:S(2)}, u32[]{:S(2)}) collective-permute-start(bf16[512,512]{1,0:T(8,128)(2,1)} %get-tuple-element.48), channel_id=1, source_target_pairs={{0,8},{4,12},{8,0},{12,4},{1,9},{5,13},{9,1},{13,5},{2,10},{6,14},... | collective-permute-start | bytes 1572872 | tf_op jit(solution)/shard_map/L_kv2/ppermute | solution.py:34
  10.1 26.9 %collective-permute-done.3.refs_3_ = bf16[512,512]{1,0:T(8,128)(2,1)} collective-permute-done((bf16[512,512]{1,0:T(8,128)(2,1)}, bf16[512,512]{1,0:T(8,128)(2,1)}, u32[]{:S(2)}, u32[]{:S(2)}) %collective-permute-start.3) | collective-permute-done | bytes 524320 | tf_op jit(solution)/shard_map/L_kv2/ppermute | solution.py:34
  37.0 0.6 collective-permute-done.partner_ref.refs_4_
  37.6 0.0 collective-permute-done.1.refs_2_
  37.6 0.0 collective-permute-done.2.refs_1_
  37.6 0.0 copy-start.5
  37.6 1.7 %collective-permute-start.4 = (bf16[512,1024]{1,0:T(8,128)(2,1)S(1)}, bf16[512,1024]{1,0:T(8,128)(2,1)}, u32[]{:S(2)}, u32[]{:S(2)}) collective-permute-start(bf16[512,1024]{1,0:T(8,128)(2,1)S(1)} %collective-permute-done.partner_ref.refs_4_), channel_id=1, source_target_pairs={{0,2},{2,0},{1,3},{3,1},{4,6},{6,4},{5,7},{7,5},{8,10},{10,8},{9,1... | collective-permute-start | bytes 3145736 | tf_op jit(solution)/shard_map/L_Bx1/ppermute | solution.py:34
  39.4 2.7 %collective-permute-start.6 = (bf16[512,512]{1,0:T(8,128)(2,1)}, bf16[512,512]{1,0:T(8,128)(2,1)}, u32[]{:S(2)}, u32[]{:S(2)}) collective-permute-start(bf16[512,512]{1,0:T(8,128)(2,1)} %get-tuple-element.55), channel_id=1, source_target_pairs={{0,4},{4,0},{8,12},{12,8},{1,5},{5,1},{9,13},{13,9},{2,6},{6,2},{1... | collective-permute-start | bytes 1572872 | tf_op jit(solution)/shard_map/L_kv1/ppermute | solution.py:34
  42.1 0.0 collective-permute-start.5
  42.1 0.5 collective-permute-start.9
  42.6 1.3 %collective-permute-start.7 = (bf16[512,512]{1,0:T(8,128)(2,1)}, bf16[512,512]{1,0:T(8,128)(2,1)}, u32[]{:S(2)}, u32[]{:S(2)}) collective-permute-start(bf16[512,512]{1,0:T(8,128)(2,1)} %get-tuple-element.55), channel_id=1, source_target_pairs={{0,12},{4,8},{8,4},{12,0},{1,13},{5,9},{9,5},{13,1},{2,14},{6,10},... | collective-permute-start | bytes 1572872 | tf_op jit(solution)/shard_map/L_kv3/ppermute | solution.py:34
  43.9 10.8 %collective-permute-done.6.refs_2_ = bf16[512,512]{1,0:T(8,128)(2,1)} collective-permute-done((bf16[512,512]{1,0:T(8,128)(2,1)}, bf16[512,512]{1,0:T(8,128)(2,1)}, u32[]{:S(2)}, u32[]{:S(2)}) %collective-permute-start.6) | collective-permute-done | bytes 524320 | tf_op jit(solution)/shard_map/L_kv1/ppermute | solution.py:34
  54.8 1.5 %collective-permute-start.8 = (bf16[512,512]{1,0:T(8,128)(2,1)}, bf16[512,512]{1,0:T(8,128)(2,1)}, u32[]{:S(2)}, u32[]{:S(2)}) collective-permute-start(bf16[512,512]{1,0:T(8,128)(2,1)} %collective-permute-done.3.refs_3_), channel_id=1, source_target_pairs={{0,16},{16,0},{1,17},{17,1},{2,18},{18,2},{3,19},{19,3},{4,20},{20... | collective-permute-start | bytes 1572872 | tf_op jit(solution)/shard_map/L_ykv2/ppermute | solution.py:34
  56.3 0.0 copy-done.3
  56.3 4.5 %compress.1.refs_8_ = bf16[256,1024]{1,0:T(8,128)(2,1)} custom-call(bf16[512,1024]{1,0:T(8,128)(2,1)} %refs_0_.4, bf16[512,1024]{1,0:T(8,128)(2,1)} %copy-done.3, bf16[512,1024]{1,0:T(8,128)(2,1)} %w_ref.1), custom_call_target="tpu_custom_call" | custom-call | flops 5000000000 | bytes 1000 | tf_op jit(solution)/shard_map/compress/pallas_call | solution.py:106
  60.8 0.0 copy-done.4
  60.8 0.0 copy-done.5
  60.8 4.8 %collective-permute-done.7.refs_4_ = bf16[512,512]{1,0:T(8,128)(2,1)} collective-permute-done((bf16[512,512]{1,0:T(8,128)(2,1)}, bf16[512,512]{1,0:T(8,128)(2,1)}, u32[]{:S(2)}, u32[]{:S(2)}) %collective-permute-start.7) | collective-permute-done | bytes 524320 | tf_op jit(solution)/shard_map/L_kv3/ppermute | solution.py:34
  65.6 0.0 collective-permute-done.8.refs_6_
  65.6 0.0 collective-permute-done.4.refs_6_
  65.6 0.0 collective-permute-done.5.refs_5_
  65.6 0.0 collective-permute-done.9.refs_3_
  65.6 1.6 %collective-permute-start.12 = (bf16[512,512]{1,0:T(8,128)(2,1)}, bf16[512,512]{1,0:T(8,128)(2,1)}, u32[]{:S(2)}, u32[]{:S(2)}) collective-permute-start(bf16[512,512]{1,0:T(8,128)(2,1)} %collective-permute-done.6.refs_2_), channel_id=1, source_target_pairs={{0,16},{16,0},{1,17},{17,1},{2,18},{18,2},{3,19},{19,3},{4,20},{20... | collective-permute-start | bytes 1572872 | tf_op jit(solution)/shard_map/L_ykv1/ppermute | solution.py:34
  67.2 0.5 collective-permute-start.13
  67.7 0.5 collective-permute-start.14
  68.2 3.9 %collective-permute-start.10 = (bf16[512,256]{1,0:T(8,128)(2,1)}, bf16[512,256]{1,0:T(8,128)(2,1)S(1)}, u32[]{:S(2)}, u32[]{:S(2)}) collective-permute-start(bf16[512,256]{1,0:T(8,128)(2,1)} %get-tuple-element.64), channel_id=1, source_target_pairs={{0,8},{4,12},{8,0},{12,4},{1,9},{5,13},{9,1},{13,5},{2,10},{6,14},... | collective-permute-start | bytes 786440 | tf_op jit(solution)/shard_map/L_q2/ppermute | solution.py:34
  72.1 0.0 copy-done.8
  72.1 1.2 collective-permute-start.11
  73.3 16.4 %collective-permute-done.10.refs_4_ = bf16[512,256]{1,0:T(8,128)(2,1)S(1)} collective-permute-done((bf16[512,256]{1,0:T(8,128)(2,1)}, bf16[512,256]{1,0:T(8,128)(2,1)S(1)}, u32[]{:S(2)}, u32[]{:S(2)}) %collective-permute-start.10) | collective-permute-done | bytes 262176 | tf_op jit(solution)/shard_map/L_q2/ppermute | solution.py:34
  89.7 0.0 collective-permute-done.11.refs_5_
  89.7 0.0 collective-permute-done.12.refs_5_
  89.7 0.0 collective-permute-done.13.refs_7_
  89.7 0.0 collective-permute-done.14.refs_10_
  89.7 0.0 copy-start.6
  89.7 0.1 collective-permute-start.18
  89.8 0.5 collective-permute-start.19
  90.3 0.1 collective-permute-start.20
  91.0 4.9 %collective-permute-start.15 = (bf16[1024,256]{1,0:T(8,128)(2,1)}, bf16[1024,256]{1,0:T(8,128)(2,1)S(1)}, u32[]{:S(2)}, u32[]{:S(2)}) collective-permute-start(bf16[1024,256]{1,0:T(8,128)(2,1)} %get-tuple-element.76), channel_id=1, source_target_pairs={{0,4},{4,0},{8,12},{12,8},{1,5},{5,1},{9,13},{13,9},{2,6},{6,2},{1... | collective-permute-start | bytes 1572872 | tf_op jit(solution)/shard_map/L_q1/ppermute | solution.py:34
  95.9 1.5 %collective-permute-start.16 = (bf16[512,256]{1,0:T(8,128)(2,1)S(1)}, bf16[512,256]{1,0:T(8,128)(2,1)S(1)}, u32[]{:S(2)}, u32[]{:S(2)}) collective-permute-start(bf16[512,256]{1,0:T(8,128)(2,1)S(1)} %collective-permute-done.10.refs_4_), channel_id=1, source_target_pairs={{0,16},{16,0},{1,17},{17,1},{2,18},{18,2},{3,19},{19,3},{4,20},{20... | collective-permute-start | bytes 786440 | tf_op jit(solution)/shard_map/L_yq2/ppermute | solution.py:34
  97.4 0.0 collective-permute-done.19.refs_9_
  97.4 0.5 collective-permute-start.17
  97.9 0.0 copy-done.6
  97.9 0.3 copy-done.7
  98.2 0.0 collective-permute-done.20.refs_11_
  98.2 4.8 %project_memory.1 = (bf16[256,512]{1,0:T(8,128)(2,1)}, bf16[4096,512]{1,0:T(8,128)(2,1)S(1)}) custom-call(bf16[1024,512]{1,0:T(8,128)(2,1)} %refs_0_.3, bf16[1024,512]{1,0:T(8,128)(2,1)} %refs_1_.3, bf16[512,512]{1,0:T(8,128)(2,1)} %collective-permute-done.6.refs_2_, bf16[512,512]{1,0:T(8,128)(2,1)} %collective-permute-done.3.refs_3_, ...), custom_call_target="tpu_custom_call" | custom-call | flops 4000000000 | bytes 1000 | tf_op jit(solution)/shard_map/project_memory/pallas_call | solution.py:171
  103.1 2.0 %collective-permute-start.21 = (bf16[256,512]{1,0:T(8,128)(2,1)}, bf16[256,512]{1,0:T(8,128)(2,1)S(1)}, u32[]{:S(2)}, u32[]{:S(2)}) collective-permute-start(bf16[256,512]{1,0:T(8,128)(2,1)} %get-tuple-element.85.refs_10_), channel_id=1, source_target_pairs={{0,8},{4,12},{8,0},{12,4},{1,9},{5,13},{9,1},{13,5},{2,10},{6,14},... | collective-permute-start | bytes 786440 | tf_op jit(solution)/shard_map/L_m2/ppermute | solution.py:34
  105.1 0.0 collective-permute-done.18.refs_7_
  105.1 6.4 %project_tokens.1 = (bf16[1024,512]{1,0:T(8,128)(2,1)S(1)}, bf16[4,1024,1024]{2,1,0:T(8,128)(2,1)S(1)}) custom-call(bf16[512,1024]{1,0:T(8,128)(2,1)} %refs_0_.4, bf16[512,1024]{1,0:T(8,128)(2,1)} %copy-done.5, bf16[512,1024]{1,0:T(8,128)(2,1)} %copy-done.4, bf16[512,1024]{1,0:T(8,128)(2,1)} %collective-permute-done.9.refs_3_, bf16[512,1024]{1,0:T(8,128)(2,1)} %copy-done.3, ...), custom_call_target="tpu_custom_call" | custom-call | flops 6000000000 | bytes 1000 | tf_op jit(solution)/shard_map/project_tokens/pallas_call | solution.py:215
  111.5 0.0 collective-permute-done.16.refs_6_
  111.5 0.0 collective-permute-done.17.refs_7_
  111.5 0.3 collective-permute-done.15.refs_3_
  111.8 6.2 %collective-permute-done.21.refs_11_ = bf16[256,512]{1,0:T(8,128)(2,1)S(1)} collective-permute-done((bf16[256,512]{1,0:T(8,128)(2,1)}, bf16[256,512]{1,0:T(8,128)(2,1)S(1)}, u32[]{:S(2)}, u32[]{:S(2)}) %collective-permute-start.21) | collective-permute-done | bytes 262176 | tf_op jit(solution)/shard_map/L_m2/ppermute | solution.py:34
  118.0 0.0 copy-done
  118.0 0.0 copy-done.1
  118.0 0.0 copy-done.2
  118.0 5.5 %attend.2 = bf16[512,256]{1,0:T(8,128)(2,1)S(1)} custom-call(s32[8]{0:T(128)S(1)} %copy-done.2, s32[1]{0:T(128)S(6)} %copy.9.refs_1_, bf16[1024,512]{1,0:T(8,128)(2,1)S(1)} %copy-done, bf16[1024,256]{1,0:T(8,128)(2,1)S(1)} %collective-permute-done.15.refs_3_, bf16[512,256]{1,0:T(8,128)(2,1)S(1)} %collective-permute-done.10.refs_4_, ...), custom_call_target="tpu_custom_call" | custom-call | flops 6000000000 | bytes 1000 | tf_op jit(solution)/shard_map/attend/pallas_call | solution.py:296
  123.5 0.1 collective-permute-start.22
  123.6 6.0 %attend.3 = bf16[512,512]{1,0:T(8,128)(2,1)} custom-call(s32[8]{0:T(128)S(1)} %copy-done.2, s32[1]{0:T(128)S(6)} %copy.9.refs_1_, bf16[1024,512]{1,0:T(8,128)(2,1)S(1)} %copy-done, bf16[1024,256]{1,0:T(8,128)(2,1)S(1)} %collective-permute-done.15.refs_3_, bf16[512,256]{1,0:T(8,128)(2,1)S(1)} %collective-permute-done.10.refs_4_, ...), custom_call_target="tpu_custom_call" | custom-call | flops 6000000000 | bytes 1000 | tf_op jit(solution)/shard_map/attend/pallas_call | solution.py:296
  129.7 1.2 collective-permute-done.22
  130.9 0.7 constant_dynamic-update-slice_fusion
  (7 shorter events, 0.0 us)
Async XLA Ops:
  0.0 37.6 %collective-permute-start = (bf16[512,1024]{1,0:T(8,128)(2,1)}, bf16[512,1024]{1,0:T(8,128)(2,1)S(1)}, u32[]{:S(2)}, u32[]{:S(2)}) collective-permute-start(bf16[512,1024]{1,0:T(8,128)(2,1)} %refs_0_.4), channel_id=1, source_target_pairs={{0,4},{4,0},{8,12},{12,8},{1,5},{5,1},{9,13},{13,9},{2,6},{6,2},{1... | collective-permute-start | bytes 3145736 | tf_op jit(solution)/shard_map/L_Xz/ppermute | solution.py:34
  3.0 34.6 %collective-permute-start.1 = (bf16[512,1024]{1,0:T(8,128)(2,1)}, bf16[512,1024]{1,0:T(8,128)(2,1)S(1)}, u32[]{:S(2)}, u32[]{:S(2)}) collective-permute-start(bf16[512,1024]{1,0:T(8,128)(2,1)} %refs_0_.4), channel_id=1, source_target_pairs={{0,2},{2,0},{1,3},{3,1},{4,6},{6,4},{5,7},{7,5},{8,10},{10,8},{9,1... | collective-permute-start | bytes 3145736 | tf_op jit(solution)/shard_map/L_Ax1/ppermute | solution.py:34
  4.5 33.1 %collective-permute-start.2 = (bf16[512,1024]{1,0:T(8,128)(2,1)}, bf16[512,1024]{1,0:T(8,128)(2,1)S(1)}, u32[]{:S(2)}, u32[]{:S(2)}) collective-permute-start(bf16[512,1024]{1,0:T(8,128)(2,1)} %refs_0_.4), channel_id=1, source_target_pairs={{0,1},{1,0},{2,3},{3,2},{4,5},{5,4},{6,7},{7,6},{8,9},{9,8},{10,11... | collective-permute-start | bytes 3145736 | tf_op jit(solution)/shard_map/L_A0c1/ppermute | solution.py:34
  7.5 29.5 %collective-permute-start.3 = (bf16[512,512]{1,0:T(8,128)(2,1)}, bf16[512,512]{1,0:T(8,128)(2,1)}, u32[]{:S(2)}, u32[]{:S(2)}) collective-permute-start(bf16[512,512]{1,0:T(8,128)(2,1)} %get-tuple-element.48), channel_id=1, source_target_pairs={{0,8},{4,12},{8,0},{12,4},{1,9},{5,13},{9,1},{13,5},{2,10},{6,14},... | collective-permute-start | bytes 1572872 | tf_op jit(solution)/shard_map/L_kv2/ppermute | solution.py:34
  37.6 18.7 %copy-start.3 = (bf16[512,1024]{1,0:T(8,128)(2,1)}, bf16[512,1024]{1,0:T(8,128)(2,1)S(1)}, u32[]{:S(2)}) copy-start(bf16[512,1024]{1,0:T(8,128)(2,1)S(1)} %collective-permute-done.partner_ref.refs_4_) | copy-start | bytes 3145732
  37.6 23.1 %copy-start.4 = (bf16[512,1024]{1,0:T(8,128)(2,1)}, bf16[512,1024]{1,0:T(8,128)(2,1)S(1)}, u32[]{:S(2)}) copy-start(bf16[512,1024]{1,0:T(8,128)(2,1)S(1)} %collective-permute-done.1.refs_2_) | copy-start | bytes 3145732
  37.6 23.1 %copy-start.5 = (bf16[512,1024]{1,0:T(8,128)(2,1)}, bf16[512,1024]{1,0:T(8,128)(2,1)S(1)}, u32[]{:S(2)}) copy-start(bf16[512,1024]{1,0:T(8,128)(2,1)S(1)} %collective-permute-done.2.refs_1_) | copy-start | bytes 3145732
  37.6 27.9 %collective-permute-start.4 = (bf16[512,1024]{1,0:T(8,128)(2,1)S(1)}, bf16[512,1024]{1,0:T(8,128)(2,1)}, u32[]{:S(2)}, u32[]{:S(2)}) collective-permute-start(bf16[512,1024]{1,0:T(8,128)(2,1)S(1)} %collective-permute-done.partner_ref.refs_4_), channel_id=1, source_target_pairs={{0,2},{2,0},{1,3},{3,1},{4,6},{6,4},{5,7},{7,5},{8,10},{10,8},{9,1... | collective-permute-start | bytes 3145736 | tf_op jit(solution)/shard_map/L_Bx1/ppermute | solution.py:34
  39.4 32.7 %copy-start.8 = (bf16[512,256]{1,0:T(8,128)(2,1)S(1)}, bf16[512,256]{1,0:T(8,128)(2,1)}, u32[]{:S(2)}) copy-start(bf16[512,256]{1,0:T(8,128)(2,1)} %get-tuple-element.66) | copy-start | bytes 786436
  39.4 15.4 %collective-permute-start.6 = (bf16[512,512]{1,0:T(8,128)(2,1)}, bf16[512,512]{1,0:T(8,128)(2,1)}, u32[]{:S(2)}, u32[]{:S(2)}) collective-permute-start(bf16[512,512]{1,0:T(8,128)(2,1)} %get-tuple-element.55), channel_id=1, source_target_pairs={{0,4},{4,0},{8,12},{12,8},{1,5},{5,1},{9,13},{13,9},{2,6},{6,2},{1... | collective-permute-start | bytes 1572872 | tf_op jit(solution)/shard_map/L_kv1/ppermute | solution.py:34
  42.1 23.5 %collective-permute-start.5 = (bf16[512,1024]{1,0:T(8,128)(2,1)S(1)}, bf16[512,1024]{1,0:T(8,128)(2,1)}, u32[]{:S(2)}, u32[]{:S(2)}) collective-permute-start(bf16[512,1024]{1,0:T(8,128)(2,1)S(1)} %collective-permute-done.partner_ref.refs_4_), channel_id=1, source_target_pairs={{0,1},{1,0},{2,3},{3,2},{4,5},{5,4},{6,7},{7,6},{8,9},{9,8},{10,11... | collective-permute-start | bytes 3145736 | tf_op jit(solution)/shard_map/L_B0c1/ppermute | solution.py:34
  42.1 23.5 %collective-permute-start.9 = (bf16[512,1024]{1,0:T(8,128)(2,1)S(1)}, bf16[512,1024]{1,0:T(8,128)(2,1)}, u32[]{:S(2)}, u32[]{:S(2)}) collective-permute-start(bf16[512,1024]{1,0:T(8,128)(2,1)S(1)} %collective-permute-done.1.refs_2_), channel_id=1, source_target_pairs={{0,1},{1,0},{2,3},{3,2},{4,5},{5,4},{6,7},{7,6},{8,9},{9,8},{10,11... | collective-permute-start | bytes 3145736 | tf_op jit(solution)/shard_map/L_A1c1/ppermute | solution.py:34
  42.6 23.0 %collective-permute-start.7 = (bf16[512,512]{1,0:T(8,128)(2,1)}, bf16[512,512]{1,0:T(8,128)(2,1)}, u32[]{:S(2)}, u32[]{:S(2)}) collective-permute-start(bf16[512,512]{1,0:T(8,128)(2,1)} %get-tuple-element.55), channel_id=1, source_target_pairs={{0,12},{4,8},{8,4},{12,0},{1,13},{5,9},{9,5},{13,1},{2,14},{6,10},... | collective-permute-start | bytes 1572872 | tf_op jit(solution)/shard_map/L_kv3/ppermute | solution.py:34
  54.8 10.8 %collective-permute-start.8 = (bf16[512,512]{1,0:T(8,128)(2,1)}, bf16[512,512]{1,0:T(8,128)(2,1)}, u32[]{:S(2)}, u32[]{:S(2)}) collective-permute-start(bf16[512,512]{1,0:T(8,128)(2,1)} %collective-permute-done.3.refs_3_), channel_id=1, source_target_pairs={{0,16},{16,0},{1,17},{17,1},{2,18},{18,2},{3,19},{19,3},{4,20},{20... | collective-permute-start | bytes 1572872 | tf_op jit(solution)/shard_map/L_ykv2/ppermute | solution.py:34
  65.6 24.1 %collective-permute-start.12 = (bf16[512,512]{1,0:T(8,128)(2,1)}, bf16[512,512]{1,0:T(8,128)(2,1)}, u32[]{:S(2)}, u32[]{:S(2)}) collective-permute-start(bf16[512,512]{1,0:T(8,128)(2,1)} %collective-permute-done.6.refs_2_), channel_id=1, source_target_pairs={{0,16},{16,0},{1,17},{17,1},{2,18},{18,2},{3,19},{19,3},{4,20},{20... | collective-permute-start | bytes 1572872 | tf_op jit(solution)/shard_map/L_ykv1/ppermute | solution.py:34
  67.2 22.5 %collective-permute-start.13 = (bf16[512,512]{1,0:T(8,128)(2,1)}, bf16[512,512]{1,0:T(8,128)(2,1)}, u32[]{:S(2)}, u32[]{:S(2)}) collective-permute-start(bf16[512,512]{1,0:T(8,128)(2,1)} %collective-permute-done.7.refs_4_), channel_id=1, source_target_pairs={{0,16},{16,0},{1,17},{17,1},{2,18},{18,2},{3,19},{19,3},{4,20},{20... | collective-permute-start | bytes 1572872 | tf_op jit(solution)/shard_map/L_ykv3/ppermute | solution.py:34
  67.7 22.0 %collective-permute-start.14 = (bf16[256,1024]{1,0:T(8,128)(2,1)}, bf16[256,1024]{1,0:T(8,128)(2,1)S(1)}, u32[]{:S(2)}, u32[]{:S(2)}) collective-permute-start(bf16[256,1024]{1,0:T(8,128)(2,1)} %compress.1.refs_8_), channel_id=1, source_target_pairs={{0,2},{2,0},{1,3},{3,1},{4,6},{6,4},{5,7},{7,5},{8,10},{10,8},{9,1... | collective-permute-start | bytes 1572872 | tf_op jit(solution)/shard_map/L_Cx1/ppermute | solution.py:34
  68.2 21.5 %collective-permute-start.10 = (bf16[512,256]{1,0:T(8,128)(2,1)}, bf16[512,256]{1,0:T(8,128)(2,1)S(1)}, u32[]{:S(2)}, u32[]{:S(2)}) collective-permute-start(bf16[512,256]{1,0:T(8,128)(2,1)} %get-tuple-element.64), channel_id=1, source_target_pairs={{0,8},{4,12},{8,0},{12,4},{1,9},{5,13},{9,1},{13,5},{2,10},{6,14},... | collective-permute-start | bytes 786440 | tf_op jit(solution)/shard_map/L_q2/ppermute | solution.py:34
  72.1 17.6 %collective-permute-start.11 = (bf16[512,256]{1,0:T(8,128)(2,1)S(1)}, bf16[512,256]{1,0:T(8,128)(2,1)S(1)}, u32[]{:S(2)}, u32[]{:S(2)}) collective-permute-start(bf16[512,256]{1,0:T(8,128)(2,1)S(1)} %copy-done.8), channel_id=1, source_target_pairs={{0,12},{4,8},{8,4},{12,0},{1,13},{5,9},{9,5},{13,1},{2,14},{6,10},... | collective-permute-start | bytes 786440 | tf_op jit(solution)/shard_map/L_q3/ppermute | solution.py:34
  89.7 8.2 %copy-start.6 = (bf16[256,1024]{1,0:T(8,128)(2,1)}, bf16[256,1024]{1,0:T(8,128)(2,1)S(1)}, u32[]{:S(2)}) copy-start(bf16[256,1024]{1,0:T(8,128)(2,1)S(1)} %collective-permute-done.14.refs_10_) | copy-start | bytes 1572868
  89.7 15.4 %collective-permute-start.18 = (bf16[512,1024]{1,0:T(8,128)(2,1)}, bf16[512,1024]{1,0:T(8,128)(2,1)}, u32[]{:S(2)}, u32[]{:S(2)}) collective-permute-start(bf16[512,1024]{1,0:T(8,128)(2,1)} %collective-permute-done.4.refs_6_), channel_id=1, source_target_pairs={{0,1},{1,0},{2,3},{3,2},{4,5},{5,4},{6,7},{7,6},{8,9},{9,8},{10,11... | collective-permute-start | bytes 3145736 | tf_op jit(solution)/shard_map/L_B1c1/ppermute | solution.py:34
  89.8 7.6 %collective-permute-start.19 = (bf16[256,1024]{1,0:T(8,128)(2,1)}, bf16[256,1024]{1,0:T(8,128)(2,1)S(1)}, u32[]{:S(2)}, u32[]{:S(2)}) collective-permute-start(bf16[256,1024]{1,0:T(8,128)(2,1)} %compress.1.refs_8_), channel_id=1, source_target_pairs={{0,1},{1,0},{2,3},{3,2},{4,5},{5,4},{6,7},{7,6},{8,9},{9,8},{10,11... | collective-permute-start | bytes 1572872 | tf_op jit(solution)/shard_map/L_C0c1/ppermute | solution.py:34
  90.3 7.9 %collective-permute-start.20 = (bf16[256,1024]{1,0:T(8,128)(2,1)S(1)}, bf16[256,1024]{1,0:T(8,128)(2,1)}, u32[]{:S(2)}, u32[]{:S(2)}) collective-permute-start(bf16[256,1024]{1,0:T(8,128)(2,1)S(1)} %collective-permute-done.14.refs_10_), channel_id=1, source_target_pairs={{0,1},{1,0},{2,3},{3,2},{4,5},{5,4},{6,7},{7,6},{8,9},{9,8},{10,11... | collective-permute-start | bytes 1572872 | tf_op jit(solution)/shard_map/L_C1c1/ppermute | solution.py:34
  91.0 20.8 %collective-permute-start.15 = (bf16[1024,256]{1,0:T(8,128)(2,1)}, bf16[1024,256]{1,0:T(8,128)(2,1)S(1)}, u32[]{:S(2)}, u32[]{:S(2)}) collective-permute-start(bf16[1024,256]{1,0:T(8,128)(2,1)} %get-tuple-element.76), channel_id=1, source_target_pairs={{0,4},{4,0},{8,12},{12,8},{1,5},{5,1},{9,13},{13,9},{2,6},{6,2},{1... | collective-permute-start | bytes 1572872 | tf_op jit(solution)/shard_map/L_q1/ppermute | solution.py:34
  95.9 15.6 %collective-permute-start.16 = (bf16[512,256]{1,0:T(8,128)(2,1)S(1)}, bf16[512,256]{1,0:T(8,128)(2,1)S(1)}, u32[]{:S(2)}, u32[]{:S(2)}) collective-permute-start(bf16[512,256]{1,0:T(8,128)(2,1)S(1)} %collective-permute-done.10.refs_4_), channel_id=1, source_target_pairs={{0,16},{16,0},{1,17},{17,1},{2,18},{18,2},{3,19},{19,3},{4,20},{20... | collective-permute-start | bytes 786440 | tf_op jit(solution)/shard_map/L_yq2/ppermute | solution.py:34
  97.4 0.8 copy-start.7
  97.4 14.1 %collective-permute-start.17 = (bf16[512,256]{1,0:T(8,128)(2,1)S(1)}, bf16[512,256]{1,0:T(8,128)(2,1)S(1)}, u32[]{:S(2)}, u32[]{:S(2)}) collective-permute-start(bf16[512,256]{1,0:T(8,128)(2,1)S(1)} %collective-permute-done.11.refs_5_), channel_id=1, source_target_pairs={{0,16},{16,0},{1,17},{17,1},{2,18},{18,2},{3,19},{19,3},{4,20},{20... | collective-permute-start | bytes 786440 | tf_op jit(solution)/shard_map/L_yq3/ppermute | solution.py:34
  103.1 14.9 %collective-permute-start.21 = (bf16[256,512]{1,0:T(8,128)(2,1)}, bf16[256,512]{1,0:T(8,128)(2,1)S(1)}, u32[]{:S(2)}, u32[]{:S(2)}) collective-permute-start(bf16[256,512]{1,0:T(8,128)(2,1)} %get-tuple-element.85.refs_10_), channel_id=1, source_target_pairs={{0,8},{4,12},{8,0},{12,4},{1,9},{5,13},{9,1},{13,5},{2,10},{6,14},... | collective-permute-start | bytes 786440 | tf_op jit(solution)/shard_map/L_m2/ppermute | solution.py:34
  105.1 12.9 %copy-start = (bf16[1024,512]{1,0:T(8,128)(2,1)S(1)}, bf16[1024,512]{1,0:T(8,128)(2,1)}, u32[]{:S(2)}) copy-start(bf16[1024,512]{1,0:T(8,128)(2,1)} %refs_2_.3) | copy-start | bytes 3145732
  105.1 12.9 %copy-start.1 = (bf16[256,512]{1,0:T(8,128)(2,1)S(1)}, bf16[256,512]{1,0:T(8,128)(2,1)}, u32[]{:S(2)}) copy-start(bf16[256,512]{1,0:T(8,128)(2,1)} %get-tuple-element.85.refs_10_) | copy-start | bytes 786436
  105.1 12.9 %copy-start.2 = (s32[8]{0:T(128)S(1)}, s32[8]{0:T(128)}, u32[]{:S(2)}) copy-start(s32[8]{0:T(128)} %refs_0_.6) | copy-start | bytes 100
  123.5 7.3 %collective-permute-start.22 = (bf16[512,256]{1,0:T(8,128)(2,1)S(1)}, bf16[512,256]{1,0:T(8,128)(2,1)S(1)}, u32[]{:S(2)}, u32[]{:S(2)}) collective-permute-start(bf16[512,256]{1,0:T(8,128)(2,1)S(1)} %attend.2), channel_id=1, source_target_pairs={{0,4},{4,0},{8,12},{12,8},{1,5},{5,1},{9,13},{13,9},{2,6},{6,2},{1... | collective-permute-start | bytes 786440 | tf_op jit(solution)/shard_map/L_ctx/ppermute | solution.py:34

commit v4 on v3

--- a/solution.py
+++ b/solution.py
@@ -20,7 +20,7 @@
     return pl.CostEstimate(flops=int(microseconds * 1.0e9), bytes_accessed=1000, transcendentals=0)
 F32 = jnp.float32
 ANY = pl.BlockSpec(memory_space=pl.ANY)
-MEMORY_LIMIT, TOKENS_LIMIT, VMEM_LIMIT = 58 << 20, 40 << 20, 40 << 20
+MEMORY_LIMIT, TOKENS_LIMIT, VMEM_LIMIT = 48 << 20, 38 << 20, 26 << 20
 SMEM = pl.BlockSpec(memory_space=pltpu.SMEM)
 VMEM = pl.BlockSpec(memory_space=pltpu.VMEM)
 
@@ -113,19 +113,21 @@
     )(own, partner, conv_weight)
 
 
-def weight_copies(planes, buffer, sems, owns, nears, fars):
+def weight_copies(buffer, sems, owns, nears, fars, far_order):
     plane, group = lax.axis_index("seq"), lax.axis_index("groups")
     depth = owns[0][0].shape[0]
     half = depth // 2
     pieces = [(ref.at[:, columns], aligned(plane, depth), place) for ref, columns, place in owns]
-    fars = iter(fars)
     for distance, near in enumerate(nears, 1):
         if near.shape[0] == depth:
             pieces.append((near, aligned(plane ^ distance, depth), slice(None)))
         else:
-            first = (plane ^ distance) * 2
-            pieces.append((near, aligned(first + group, half), slice(None)))
-            pieces.append((next(fars), aligned(first + 1 - group, half), slice(None)))
+            pieces.append((near, aligned((plane ^ distance) * 2 + group, half), slice(None)))
+    order = iter(far_order)
+    for far in fars:
+        for i in range(far.shape[0] // half):
+            place = aligned((plane ^ next(order)) * 2 + 1 - group, half)
+            pieces.append((far.at[pl.ds(i * half, half), :], place, slice(None)))
     copies = []
     for ref, rows, place in pieces:
         copies.append(pltpu.make_async_copy(ref, buffer.at[rows, place], sems.at[len(copies)]))
@@ -137,25 +139,30 @@
     return (tensor ^ (index // sub_size)) * sub_size + (sub ^ (index % sub_size))
 
 
-def memory_kernel(planes, tensor_size, sub_size, *refs):
-    blocks, others = tensor_size * sub_size, planes - 1
+def memory_kernel(planes, tensor_size, sub_size, far_order, halves, *refs):
+    blocks = tensor_size * sub_size
     wk, wv = refs[:2]
-    nears, fars, refs = refs[2 : 2 + others], refs[2 + others : 2 + 2 * others], refs[2 + 2 * others :]
+    nears, fars, refs = refs[2 : planes + 1], refs[planes + 1 : planes + 1 + halves], refs[planes + 1 + halves :]
     pieces, (out, wbuf, xbuf, acc, xsem, wsem) = refs[:blocks], refs[blocks:]
     width = wbuf.shape[1] // 2
     columns = aligned(lax.axis_index("seq") & 1, width)
     owns = [(wk, columns, slice(0, width)), (wv, columns, slice(width, 2 * width))]
-    wcopies = weight_copies(planes, wbuf, wsem, owns, nears, fars)
+    wcopies = weight_copies(wbuf, wsem, owns, nears, fars, far_order)
     xcopies = [pltpu.make_async_copy(pieces[j], xbuf.at[j], xsem.at[j]) for j in range(blocks)]
-    run_copies(wcopies + xcopies)
-    product_loop(tensor_size, sub_size, xbuf, pl.ds(0, out.shape[0]), wbuf, acc, out)
-
-
-def product_loop(tensor_size, sub_size, xbuf, rows, wbuf, acc, out):
+    for copy in wcopies + xcopies:
+        copy.start()
+    for copy in wcopies:
+        copy.wait()
+    product_loop(tensor_size, sub_size, xbuf, wbuf, acc, out, xcopies)
+
+
+def product_loop(tensor_size, sub_size, xbuf, wbuf, acc, out, waits=()):
     blocks, chunk = xbuf.shape[0], xbuf.shape[2]
     for j in range(blocks):
+        if waits:
+            waits[j].wait()
         weight = aligned(block_owner(j, tensor_size, sub_size), chunk)
-        part = jnp.dot(xbuf[j, rows, :], wbuf[weight, :], preferred_element_type=F32)
+        part = jnp.dot(xbuf[j], wbuf[weight, :], preferred_element_type=F32)
         if j:
             part += acc[...]
         if j < blocks - 1:
@@ -164,12 +171,12 @@
             out[...] = part.astype(BF)
 
 
-def project_memory(planes, tensor_size, sub_size, wk, wv, nears, fars, pieces):
+def project_memory(planes, tensor_size, sub_size, wk, wv, nears, fars, far_order, pieces):
     depth, columns = wk.shape
     blocks, (rows, chunk) = len(pieces), pieces[0].shape
     operands = [wk, wv, *nears, *fars, *pieces]
     return pl.pallas_call(
-        functools.partial(memory_kernel, planes, tensor_size, sub_size),
+        functools.partial(memory_kernel, planes, tensor_size, sub_size, far_order, len(fars)),
         out_shape=[jax.ShapeDtypeStruct((rows, columns), BF), pltpu.VMEM((depth * planes, columns), BF)],
         in_specs=[ANY] * len(operands),
         out_specs=[VMEM, VMEM],
@@ -224,24 +231,73 @@
     )(*own, *partner, resident(weights))
 
 
-def attend_kernel(side, planes, tensor_size, sub_size, halves, *refs):
-    segments, length, wq = refs[:3]
-    refs = refs[3:]
-    nears, fars, refs = refs[: planes - 1], refs[planes - 1 : planes - 1 + halves], refs[planes - 1 + halves :]
-    xbuf, kvbuf, refs = refs[0], refs[1], refs[2:]
-    mems, refs = refs[: planes // 2], refs[planes // 2 :]
-    out, wbuf, acc, qbuf, membuf, obuf, wsem, ksem = refs
+SCALE = HD ** (-0.5) * math.log2(math.e)
+CONTRACT = (((1,), (1,)), ((), ()))
+
+
+def local_kernel(side, planes, tensor_size, sub_size, far_order, halves, *refs):
+    refs = refs[1:]
+    if halves is None:
+        wbuf, xbuf, kvbuf, queries, sums, largest, totals = refs
+    else:
+        wq, refs = refs[0], refs[1:]
+        nears, fars, refs = refs[: planes - 1], refs[planes - 1 : planes - 1 + halves], refs[planes - 1 + halves :]
+        xbuf, kvbuf, queries, sums, largest, totals, wbuf, wsem = refs
+        owns = [(wq, aligned(lax.axis_index("seq") & 1, wbuf.shape[1]), slice(None))]
+        run_copies(weight_copies(wbuf, wsem, owns, nears, fars, far_order))
+    rows_here, width = queries.shape
+    here = pl.ds(side * rows_here, rows_here)
+    product_loop(tensor_size, sub_size, xbuf.at[:, here, :], wbuf, sums, queries)
+    row = lax.broadcasted_iota(jnp.int32, (SEG, SEG), 0)
+    causal = row >= lax.broadcasted_iota(jnp.int32, (SEG, SEG), 1)
+    for a in range(rows_here // SEG):
+        rows = slice(a * SEG, (a + 1) * SEG)
+        kvrows = slice(side * rows_here + a * SEG, side * rows_here + (a + 1) * SEG)
+        for h in range(width // HD):
+            ks, vs = slice(h * HD, (h + 1) * HD), slice(width + h * HD, width + (h + 1) * HD)
+            scores = lax.dot_general(queries[rows, ks], kvbuf[kvrows, ks], CONTRACT, preferred_element_type=F32)
+            scores = jnp.where(causal, scores * SCALE, -jnp.inf)
+            best = jnp.max(scores, axis=1, keepdims=True)
+            weights = jnp.exp2(scores - best)
+            largest[rows, ks] = jnp.broadcast_to(best, (SEG, HD))
+            totals[rows, ks] = jnp.broadcast_to(jnp.sum(weights, axis=1, keepdims=True), (SEG, HD))
+            sums[rows, ks] = jnp.dot(weights.astype(BF), kvbuf[kvrows, vs], preferred_element_type=F32)
+
+
+def attend_local(side, planes, tensor_size, sub_size, turn, weight, far_order, held, kv_tok):
+    rows, width = held.shape[1] // 2, kv_tok.shape[1] // 2
+    state = [pltpu.VMEM((rows, width), BF)] + [pltpu.VMEM((rows, width), F32)] * 3
+    scratch, halves = [], None
+    if isinstance(weight, tuple):
+        wq, nears, fars = weight
+        operands, halves = [wq, *nears, *fars], len(fars)
+        specs = [ANY] * len(operands)
+        state.append(pltpu.VMEM((wq.shape[0] * planes, width), BF))
+        scratch = [pltpu.SemaphoreType.DMA((planes + len(far_order),))]
+    else:
+        operands, specs = [resident(weight)], [VMEM]
+    return pl.pallas_call(
+        functools.partial(local_kernel, side, planes, tensor_size, sub_size, far_order, halves),
+        out_shape=state,
+        in_specs=[SMEM] + specs + [VMEM] * 2,
+        out_specs=[VMEM] * len(state),
+        scratch_shapes=scratch,
+        compiler_params=pltpu.CompilerParams(vmem_limit_bytes=VMEM_LIMIT),
+        cost_estimate=cost(4),
+        name="attend_local",
+    )(turn, *operands, resident(held), resident(kv_tok))
+
+
+def far_kernel(side, planes, segments, length, queries, sums, largest, totals, *refs):
+    mems, (out, membuf, obuf, sems) = refs[: planes // 2], refs[planes // 2 :]
     plane = lax.axis_index("seq")
-    rows_here, width = qbuf.shape
+    rows_here, width = obuf.shape
     slots = rows_here // SEG
-    owns = [(wq, aligned(plane & 1, width), slice(0, width))]
-    wcopies = weight_copies(planes, wbuf, wsem, owns, nears, fars)
     count = mems[0].shape[0]
-    kcopies = []
+    copies = []
     for i, mem in enumerate(mems):
-        kcopies.append(pltpu.make_async_copy(mem, membuf.at[pl.ds(i * count, count), :], ksem.at[1 + i]))
-    for copy in wcopies + kcopies:
-        copy.start()
+        copies.append(pltpu.make_async_copy(mem, membuf.at[pl.ds(i * count, count), :], sems.at[1 + i]))
+        copies[-1].start()
     per_plane = count // 2
     mem_total = membuf.shape[0]
     column = lax.broadcasted_iota(jnp.int32, (1, mem_total), 1)
@@ -251,64 +307,48 @@
             start = distance * per_plane + i * MEM
             inside = (column >= start) & (column < start + MEM)
             owner = jnp.where(inside, segments[(plane ^ distance) * slots + i], owner)
-    row = lax.broadcasted_iota(jnp.int32, (SEG, SEG), 0)
-    causal = row >= lax.broadcasted_iota(jnp.int32, (SEG, SEG), 1)
     position = lax.broadcasted_iota(jnp.int32, (SEG, HD), 0)
-    contract = (((1,), (1,)), ((), ()))
-    scale = HD ** (-0.5) * math.log2(math.e)
-    for copy in wcopies:
-        copy.wait()
-    product_loop(tensor_size, sub_size, xbuf, pl.ds(side * rows_here, rows_here), wbuf, acc, qbuf)
-    for copy in kcopies:
+    for copy in copies:
         copy.wait()
     for a in range(slots):
         rows = slice(a * SEG, (a + 1) * SEG)
-        kvrows = slice(side * rows_here + a * SEG, side * rows_here + (a + 1) * SEG)
         segment = segments[(plane ^ side) * slots + a]
         allowed = owner < segment
         valid = position + segment * SEG < length[0]
         for h in range(width // HD):
             ks, vs = slice(h * HD, (h + 1) * HD), slice(width + h * HD, width + (h + 1) * HD)
-            query = qbuf[rows, ks]
-            near = lax.dot_general(query, kvbuf[kvrows, ks], contract, preferred_element_type=F32)
-            far = lax.dot_general(query, membuf[:, ks], contract, preferred_element_type=F32)
-            near = jnp.where(causal, near * scale, -jnp.inf)
-            far = jnp.where(allowed, far * scale, -jnp.inf)
-            best = jnp.maximum(
-                jnp.max(near, axis=1, keepdims=True), jnp.max(far, axis=1, keepdims=True)
-            )
-            near, far = jnp.exp2(near - best), jnp.exp2(far - best)
-            denominator = jnp.sum(near, axis=1, keepdims=True) + jnp.sum(far, axis=1, keepdims=True)
-            numerator = jnp.dot(near.astype(BF), kvbuf[kvrows, vs], preferred_element_type=F32)
-            numerator += jnp.dot(far.astype(BF), membuf[:, vs], preferred_element_type=F32)
+            scores = lax.dot_general(queries[rows, ks], membuf[:, ks], CONTRACT, preferred_element_type=F32)
+            scores = jnp.where(allowed, scores * SCALE, -jnp.inf)
+            before = largest[rows, ks]
+            best = jnp.maximum(before[:, :1], jnp.max(scores, axis=1, keepdims=True))
+            weights = jnp.exp2(scores - best)
+            factor = jnp.exp2(before - best)
+            denominator = totals[rows, ks] * factor + jnp.sum(weights, axis=1, keepdims=True)
+            numerator = sums[rows, ks] * factor
+            numerator += jnp.dot(weights.astype(BF), membuf[:, vs], preferred_element_type=F32)
             obuf[rows, ks] = jnp.where(valid, numerator / denominator, 0.0).astype(BF)
     dest = out if side else out.at[:, aligned(plane & 1, width)]
-    copy = pltpu.make_async_copy(obuf, dest, ksem.at[0])
+    copy = pltpu.make_async_copy(obuf, dest, sems.at[0])
     copy.start()
     copy.wait()
 
 
-def attend(side, planes, tensor_size, sub_size, segments, length, wq, nears, fars, held, kv_tok, mems):
-    depth, columns = wq.shape
-    rows, width = held.shape[1] // 2, columns // 2
+def attend(side, planes, segments, length, state, mems):
+    rows, width = state[0].shape
     mem_total = len(mems) * mems[0].shape[0]
-    operands = [segments, length, wq, *nears, *fars, resident(held), resident(kv_tok), *mems]
-    return pl.pallas_call(
-        functools.partial(attend_kernel, side, planes, tensor_size, sub_size, len(fars)),
+    operands = [segments, length, *(resident(value) for value in state), *mems]
+    return pl.pallas_call(
+        functools.partial(far_kernel, side, planes),
         out_shape=jax.ShapeDtypeStruct((rows, width if side else 2 * width), BF),
-        in_specs=[SMEM, SMEM] + [ANY] * (len(operands) - 4 - len(mems)) + [VMEM] * 2 + [ANY] * len(mems),
+        in_specs=[SMEM, SMEM] + [VMEM] * len(state) + [ANY] * len(mems),
         out_specs=ANY,
         scratch_shapes=[
-            pltpu.VMEM((depth * planes, width), BF),
-            pltpu.VMEM((rows, width), F32),
-            pltpu.VMEM((rows, width), BF),
             pltpu.VMEM((mem_total, 2 * width), BF),
             pltpu.VMEM((rows, width), BF),
-            pltpu.SemaphoreType.DMA((1 + len(nears) + len(fars),)),
             pltpu.SemaphoreType.DMA((1 + len(mems),)),
         ],
         compiler_params=pltpu.CompilerParams(vmem_limit_bytes=VMEM_LIMIT),
-        cost_estimate=cost(6),
+        cost_estimate=cost(4),
         name="attend",
     )(*operands)
 
@@ -362,14 +402,20 @@
         sends |= within(got[f"Ax{k}"], f"A{k}")
     (both,) = stage(sends, compress(activations, partner, conv_weight))
     far_planes = range(2, planes)
-    stage(distant(far_planes, "q") | relayed(second, "kv") | across(both, "C"))
-    sends = within(both, "C0") | {"q1": (q_whole, "seq", 1)} | relayed(far_planes, "q")
+    second_kv = jnp.concatenate([got[f"kv{d}"] for d in second], axis=0)
+    stage(
+        distant(far_planes, "q")
+        | {"q1": (q_whole, "seq", 1), "ykv": (second_kv, "groups", 1)}
+        | across(both, "C")
+    )
+    sends = within(both, "C0") | relayed(far_planes, "q")
     for label in ("C", "B"):
         for k in range(1, tensor_size):
             sends |= within(got[f"{label}x{k}"], f"{label}{k}")
     before = tuple(got[key] for key in fresh)
     for key, (value, axis, distance) in sends.items():
-        got[key] = swap(after(value, *before), axis, distance, key)
+        held = before if axis == "groups" else ()
+        got[key] = swap(after(value, *held), axis, distance, key)
 
     def pieces(block, label):
         whole = []
@@ -381,15 +427,18 @@
     own_pieces, partner_pieces = pieces(activations, "A"), pieces(partner, "B")
     compressed_pieces = pieces(both, "C")
     sizes = (planes, tensor_size, sub_size)
-    kv_parts = ([got[f"kv{d}"] for d in every], [got[f"ykv{d}"] for d in every])
+    kv_parts = ([got[f"kv{d}"] for d in every], [got[f"ykv{d}"] for d in first] + [got["ykv"]], first + second)
     kv_mem, kv_held = project_memory(*sizes, key_weight, value_weight, *kv_parts, compressed_pieces)
     mems = [kv_mem] + [swap(kv_mem, "seq", d, f"m{d}") for d in range(2, planes, 2)]
     kv_tok, held = project_tokens(tensor_size, sub_size, own_pieces, partner_pieces, kv_held)
-    q_parts = ([got[f"q{d}"] for d in every], [got[f"yq{d}"] for d in far_planes])
-    shared = (book_length, query_weight, *q_parts, held, kv_tok, mems)
-    theirs = attend(1, *sizes, segment_for_slot, *shared)
+    q_parts = (query_weight, [got[f"q{d}"] for d in every], [got[f"yq{d}"] for d in far_planes])
+    q_order = list(far_planes)
+    *state, q_held = attend_local(1, *sizes, segment_for_slot, q_parts, q_order, held, kv_tok)
+    theirs = attend(1, planes, segment_for_slot, book_length, state, mems)
     returned = swap(theirs, "seq", 1, "ctx")
-    mine = attend(0, *sizes, after(segment_for_slot, theirs), *shared)
+    turn = after(segment_for_slot, theirs)
+    state = attend_local(0, *sizes, turn, q_held, q_order, held, kv_tok)
+    mine = attend(0, planes, segment_for_slot, book_length, state, mems)
     return lax.dynamic_update_slice(mine, returned, (0, (1 - parity) * theirs.shape[1]))
 
 

time: 132 us -> 128 us (0.970)
  starting transfers between devices: 32.3 us -> 26.6 us
  waiting for transfers between devices: 67.3 us -> 69.3 us
  local copies, waits for them, and re-layouts: 1.04 us -> 2.41 us
    ppermute x23 -> x22, starting transfers between devices: 32.3 us -> 26.6 us  [swap(): return lax.ppermute(value, axis, [(i, i ^ distance) for i in range(size)])]
    ppermute x23 -> x22, waiting for transfers between devices: 67.3 us -> 69.3 us  [swap(): return lax.ppermute(value, axis, [(i, i ^ distance) for i in range(size)])]
    unnamed x18 -> x20, local copies, waits for them, and re-layouts: 0.32 us -> 1.69 us
    pallas_call x2 -> x4, Pallas kernels: 11.6 us -> 12.3 us  [the longest x2 6.57 us: attend_local(): pl.pallas_call(functools.partial(local_kernel, side, planes, tensor_size,...]
  transfers between devices with their start and end apart: 23 -> 22, of which waited for: 8 -> 9; matrix products, arithmetic and copies ran while one was open for 0% -> 0% of each run, Pallas kernels for 19% -> 21%
where the time goes in v4:
time: 128 us
  waiting for transfers between devices  69.3 us (54%)
  Pallas kernels  29.1 us (23%)
  starting transfers between devices  26.6 us (21%)
  local copies, waits for them, and re-layouts  2.41 us (2%)
    ppermute x22, waiting for transfers between devices, swap(): return lax.ppermute(value, axis, [(i, i ^ distance) for i in range(size)])  69.3 us
    ppermute x22, starting transfers between devices, swap(): return lax.ppermute(value, axis, [(i, i ^ distance) for i in range(size)])  26.6 us
    pallas_call x2, Pallas kernels, attend_local(): pl.pallas_call(functools.partial(local_kernel, side, planes, tensor_size,...  6.57 us
    pallas_call x1, Pallas kernels, project_tokens(): pl.pallas_call(functools.partial(tokens_kernel, tensor_size, sub_size), o...  5.84 us
    pallas_call x2, Pallas kernels, attend(): pl.pallas_call(functools.partial(far_kernel, side, planes), out_shape=jax...  5.76 us
    pallas_call x1, Pallas kernels, compress(): pl.pallas_call(compress_kernel, out_shape=jax.ShapeDtypeStruct((2 * count...  4.51 us
    pallas_call x1, Pallas kernels, project_memory(): pl.pallas_call(functools.partial(memory_kernel, planes, tensor_size, sub_...  3.54 us
    pallas_call x1, Pallas kernels, split_weights(): pl.pallas_call(split_kernel, out_shape=[jax.ShapeDtypeStruct(s, BF) for s...  2.91 us
  transfers between devices with their start and end apart: 22, of which 9 were waited for; matrix products, arithmetic and copies ran while one was open for 0% of the time, Pallas kernels for 21%

profile of v4, /device:TPU:0, one launch (start us, length us, event | category | flops | bytes accessed | tf_op | source)
XLA Modules:
  0.0 128.3 jit_solution(7844253647343905010)
XLA Ops:
  0.0 3.0 %collective-permute-start = (bf16[512,1024]{1,0:T(8,128)(2,1)}, bf16[512,1024]{1,0:T(8,128)(2,1)}, u32[]{:S(2)}, u32[]{:S(2)}) collective-permute-start(bf16[512,1024]{1,0:T(8,128)(2,1)} %refs_0_.4), channel_id=1, source_target_pairs={{0,4},{4,0},{8,12},{12,8},{1,5},{5,1},{9,13},{13,9},{2,6},{6,2},{1... | collective-permute-start | bytes 3145736 | tf_op jit(solution)/shard_map/L_Xz/ppermute | solution.py:34
  3.0 1.5 %collective-permute-start.1 = (bf16[512,1024]{1,0:T(8,128)(2,1)}, bf16[512,1024]{1,0:T(8,128)(2,1)}, u32[]{:S(2)}, u32[]{:S(2)}) collective-permute-start(bf16[512,1024]{1,0:T(8,128)(2,1)} %refs_0_.4), channel_id=1, source_target_pairs={{0,2},{2,0},{1,3},{3,1},{4,6},{6,4},{5,7},{7,5},{8,10},{10,8},{9,1... | collective-permute-start | bytes 3145736 | tf_op jit(solution)/shard_map/L_Ax1/ppermute | solution.py:34
  4.5 0.0 collective-permute-start.2
  4.5 2.9 %split_weights.1 = (bf16[512,512]{1,0:T(8,128)(2,1)}, bf16[512,512]{1,0:T(8,128)(2,1)}, bf16[512,256]{1,0:T(8,128)(2,1)}, bf16[512,256]{1,0:T(8,128)(2,1)}, bf16[1024,256]{1,0:T(8,128)(2,1)}) custom-call(bf16[1024,512]{1,0:T(8,128)(2,1)} %refs_0_.3, bf16[1024,512]{1,0:T(8,128)(2,1)} %refs_1_.2, bf16[1024,512]{1,0:T(8,128)(2,1)} %refs_1_.3), custom_call_target="tpu_custom_call" | custom-call | flops 2000000000 | bytes 1000 | tf_op jit(solution)/shard_map/split_weights/pallas_call | solution.py:74
  7.4 2.7 %collective-permute-start.3 = (bf16[512,512]{1,0:T(8,128)(2,1)}, bf16[512,512]{1,0:T(8,128)(2,1)S(1)}, u32[]{:S(2)}, u32[]{:S(2)}) collective-permute-start(bf16[512,512]{1,0:T(8,128)(2,1)} %get-tuple-element.52), channel_id=1, source_target_pairs={{0,8},{4,12},{8,0},{12,4},{1,9},{5,13},{9,1},{13,5},{2,10},{6,14},... | collective-permute-start | bytes 1572872 | tf_op jit(solution)/shard_map/L_kv2/ppermute | solution.py:34
  10.1 26.9 %collective-permute-done.3.refs_3_ = bf16[512,512]{1,0:T(8,128)(2,1)S(1)} collective-permute-done((bf16[512,512]{1,0:T(8,128)(2,1)}, bf16[512,512]{1,0:T(8,128)(2,1)S(1)}, u32[]{:S(2)}, u32[]{:S(2)}) %collective-permute-start.3) | collective-permute-done | bytes 524320 | tf_op jit(solution)/shard_map/L_kv2/ppermute | solution.py:34
  37.0 0.7 collective-permute-done.partner_ref.refs_4_
  37.7 0.0 collective-permute-done.1.refs_2_
  37.7 0.0 collective-permute-done.2.refs_1_
  37.7 1.7 %collective-permute-start.4 = (bf16[512,1024]{1,0:T(8,128)(2,1)}, bf16[512,1024]{1,0:T(8,128)(2,1)}, u32[]{:S(2)}, u32[]{:S(2)}) collective-permute-start(bf16[512,1024]{1,0:T(8,128)(2,1)} %collective-permute-done.partner_ref.refs_4_), channel_id=1, source_target_pairs={{0,2},{2,0},{1,3},{3,1},{4,6},{6,4},{5,7},{7,5},{8,10},{10,8},{9,1... | collective-permute-start | bytes 3145736 | tf_op jit(solution)/shard_map/L_Bx1/ppermute | solution.py:34
  39.4 2.6 %collective-permute-start.6 = (bf16[512,512]{1,0:T(8,128)(2,1)}, bf16[512,512]{1,0:T(8,128)(2,1)S(1)}, u32[]{:S(2)}, u32[]{:S(2)}) collective-permute-start(bf16[512,512]{1,0:T(8,128)(2,1)} %get-tuple-element.59), channel_id=1, source_target_pairs={{0,4},{4,0},{8,12},{12,8},{1,5},{5,1},{9,13},{13,9},{2,6},{6,2},{1... | collective-permute-start | bytes 1572872 | tf_op jit(solution)/shard_map/L_kv1/ppermute | solution.py:34
  42.0 0.0 collective-permute-start.5
  42.0 0.5 collective-permute-start.9
  42.5 1.3 %collective-permute-start.7 = (bf16[512,512]{1,0:T(8,128)(2,1)}, bf16[512,512]{1,0:T(8,128)(2,1)S(1)}, u32[]{:S(2)}, u32[]{:S(2)}) collective-permute-start(bf16[512,512]{1,0:T(8,128)(2,1)} %get-tuple-element.59), channel_id=1, source_target_pairs={{0,12},{4,8},{8,4},{12,0},{1,13},{5,9},{9,5},{13,1},{2,14},{6,10},... | collective-permute-start | bytes 1572872 | tf_op jit(solution)/shard_map/L_kv3/ppermute | solution.py:34
  43.8 10.8 %collective-permute-done.6.refs_2_ = bf16[512,512]{1,0:T(8,128)(2,1)S(1)} collective-permute-done((bf16[512,512]{1,0:T(8,128)(2,1)}, bf16[512,512]{1,0:T(8,128)(2,1)S(1)}, u32[]{:S(2)}, u32[]{:S(2)}) %collective-permute-start.6) | collective-permute-done | bytes 524320 | tf_op jit(solution)/shard_map/L_kv1/ppermute | solution.py:34
  54.6 1.5 %collective-permute-start.8 = (bf16[512,512]{1,0:T(8,128)(2,1)S(1)}, bf16[512,512]{1,0:T(8,128)(2,1)S(1)}, u32[]{:S(2)}, u32[]{:S(2)}) collective-permute-start(bf16[512,512]{1,0:T(8,128)(2,1)S(1)} %collective-permute-done.3.refs_3_), channel_id=1, source_target_pairs={{0,16},{16,0},{1,17},{17,1},{2,18},{18,2},{3,19},{19,3},{4,20},{20... | collective-permute-start | bytes 1572872 | tf_op jit(solution)/shard_map/L_ykv2/ppermute | solution.py:34
  56.2 4.5 %compress.1.refs_7_ = bf16[256,1024]{1,0:T(8,128)(2,1)} custom-call(bf16[512,1024]{1,0:T(8,128)(2,1)} %refs_0_.4, bf16[512,1024]{1,0:T(8,128)(2,1)} %collective-permute-done.partner_ref.refs_4_, bf16[512,1024]{1,0:T(8,128)(2,1)} %w_ref.1), custom_call_target="tpu_custom_call" | custom-call | flops 5000000000 | bytes 1000 | tf_op jit(solution)/shard_map/compress/pallas_call | solution.py:106
  60.7 4.7 %collective-permute-done.7.refs_4_ = bf16[512,512]{1,0:T(8,128)(2,1)S(1)} collective-permute-done((bf16[512,512]{1,0:T(8,128)(2,1)}, bf16[512,512]{1,0:T(8,128)(2,1)S(1)}, u32[]{:S(2)}, u32[]{:S(2)}) %collective-permute-start.7) | collective-permute-done | bytes 524320 | tf_op jit(solution)/shard_map/L_kv3/ppermute | solution.py:34
  65.3 0.0 collective-permute-done.8.refs_5_
  65.3 0.0 collective-permute-done.4.refs_6_
  65.4 0.0 collective-permute-done.5.refs_5_
  65.4 0.0 collective-permute-done.9.refs_3_
  65.4 0.1 pad_maximum_fusion
  65.4 1.6 %collective-permute-start.13 = (bf16[1024,512]{1,0:T(8,128)(2,1)S(1)}, bf16[1024,512]{1,0:T(8,128)(2,1)S(1)}, u32[]{:S(2)}, u32[]{:S(2)}) collective-permute-start(bf16[1024,512]{1,0:T(8,128)(2,1)S(1)} %pad_maximum_fusion), channel_id=1, source_target_pairs={{0,16},{16,0},{1,17},{17,1},{2,18},{18,2},{3,19},{19,3},{4,20},{20... | collective-permute-start | bytes 3145736 | tf_op jit(solution)/shard_map/L_ykv/ppermute | solution.py:34
  67.0 0.0 copy-done.6
  67.0 0.0 copy-done.7
  67.0 2.8 %collective-permute-start.12 = (bf16[1024,256]{1,0:T(8,128)(2,1)S(1)}, bf16[1024,256]{1,0:T(8,128)(2,1)S(1)}, u32[]{:S(2)}, u32[]{:S(2)}) collective-permute-start(bf16[1024,256]{1,0:T(8,128)(2,1)S(1)} %copy-done.7), channel_id=1, source_target_pairs={{0,4},{4,0},{8,12},{12,8},{1,5},{5,1},{9,13},{13,9},{2,6},{6,2},{1... | collective-permute-start | bytes 1572872 | tf_op jit(solution)/shard_map/L_q1/ppermute | solution.py:34
  69.9 0.5 collective-permute-start.14
  70.4 0.0 copy-done.9
  70.4 1.2 collective-permute-start.10
  71.7 0.0 copy-done.8
  71.7 1.5 %collective-permute-start.11 = (bf16[512,256]{1,0:T(8,128)(2,1)S(1)}, bf16[512,256]{1,0:T(8,128)(2,1)S(1)}, u32[]{:S(2)}, u32[]{:S(2)}) collective-permute-start(bf16[512,256]{1,0:T(8,128)(2,1)S(1)} %copy-done.8), channel_id=1, source_target_pairs={{0,12},{4,8},{8,4},{12,0},{1,13},{5,9},{9,5},{13,1},{2,14},{6,10},... | collective-permute-start | bytes 786440 | tf_op jit(solution)/shard_map/L_q3/ppermute | solution.py:34
  73.1 14.8 %collective-permute-done.10.refs_3_ = bf16[512,256]{1,0:T(8,128)(2,1)S(1)} collective-permute-done((bf16[512,256]{1,0:T(8,128)(2,1)S(1)}, bf16[512,256]{1,0:T(8,128)(2,1)S(1)}, u32[]{:S(2)}, u32[]{:S(2)}) %collective-permute-start.10) | collective-permute-done | bytes 262176 | tf_op jit(solution)/shard_map/L_q2/ppermute | solution.py:34
  87.9 0.0 collective-permute-start.17
  87.9 6.6 %collective-permute-done.11.refs_4_ = bf16[512,256]{1,0:T(8,128)(2,1)S(1)} collective-permute-done((bf16[512,256]{1,0:T(8,128)(2,1)S(1)}, bf16[512,256]{1,0:T(8,128)(2,1)S(1)}, u32[]{:S(2)}, u32[]{:S(2)}) %collective-permute-start.11) | collective-permute-done | bytes 262176 | tf_op jit(solution)/shard_map/L_q3/ppermute | solution.py:34
  94.5 0.0 collective-permute-start.18
  94.5 0.0 collective-permute-done.12.refs_2_
  94.5 0.7 copy-done.2
  95.2 0.0 collective-permute-done.14.refs_9_
  95.2 0.0 collective-permute-done.13.refs_6_
  95.2 1.0 copy-done.5
  96.2 0.0 collective-permute-start.19
  96.9 0.0 copy-start
  96.9 1.0 collective-permute-start.15
  97.8 1.1 collective-permute-start.16
  99.0 0.0 collective-permute-done.18.refs_8_
  99.0 0.0 collective-permute-done.19.refs_10_
  99.0 3.5 %project_memory.1 = (bf16[256,512]{1,0:T(8,128)(2,1)S(1)}, bf16[4096,512]{1,0:T(8,128)(2,1)S(1)}) custom-call(bf16[1024,512]{1,0:T(8,128)(2,1)} %refs_0_.3, bf16[1024,512]{1,0:T(8,128)(2,1)} %refs_1_.2, bf16[512,512]{1,0:T(8,128)(2,1)S(1)} %collective-permute-done.6.refs_2_, bf16[512,512]{1,0:T(8,128)(2,1)S(1)} %collective-permute-done.3.refs_3_, ...), custom_call_target="tpu_custom_call" | custom-call | flops 4000000000 | bytes 1000 | tf_op jit(solution)/shard_map/project_memory/pallas_call | solution.py:178
  102.5 2.0 %collective-permute-start.20 = (bf16[256,512]{1,0:T(8,128)(2,1)S(1)}, bf16[256,512]{1,0:T(8,128)(2,1)S(1)}, u32[]{:S(2)}, u32[]{:S(2)}) collective-permute-start(bf16[256,512]{1,0:T(8,128)(2,1)S(1)} %get-tuple-element.90.refs_0_), channel_id=1, source_target_pairs={{0,8},{4,12},{8,0},{12,4},{1,9},{5,13},{9,1},{13,5},{2,10},{6,14},... | collective-permute-start | bytes 786440 | tf_op jit(solution)/shard_map/L_m2/ppermute | solution.py:34
  104.5 0.0 collective-permute-done.17.refs_7_
  104.5 0.0 copy-start.4
  104.6 5.8 %project_tokens.1 = (bf16[1024,512]{1,0:T(8,128)(2,1)S(1)}, bf16[4,1024,1024]{2,1,0:T(8,128)(2,1)S(1)}) custom-call(bf16[512,1024]{1,0:T(8,128)(2,1)S(1)} %copy-done, bf16[512,1024]{1,0:T(8,128)(2,1)S(1)} %collective-permute-done.2.refs_1_, bf16[512,1024]{1,0:T(8,128)(2,1)} %collective-permute-done.1.refs_2_, ...), custom_call_target="tpu_custom_call" | custom-call | flops 6000000000 | bytes 1000 | tf_op jit(solution)/shard_map/project_tokens/pallas_call | solution.py:222
  110.4 0.0 collective-permute-done.15.refs_5_
  110.4 0.9 collective-permute-done.16.refs_6_
  111.3 0.0 copy-done.1
  111.3 0.0 copy-done.4
  111.3 3.4 %attend_local.2 = (bf16[512,256]{1,0:T(8,128)(2,1)S(1)}, f32[512,256]{1,0:T(8,128)S(1)}, f32[512,256]{1,0:T(8,128)S(1)}, f32[512,256]{1,0:T(8,128)S(1)}, bf16[4096,256]{1,0:T(8,128)(2,1)S(1)}) custom-call(s32[8]{0:T(128)S(1)} %copy-done.4, bf16[1024,512]{1,0:T(8,128)(2,1)S(1)} %copy-done.1, bf16[1024,256]{1,0:T(8,128)(2,1)S(1)} %collective-permute-done.12.refs_2_, ...), custom_call_target="tpu_custom_call" | custom-call | flops 4000000000 | bytes 1000 | tf_op jit(solution)/shard_map/attend_local/pallas_call | solution.py:279
  114.7 2.6 %collective-permute-done.20.refs_1_ = bf16[256,512]{1,0:T(8,128)(2,1)S(1)} collective-permute-done((bf16[256,512]{1,0:T(8,128)(2,1)S(1)}, bf16[256,512]{1,0:T(8,128)(2,1)S(1)}, u32[]{:S(2)}, u32[]{:S(2)}) %collective-permute-start.20) | collective-permute-done | bytes 262176 | tf_op jit(solution)/shard_map/L_m2/ppermute | solution.py:34
  117.3 2.5 %attend.2 = bf16[512,256]{1,0:T(8,128)(2,1)S(1)} custom-call(s32[8]{0:T(128)S(1)} %copy-done.4, s32[1]{0:T(128)S(6)} %copy.9.length, bf16[512,256]{1,0:T(8,128)(2,1)S(1)} %get-tuple-element.86.queries, f32[512,256]{1,0:T(8,128)S(1)} %get-tuple-element.87.sums, f32[512,256]{1,0:T(8,128)S(1)} %get-tuple-element.88.largest, ...), custom_call_target="tpu_custom_call" | custom-call | flops 4000000000 | bytes 1000 | tf_op jit(solution)/shard_map/attend/pallas_call | solution.py:340
  119.8 0.1 collective-permute-start.21
  119.9 3.2 %attend_local.3 = (bf16[512,256]{1,0:T(8,128)(2,1)S(1)}, f32[512,256]{1,0:T(8,128)S(1)}, f32[512,256]{1,0:T(8,128)S(1)}, f32[512,256]{1,0:T(8,128)S(1)}) custom-call(s32[8]{0:T(128)S(1)} %copy-done.4, bf16[4096,256]{1,0:T(8,128)(2,1)S(1)} %get-tuple-element.92.refs_1_, bf16[4,1024,1024]{2,1,0:T(8,128)(2,1)S(1)} %get-tuple-element.84.refs_7_.refs_2_, ...), custom_call_target="tpu_custom_call" | custom-call | flops 4000000000 | bytes 1000 | tf_op jit(solution)/shard_map/attend_local/pallas_call | solution.py:279
  123.1 3.2 %attend.3 = bf16[512,512]{1,0:T(8,128)(2,1)} custom-call(s32[8]{0:T(128)S(1)} %copy-done.4, s32[1]{0:T(128)S(6)} %copy.9.length, bf16[512,256]{1,0:T(8,128)(2,1)S(1)} %get-tuple-element.93.queries, f32[512,256]{1,0:T(8,128)S(1)} %get-tuple-element.94.sums, f32[512,256]{1,0:T(8,128)S(1)} %get-tuple-element.95.largest, ...), custom_call_target="tpu_custom_call" | custom-call | flops 4000000000 | bytes 1000 | tf_op jit(solution)/shard_map/attend/pallas_call | solution.py:340
  126.3 1.3 %collective-permute-done.21 = bf16[512,256]{1,0:T(8,128)(2,1)S(1)} collective-permute-done((bf16[512,256]{1,0:T(8,128)(2,1)S(1)}, bf16[512,256]{1,0:T(8,128)(2,1)S(1)}, u32[]{:S(2)}, u32[]{:S(2)}) %collective-permute-start.21) | collective-permute-done | bytes 262176 | tf_op jit(solution)/shard_map/L_ctx/ppermute | solution.py:34
  127.6 0.7 constant_dynamic-update-slice_fusion
  (10 shorter events, 0.0 us)
Async XLA Ops:
  0.0 37.7 %collective-permute-start = (bf16[512,1024]{1,0:T(8,128)(2,1)}, bf16[512,1024]{1,0:T(8,128)(2,1)}, u32[]{:S(2)}, u32[]{:S(2)}) collective-permute-start(bf16[512,1024]{1,0:T(8,128)(2,1)} %refs_0_.4), channel_id=1, source_target_pairs={{0,4},{4,0},{8,12},{12,8},{1,5},{5,1},{9,13},{13,9},{2,6},{6,2},{1... | collective-permute-start | bytes 3145736 | tf_op jit(solution)/shard_map/L_Xz/ppermute | solution.py:34
  3.0 34.7 %collective-permute-start.1 = (bf16[512,1024]{1,0:T(8,128)(2,1)}, bf16[512,1024]{1,0:T(8,128)(2,1)}, u32[]{:S(2)}, u32[]{:S(2)}) collective-permute-start(bf16[512,1024]{1,0:T(8,128)(2,1)} %refs_0_.4), channel_id=1, source_target_pairs={{0,2},{2,0},{1,3},{3,1},{4,6},{6,4},{5,7},{7,5},{8,10},{10,8},{9,1... | collective-permute-start | bytes 3145736 | tf_op jit(solution)/shard_map/L_Ax1/ppermute | solution.py:34
  4.5 33.2 %collective-permute-start.2 = (bf16[512,1024]{1,0:T(8,128)(2,1)}, bf16[512,1024]{1,0:T(8,128)(2,1)S(1)}, u32[]{:S(2)}, u32[]{:S(2)}) collective-permute-start(bf16[512,1024]{1,0:T(8,128)(2,1)} %refs_0_.4), channel_id=1, source_target_pairs={{0,1},{1,0},{2,3},{3,2},{4,5},{5,4},{6,7},{7,6},{8,9},{9,8},{10,11... | collective-permute-start | bytes 3145736 | tf_op jit(solution)/shard_map/L_A0c1/ppermute | solution.py:34
  7.4 29.6 %collective-permute-start.3 = (bf16[512,512]{1,0:T(8,128)(2,1)}, bf16[512,512]{1,0:T(8,128)(2,1)S(1)}, u32[]{:S(2)}, u32[]{:S(2)}) collective-permute-start(bf16[512,512]{1,0:T(8,128)(2,1)} %get-tuple-element.52), channel_id=1, source_target_pairs={{0,8},{4,12},{8,0},{12,4},{1,9},{5,13},{9,1},{13,5},{2,10},{6,14},... | collective-permute-start | bytes 1572872 | tf_op jit(solution)/shard_map/L_kv2/ppermute | solution.py:34
  37.7 27.6 %collective-permute-start.4 = (bf16[512,1024]{1,0:T(8,128)(2,1)}, bf16[512,1024]{1,0:T(8,128)(2,1)}, u32[]{:S(2)}, u32[]{:S(2)}) collective-permute-start(bf16[512,1024]{1,0:T(8,128)(2,1)} %collective-permute-done.partner_ref.refs_4_), channel_id=1, source_target_pairs={{0,2},{2,0},{1,3},{3,1},{4,6},{6,4},{5,7},{7,5},{8,10},{10,8},{9,1... | collective-permute-start | bytes 3145736 | tf_op jit(solution)/shard_map/L_Bx1/ppermute | solution.py:34
  39.4 15.2 %collective-permute-start.6 = (bf16[512,512]{1,0:T(8,128)(2,1)}, bf16[512,512]{1,0:T(8,128)(2,1)S(1)}, u32[]{:S(2)}, u32[]{:S(2)}) collective-permute-start(bf16[512,512]{1,0:T(8,128)(2,1)} %get-tuple-element.59), channel_id=1, source_target_pairs={{0,4},{4,0},{8,12},{12,8},{1,5},{5,1},{9,13},{13,9},{2,6},{6,2},{1... | collective-permute-start | bytes 1572872 | tf_op jit(solution)/shard_map/L_kv1/ppermute | solution.py:34
  42.0 23.4 %collective-permute-start.5 = (bf16[512,1024]{1,0:T(8,128)(2,1)}, bf16[512,1024]{1,0:T(8,128)(2,1)}, u32[]{:S(2)}, u32[]{:S(2)}) collective-permute-start(bf16[512,1024]{1,0:T(8,128)(2,1)} %collective-permute-done.partner_ref.refs_4_), channel_id=1, source_target_pairs={{0,1},{1,0},{2,3},{3,2},{4,5},{5,4},{6,7},{7,6},{8,9},{9,8},{10,11... | collective-permute-start | bytes 3145736 | tf_op jit(solution)/shard_map/L_B0c1/ppermute | solution.py:34
  42.0 23.4 %collective-permute-start.9 = (bf16[512,1024]{1,0:T(8,128)(2,1)}, bf16[512,1024]{1,0:T(8,128)(2,1)}, u32[]{:S(2)}, u32[]{:S(2)}) collective-permute-start(bf16[512,1024]{1,0:T(8,128)(2,1)} %collective-permute-done.1.refs_2_), channel_id=1, source_target_pairs={{0,1},{1,0},{2,3},{3,2},{4,5},{5,4},{6,7},{7,6},{8,9},{9,8},{10,11... | collective-permute-start | bytes 3145736 | tf_op jit(solution)/shard_map/L_A1c1/ppermute | solution.py:34
  42.5 22.9 %collective-permute-start.7 = (bf16[512,512]{1,0:T(8,128)(2,1)}, bf16[512,512]{1,0:T(8,128)(2,1)S(1)}, u32[]{:S(2)}, u32[]{:S(2)}) collective-permute-start(bf16[512,512]{1,0:T(8,128)(2,1)} %get-tuple-element.59), channel_id=1, source_target_pairs={{0,12},{4,8},{8,4},{12,0},{1,13},{5,9},{9,5},{13,1},{2,14},{6,10},... | collective-permute-start | bytes 1572872 | tf_op jit(solution)/shard_map/L_kv3/ppermute | solution.py:34
  54.6 10.7 %collective-permute-start.8 = (bf16[512,512]{1,0:T(8,128)(2,1)S(1)}, bf16[512,512]{1,0:T(8,128)(2,1)S(1)}, u32[]{:S(2)}, u32[]{:S(2)}) collective-permute-start(bf16[512,512]{1,0:T(8,128)(2,1)S(1)} %collective-permute-done.3.refs_3_), channel_id=1, source_target_pairs={{0,16},{16,0},{1,17},{17,1},{2,18},{18,2},{3,19},{19,3},{4,20},{20... | collective-permute-start | bytes 1572872 | tf_op jit(solution)/shard_map/L_ykv2/ppermute | solution.py:34
  60.7 6.4 %copy-start.7 = (bf16[1024,256]{1,0:T(8,128)(2,1)S(1)}, bf16[1024,256]{1,0:T(8,128)(2,1)}, u32[]{:S(2)}) copy-start(bf16[1024,256]{1,0:T(8,128)(2,1)} %get-tuple-element.72) | copy-start | bytes 1572868
  60.7 9.7 %copy-start.9 = (bf16[512,256]{1,0:T(8,128)(2,1)S(1)}, bf16[512,256]{1,0:T(8,128)(2,1)}, u32[]{:S(2)}) copy-start(bf16[512,256]{1,0:T(8,128)(2,1)} %get-tuple-element.68) | copy-start | bytes 786436
  60.7 11.0 %copy-start.8 = (bf16[512,256]{1,0:T(8,128)(2,1)S(1)}, bf16[512,256]{1,0:T(8,128)(2,1)}, u32[]{:S(2)}) copy-start(bf16[512,256]{1,0:T(8,128)(2,1)} %get-tuple-element.70) | copy-start | bytes 786436
  65.3 1.7 %copy-start.6 = (bf16[512,512]{1,0:T(8,128)(2,1)}, bf16[512,512]{1,0:T(8,128)(2,1)S(1)}, u32[]{:S(2)}) copy-start(bf16[512,512]{1,0:T(8,128)(2,1)S(1)} %collective-permute-done.8.refs_5_) | copy-start | bytes 1572868
  65.4 29.8 %collective-permute-start.13 = (bf16[1024,512]{1,0:T(8,128)(2,1)S(1)}, bf16[1024,512]{1,0:T(8,128)(2,1)S(1)}, u32[]{:S(2)}, u32[]{:S(2)}) collective-permute-start(bf16[1024,512]{1,0:T(8,128)(2,1)S(1)} %pad_maximum_fusion), channel_id=1, source_target_pairs={{0,16},{16,0},{1,17},{17,1},{2,18},{18,2},{3,19},{19,3},{4,20},{20... | collective-permute-start | bytes 3145736 | tf_op jit(solution)/shard_map/L_ykv/ppermute | solution.py:34
  67.0 27.5 %collective-permute-start.12 = (bf16[1024,256]{1,0:T(8,128)(2,1)S(1)}, bf16[1024,256]{1,0:T(8,128)(2,1)S(1)}, u32[]{:S(2)}, u32[]{:S(2)}) collective-permute-start(bf16[1024,256]{1,0:T(8,128)(2,1)S(1)} %copy-done.7), channel_id=1, source_target_pairs={{0,4},{4,0},{8,12},{12,8},{1,5},{5,1},{9,13},{13,9},{2,6},{6,2},{1... | collective-permute-start | bytes 1572872 | tf_op jit(solution)/shard_map/L_q1/ppermute | solution.py:34
  69.9 25.4 %collective-permute-start.14 = (bf16[256,1024]{1,0:T(8,128)(2,1)}, bf16[256,1024]{1,0:T(8,128)(2,1)}, u32[]{:S(2)}, u32[]{:S(2)}) collective-permute-start(bf16[256,1024]{1,0:T(8,128)(2,1)} %compress.1.refs_7_), channel_id=1, source_target_pairs={{0,2},{2,0},{1,3},{3,1},{4,6},{6,4},{5,7},{7,5},{8,10},{10,8},{9,1... | collective-permute-start | bytes 1572872 | tf_op jit(solution)/shard_map/L_Cx1/ppermute | solution.py:34
  70.4 17.5 %collective-permute-start.10 = (bf16[512,256]{1,0:T(8,128)(2,1)S(1)}, bf16[512,256]{1,0:T(8,128)(2,1)S(1)}, u32[]{:S(2)}, u32[]{:S(2)}) collective-permute-start(bf16[512,256]{1,0:T(8,128)(2,1)S(1)} %copy-done.9), channel_id=1, source_target_pairs={{0,8},{4,12},{8,0},{12,4},{1,9},{5,13},{9,1},{13,5},{2,10},{6,14},... | collective-permute-start | bytes 786440 | tf_op jit(solution)/shard_map/L_q2/ppermute | solution.py:34
  71.7 22.9 %collective-permute-start.11 = (bf16[512,256]{1,0:T(8,128)(2,1)S(1)}, bf16[512,256]{1,0:T(8,128)(2,1)S(1)}, u32[]{:S(2)}, u32[]{:S(2)}) collective-permute-start(bf16[512,256]{1,0:T(8,128)(2,1)S(1)} %copy-done.8), channel_id=1, source_target_pairs={{0,12},{4,8},{8,4},{12,0},{1,13},{5,9},{9,5},{13,1},{2,14},{6,10},... | collective-permute-start | bytes 786440 | tf_op jit(solution)/shard_map/L_q3/ppermute | solution.py:34
  87.9 16.6 %collective-permute-start.17 = (bf16[512,1024]{1,0:T(8,128)(2,1)}, bf16[512,1024]{1,0:T(8,128)(2,1)}, u32[]{:S(2)}, u32[]{:S(2)}) collective-permute-start(bf16[512,1024]{1,0:T(8,128)(2,1)} %collective-permute-done.4.refs_6_), channel_id=1, source_target_pairs={{0,1},{1,0},{2,3},{3,2},{4,5},{5,4},{6,7},{7,6},{8,9},{9,8},{10,11... | collective-permute-start | bytes 3145736 | tf_op jit(solution)/shard_map/L_B1c1/ppermute | solution.py:34
  94.5 0.7 copy-start.2
  94.5 4.4 %collective-permute-start.18 = (bf16[256,1024]{1,0:T(8,128)(2,1)}, bf16[256,1024]{1,0:T(8,128)(2,1)}, u32[]{:S(2)}, u32[]{:S(2)}) collective-permute-start(bf16[256,1024]{1,0:T(8,128)(2,1)} %compress.1.refs_7_), channel_id=1, source_target_pairs={{0,1},{1,0},{2,3},{3,2},{4,5},{5,4},{6,7},{7,6},{8,9},{9,8},{10,11... | collective-permute-start | bytes 1572872 | tf_op jit(solution)/shard_map/L_C0c1/ppermute | solution.py:34
  95.2 1.0 copy-start.5
  96.2 2.8 %collective-permute-start.19 = (bf16[256,1024]{1,0:T(8,128)(2,1)}, bf16[256,1024]{1,0:T(8,128)(2,1)}, u32[]{:S(2)}, u32[]{:S(2)}) collective-permute-start(bf16[256,1024]{1,0:T(8,128)(2,1)} %collective-permute-done.14.refs_9_), channel_id=1, source_target_pairs={{0,1},{1,0},{2,3},{3,2},{4,5},{5,4},{6,7},{7,6},{8,9},{9,8},{10,11... | collective-permute-start | bytes 1572872 | tf_op jit(solution)/shard_map/L_C1c1/ppermute | solution.py:34
  96.9 7.7 %copy-start = (bf16[512,1024]{1,0:T(8,128)(2,1)S(1)}, bf16[512,1024]{1,0:T(8,128)(2,1)}, u32[]{:S(2)}) copy-start(bf16[512,1024]{1,0:T(8,128)(2,1)} %refs_0_.4) | copy-start | bytes 3145732
  96.9 13.5 %collective-permute-start.15 = (bf16[512,256]{1,0:T(8,128)(2,1)S(1)}, bf16[512,256]{1,0:T(8,128)(2,1)S(1)}, u32[]{:S(2)}, u32[]{:S(2)}) collective-permute-start(bf16[512,256]{1,0:T(8,128)(2,1)S(1)} %collective-permute-done.10.refs_3_), channel_id=1, source_target_pairs={{0,16},{16,0},{1,17},{17,1},{2,18},{18,2},{3,19},{19,3},{4,20},{20... | collective-permute-start | bytes 786440 | tf_op jit(solution)/shard_map/L_yq2/ppermute | solution.py:34
  97.8 13.4 %collective-permute-start.16 = (bf16[512,256]{1,0:T(8,128)(2,1)}, bf16[512,256]{1,0:T(8,128)(2,1)S(1)}, u32[]{:S(2)}, u32[]{:S(2)}) collective-permute-start(bf16[512,256]{1,0:T(8,128)(2,1)} %copy-done.2), channel_id=1, source_target_pairs={{0,16},{16,0},{1,17},{17,1},{2,18},{18,2},{3,19},{19,3},{4,20},{20... | collective-permute-start | bytes 786440 | tf_op jit(solution)/shard_map/L_yq3/ppermute | solution.py:34
  102.5 14.7 %collective-permute-start.20 = (bf16[256,512]{1,0:T(8,128)(2,1)S(1)}, bf16[256,512]{1,0:T(8,128)(2,1)S(1)}, u32[]{:S(2)}, u32[]{:S(2)}) collective-permute-start(bf16[256,512]{1,0:T(8,128)(2,1)S(1)} %get-tuple-element.90.refs_0_), channel_id=1, source_target_pairs={{0,8},{4,12},{8,0},{12,4},{1,9},{5,13},{9,1},{13,5},{2,10},{6,14},... | collective-permute-start | bytes 786440 | tf_op jit(solution)/shard_map/L_m2/ppermute | solution.py:34
  104.5 6.7 %copy-start.1 = (bf16[1024,512]{1,0:T(8,128)(2,1)S(1)}, bf16[1024,512]{1,0:T(8,128)(2,1)}, u32[]{:S(2)}) copy-start(bf16[1024,512]{1,0:T(8,128)(2,1)} %refs_1_.3) | copy-start | bytes 3145732
  104.5 6.7 %copy-start.3 = (bf16[512,256]{1,0:T(8,128)(2,1)S(1)}, bf16[512,256]{1,0:T(8,128)(2,1)}, u32[]{:S(2)}) copy-start(bf16[512,256]{1,0:T(8,128)(2,1)} %copy-done.2) | copy-start | bytes 786436
  104.5 6.7 %copy-start.4 = (s32[8]{0:T(128)S(1)}, s32[8]{0:T(128)}, u32[]{:S(2)}) copy-start(s32[8]{0:T(128)} %segments.3) | copy-start | bytes 100
  119.8 7.8 %collective-permute-start.21 = (bf16[512,256]{1,0:T(8,128)(2,1)S(1)}, bf16[512,256]{1,0:T(8,128)(2,1)S(1)}, u32[]{:S(2)}, u32[]{:S(2)}) collective-permute-start(bf16[512,256]{1,0:T(8,128)(2,1)S(1)} %attend.2), channel_id=1, source_target_pairs={{0,4},{4,0},{8,12},{12,8},{1,5},{5,1},{9,13},{13,9},{2,6},{6,2},{1... | collective-permute-start | bytes 786440 | tf_op jit(solution)/shard_map/L_ctx/ppermute | solution.py:34

commit v5 on v4

--- a/solution.py
+++ b/solution.py
@@ -389,7 +389,7 @@
     fresh = []
     every = range(1, planes)
     first = [2] if planes > 2 else []
-    second = [d for d in every if d not in first]
+    second = [d for d in every[::-1] if d not in first]
     stage(
         {"Xz": (activations, "seq", 1)}
         | across(activations, "A")
@@ -397,9 +397,7 @@
         | distant(first, "kv")
     )
     partner = got["Xz"]
-    sends = across(partner, "B") | within(partner, "B0") | distant(second, "kv") | relayed(first, "kv")
-    for k in range(1, tensor_size):
-        sends |= within(got[f"Ax{k}"], f"A{k}")
+    sends = across(partner, "B") | distant(second, "kv") | relayed(first, "kv")
     (both,) = stage(sends, compress(activations, partner, conv_weight))
     far_planes = range(2, planes)
     second_kv = jnp.concatenate([got[f"kv{d}"] for d in second], axis=0)
@@ -408,8 +406,8 @@
         | {"q1": (q_whole, "seq", 1), "ykv": (second_kv, "groups", 1)}
         | across(both, "C")
     )
-    sends = within(both, "C0") | relayed(far_planes, "q")
-    for label in ("C", "B"):
+    sends = within(both, "C0") | within(partner, "B0") | relayed(far_planes, "q")
+    for label in ("C", "B", "A"):
         for k in range(1, tensor_size):
             sends |= within(got[f"{label}x{k}"], f"{label}{k}")
     before = tuple(got[key] for key in fresh)

time: 128 us -> 127 us (level)
  transfers between devices with their start and end apart: 22 -> 22, of which waited for: 9 -> 10; matrix products, arithmetic and copies ran while one was open for 0% -> 0% of each run, Pallas kernels for 21% -> 21%
where the time goes in v5:
time: 127 us; the launch traced here: 126 us
  waiting for transfers between devices  68.5 us (54%)
  Pallas kernels  29.1 us (23%)
  starting transfers between devices  26.1 us (21%)
  local copies, waits for them, and re-layouts  1.72 us (1%)
    ppermute x22, waiting for transfers between devices, swap(): return lax.ppermute(value, axis, [(i, i ^ distance) for i in range(size)])  68.5 us
    ppermute x22, starting transfers between devices, swap(): return lax.ppermute(value, axis, [(i, i ^ distance) for i in range(size)])  26.1 us
    pallas_call x2, Pallas kernels, attend_local(): pl.pallas_call(functools.partial(local_kernel, side, planes, tensor_size,...  6.59 us
    pallas_call x1, Pallas kernels, project_tokens(): pl.pallas_call(functools.partial(tokens_kernel, tensor_size, sub_size), o...  5.84 us
    pallas_call x2, Pallas kernels, attend(): pl.pallas_call(functools.partial(far_kernel, side, planes), out_shape=jax...  5.75 us
    pallas_call x1, Pallas kernels, compress(): pl.pallas_call(compress_kernel, out_shape=jax.ShapeDtypeStruct((2 * count...  4.51 us
    pallas_call x1, Pallas kernels, project_memory(): pl.pallas_call(functools.partial(memory_kernel, planes, tensor_size, sub_...  3.54 us
    pallas_call x1, Pallas kernels, split_weights(): pl.pallas_call(split_kernel, out_shape=[jax.ShapeDtypeStruct(s, BF) for s...  2.91 us
  transfers between devices with their start and end apart: 22, of which 10 were waited for; matrix products, arithmetic and copies ran while one was open for 0% of the time, Pallas kernels for 21%

profile of v5, /device:TPU:0, one launch (start us, length us, event | category | flops | bytes accessed | tf_op | source)
XLA Modules:
  0.0 126.4 jit_solution(9804482101615371681)
XLA Ops:
  0.0 3.0 %collective-permute-start = (bf16[512,1024]{1,0:T(8,128)(2,1)}, bf16[512,1024]{1,0:T(8,128)(2,1)}, u32[]{:S(2)}, u32[]{:S(2)}) collective-permute-start(bf16[512,1024]{1,0:T(8,128)(2,1)} %refs_0_.4), channel_id=1, source_target_pairs={{0,4},{4,0},{8,12},{12,8},{1,5},{5,1},{9,13},{13,9},{2,6},{6,2},{1... | collective-permute-start | bytes 3145736 | tf_op jit(solution)/shard_map/L_Xz/ppermute | solution.py:34
  3.0 1.5 %collective-permute-start.1 = (bf16[512,1024]{1,0:T(8,128)(2,1)}, bf16[512,1024]{1,0:T(8,128)(2,1)}, u32[]{:S(2)}, u32[]{:S(2)}) collective-permute-start(bf16[512,1024]{1,0:T(8,128)(2,1)} %refs_0_.4), channel_id=1, source_target_pairs={{0,2},{2,0},{1,3},{3,1},{4,6},{6,4},{5,7},{7,5},{8,10},{10,8},{9,1... | collective-permute-start | bytes 3145736 | tf_op jit(solution)/shard_map/L_Ax1/ppermute | solution.py:34
  4.5 0.0 collective-permute-start.2
  4.5 2.9 %split_weights.1 = (bf16[512,512]{1,0:T(8,128)(2,1)}, bf16[512,512]{1,0:T(8,128)(2,1)}, bf16[512,256]{1,0:T(8,128)(2,1)}, bf16[512,256]{1,0:T(8,128)(2,1)}, bf16[1024,256]{1,0:T(8,128)(2,1)}) custom-call(bf16[1024,512]{1,0:T(8,128)(2,1)} %refs_0_.3, bf16[1024,512]{1,0:T(8,128)(2,1)} %refs_1_.2, bf16[1024,512]{1,0:T(8,128)(2,1)} %refs_1_.3), custom_call_target="tpu_custom_call" | custom-call | flops 2000000000 | bytes 1000 | tf_op jit(solution)/shard_map/split_weights/pallas_call | solution.py:74
  7.4 2.7 %collective-permute-start.3 = (bf16[512,512]{1,0:T(8,128)(2,1)}, bf16[512,512]{1,0:T(8,128)(2,1)S(1)}, u32[]{:S(2)}, u32[]{:S(2)}) collective-permute-start(bf16[512,512]{1,0:T(8,128)(2,1)} %get-tuple-element.49), channel_id=1, source_target_pairs={{0,8},{4,12},{8,0},{12,4},{1,9},{5,13},{9,1},{13,5},{2,10},{6,14},... | collective-permute-start | bytes 1572872 | tf_op jit(solution)/shard_map/L_kv2/ppermute | solution.py:34
  10.1 26.9 %collective-permute-done.3.refs_3_ = bf16[512,512]{1,0:T(8,128)(2,1)S(1)} collective-permute-done((bf16[512,512]{1,0:T(8,128)(2,1)}, bf16[512,512]{1,0:T(8,128)(2,1)S(1)}, u32[]{:S(2)}, u32[]{:S(2)}) %collective-permute-start.3) | collective-permute-done | bytes 524320 | tf_op jit(solution)/shard_map/L_kv2/ppermute | solution.py:34
  37.0 0.7 collective-permute-done.partner_ref.refs_4_
  37.7 0.0 collective-permute-done.1.refs_2_
  37.7 0.0 collective-permute-done.2.refs_1_
  37.7 1.7 %collective-permute-start.4 = (bf16[512,1024]{1,0:T(8,128)(2,1)}, bf16[512,1024]{1,0:T(8,128)(2,1)}, u32[]{:S(2)}, u32[]{:S(2)}) collective-permute-start(bf16[512,1024]{1,0:T(8,128)(2,1)} %collective-permute-done.partner_ref.refs_4_), channel_id=1, source_target_pairs={{0,2},{2,0},{1,3},{3,1},{4,6},{6,4},{5,7},{7,5},{8,10},{10,8},{9,1... | collective-permute-start | bytes 3145736 | tf_op jit(solution)/shard_map/L_Bx1/ppermute | solution.py:34
  39.4 3.6 %collective-permute-start.5 = (bf16[512,512]{1,0:T(8,128)(2,1)}, bf16[512,512]{1,0:T(8,128)(2,1)S(1)}, u32[]{:S(2)}, u32[]{:S(2)}) collective-permute-start(bf16[512,512]{1,0:T(8,128)(2,1)} %get-tuple-element.56), channel_id=1, source_target_pairs={{0,12},{4,8},{8,4},{12,0},{1,13},{5,9},{9,5},{13,1},{2,14},{6,10},... | collective-permute-start | bytes 1572872 | tf_op jit(solution)/shard_map/L_kv3/ppermute | solution.py:34
  43.0 0.0 collective-permute-start.6
  43.0 1.5 %collective-permute-start.7 = (bf16[512,512]{1,0:T(8,128)(2,1)S(1)}, bf16[512,512]{1,0:T(8,128)(2,1)S(1)}, u32[]{:S(2)}, u32[]{:S(2)}) collective-permute-start(bf16[512,512]{1,0:T(8,128)(2,1)S(1)} %collective-permute-done.3.refs_3_), channel_id=1, source_target_pairs={{0,16},{16,0},{1,17},{17,1},{2,18},{18,2},{3,19},{19,3},{4,20},{20... | collective-permute-start | bytes 1572872 | tf_op jit(solution)/shard_map/L_ykv2/ppermute | solution.py:34
  44.5 4.5 %compress.1.refs_7_ = bf16[256,1024]{1,0:T(8,128)(2,1)} custom-call(bf16[512,1024]{1,0:T(8,128)(2,1)} %refs_0_.4, bf16[512,1024]{1,0:T(8,128)(2,1)} %collective-permute-done.partner_ref.refs_4_, bf16[512,1024]{1,0:T(8,128)(2,1)} %w_ref.1), custom_call_target="tpu_custom_call" | custom-call | flops 5000000000 | bytes 1000 | tf_op jit(solution)/shard_map/compress/pallas_call | solution.py:106
  49.0 7.3 %collective-permute-done.5.refs_4_ = bf16[512,512]{1,0:T(8,128)(2,1)S(1)} collective-permute-done((bf16[512,512]{1,0:T(8,128)(2,1)}, bf16[512,512]{1,0:T(8,128)(2,1)S(1)}, u32[]{:S(2)}, u32[]{:S(2)}) %collective-permute-start.5) | collective-permute-done | bytes 524320 | tf_op jit(solution)/shard_map/L_kv3/ppermute | solution.py:34
  56.3 9.0 %collective-permute-done.6.refs_2_ = bf16[512,512]{1,0:T(8,128)(2,1)S(1)} collective-permute-done((bf16[512,512]{1,0:T(8,128)(2,1)}, bf16[512,512]{1,0:T(8,128)(2,1)S(1)}, u32[]{:S(2)}, u32[]{:S(2)}) %collective-permute-start.6) | collective-permute-done | bytes 524320 | tf_op jit(solution)/shard_map/L_kv1/ppermute | solution.py:34
  65.3 0.0 collective-permute-done.7.refs_5_
  65.3 0.0 collective-permute-done.4.refs_6_
  65.3 0.1 pad_maximum_fusion
  65.4 1.6 %collective-permute-start.11 = (bf16[1024,512]{1,0:T(8,128)(2,1)S(1)}, bf16[1024,512]{1,0:T(8,128)(2,1)S(1)}, u32[]{:S(2)}, u32[]{:S(2)}) collective-permute-start(bf16[1024,512]{1,0:T(8,128)(2,1)S(1)} %pad_maximum_fusion), channel_id=1, source_target_pairs={{0,16},{16,0},{1,17},{17,1},{2,18},{18,2},{3,19},{19,3},{4,20},{20... | collective-permute-start | bytes 3145736 | tf_op jit(solution)/shard_map/L_ykv/ppermute | solution.py:34
  67.0 0.0 copy-done.6
  67.0 0.0 copy-done.7
  67.0 1.7 %collective-permute-start.10 = (bf16[1024,256]{1,0:T(8,128)(2,1)S(1)}, bf16[1024,256]{1,0:T(8,128)(2,1)S(1)}, u32[]{:S(2)}, u32[]{:S(2)}) collective-permute-start(bf16[1024,256]{1,0:T(8,128)(2,1)S(1)} %copy-done.7), channel_id=1, source_target_pairs={{0,4},{4,0},{8,12},{12,8},{1,5},{5,1},{9,13},{13,9},{2,6},{6,2},{1... | collective-permute-start | bytes 1572872 | tf_op jit(solution)/shard_map/L_q1/ppermute | solution.py:34
  68.7 0.5 collective-permute-start.12
  69.2 0.0 copy-done.9
  69.2 0.5 collective-permute-start.8
  69.7 0.0 copy-done.8
  69.7 2.2 %collective-permute-start.9 = (bf16[512,256]{1,0:T(8,128)(2,1)S(1)}, bf16[512,256]{1,0:T(8,128)(2,1)S(1)}, u32[]{:S(2)}, u32[]{:S(2)}) collective-permute-start(bf16[512,256]{1,0:T(8,128)(2,1)S(1)} %copy-done.8), channel_id=1, source_target_pairs={{0,12},{4,8},{8,4},{12,0},{1,13},{5,9},{9,5},{13,1},{2,14},{6,10},... | collective-permute-start | bytes 786440 | tf_op jit(solution)/shard_map/L_q3/ppermute | solution.py:34
  71.9 14.8 %collective-permute-done.8.refs_3_ = bf16[512,256]{1,0:T(8,128)(2,1)S(1)} collective-permute-done((bf16[512,256]{1,0:T(8,128)(2,1)S(1)}, bf16[512,256]{1,0:T(8,128)(2,1)S(1)}, u32[]{:S(2)}, u32[]{:S(2)}) %collective-permute-start.8) | collective-permute-done | bytes 262176 | tf_op jit(solution)/shard_map/L_q2/ppermute | solution.py:34
  86.7 0.0 collective-permute-start.15
  86.7 4.3 %collective-permute-done.9.refs_4_ = bf16[512,256]{1,0:T(8,128)(2,1)S(1)} collective-permute-done((bf16[512,256]{1,0:T(8,128)(2,1)S(1)}, bf16[512,256]{1,0:T(8,128)(2,1)S(1)}, u32[]{:S(2)}, u32[]{:S(2)}) %collective-permute-start.9) | collective-permute-done | bytes 262176 | tf_op jit(solution)/shard_map/L_q3/ppermute | solution.py:34
  91.0 0.0 collective-permute-start.16
  91.0 0.8 collective-permute-done.10.refs_2_
  91.8 0.0 copy-done.2
  91.8 0.0 collective-permute-start.17
  91.8 0.0 collective-permute-done.12.refs_9_
  91.8 0.5 collective-permute-start.18
  92.3 0.0 collective-permute-done.11.refs_6_
  92.3 1.0 copy-done.5
  93.3 0.1 collective-permute-start.19
  94.0 0.0 copy-start
  94.0 2.2 %collective-permute-done.18.refs_8_ = bf16[256,1024]{1,0:T(8,128)(2,1)} collective-permute-done((bf16[256,1024]{1,0:T(8,128)(2,1)}, bf16[256,1024]{1,0:T(8,128)(2,1)}, u32[]{:S(2)}, u32[]{:S(2)}) %collective-permute-start.18) | collective-permute-done | bytes 524320 | tf_op jit(solution)/shard_map/L_C0c1/ppermute | solution.py:34
  96.2 0.9 collective-permute-start.13
  97.2 0.0 collective-permute-done.19.refs_10_
  97.2 1.1 collective-permute-start.14
  98.3 3.5 %project_memory.1 = (bf16[256,512]{1,0:T(8,128)(2,1)S(1)}, bf16[4096,512]{1,0:T(8,128)(2,1)S(1)}) custom-call(bf16[1024,512]{1,0:T(8,128)(2,1)} %refs_0_.3, bf16[1024,512]{1,0:T(8,128)(2,1)} %refs_1_.2, bf16[512,512]{1,0:T(8,128)(2,1)S(1)} %collective-permute-done.6.refs_2_, bf16[512,512]{1,0:T(8,128)(2,1)S(1)} %collective-permute-done.3.refs_3_, ...), custom_call_target="tpu_custom_call" | custom-call | flops 4000000000 | bytes 1000 | tf_op jit(solution)/shard_map/project_memory/pallas_call | solution.py:178
  101.8 0.0 collective-permute-done.15.refs_3_
  101.8 2.6 %collective-permute-start.20 = (bf16[256,512]{1,0:T(8,128)(2,1)S(1)}, bf16[256,512]{1,0:T(8,128)(2,1)S(1)}, u32[]{:S(2)}, u32[]{:S(2)}) collective-permute-start(bf16[256,512]{1,0:T(8,128)(2,1)S(1)} %get-tuple-element.84.refs_0_), channel_id=1, source_target_pairs={{0,8},{4,12},{8,0},{12,4},{1,9},{5,13},{9,1},{13,5},{2,10},{6,14},... | collective-permute-start | bytes 786440 | tf_op jit(solution)/shard_map/L_m2/ppermute | solution.py:34
  104.5 0.0 collective-permute-done.16.refs_5_
  104.5 0.0 collective-permute-done.17.refs_7_
  104.5 0.0 copy-done
  104.5 0.0 copy-start.1
  104.5 0.0 copy-start.4
  104.5 5.8 %project_tokens.1 = (bf16[1024,512]{1,0:T(8,128)(2,1)S(1)}, bf16[4,1024,1024]{2,1,0:T(8,128)(2,1)S(1)}) custom-call(bf16[512,1024]{1,0:T(8,128)(2,1)S(1)} %copy-done, bf16[512,1024]{1,0:T(8,128)(2,1)S(1)} %collective-permute-done.2.refs_1_, bf16[512,1024]{1,0:T(8,128)(2,1)} %collective-permute-done.1.refs_2_, ...), custom_call_target="tpu_custom_call" | custom-call | flops 6000000000 | bytes 1000 | tf_op jit(solution)/shard_map/project_tokens/pallas_call | solution.py:222
  110.4 0.0 collective-permute-done.13.refs_5_
  110.4 0.0 collective-permute-done.14.refs_6_
  110.4 3.4 %attend_local.2 = (bf16[512,256]{1,0:T(8,128)(2,1)S(1)}, f32[512,256]{1,0:T(8,128)S(1)}, f32[512,256]{1,0:T(8,128)S(1)}, f32[512,256]{1,0:T(8,128)S(1)}, bf16[4096,256]{1,0:T(8,128)(2,1)S(1)}) custom-call(s32[8]{0:T(128)S(1)} %copy-done.4, bf16[1024,512]{1,0:T(8,128)(2,1)S(1)} %copy-done.1, bf16[1024,256]{1,0:T(8,128)(2,1)S(1)} %collective-permute-done.10.refs_2_, ...), custom_call_target="tpu_custom_call" | custom-call | flops 4000000000 | bytes 1000 | tf_op jit(solution)/shard_map/attend_local/pallas_call | solution.py:279
  113.8 2.4 %collective-permute-done.20.refs_1_ = bf16[256,512]{1,0:T(8,128)(2,1)S(1)} collective-permute-done((bf16[256,512]{1,0:T(8,128)(2,1)S(1)}, bf16[256,512]{1,0:T(8,128)(2,1)S(1)}, u32[]{:S(2)}, u32[]{:S(2)}) %collective-permute-start.20) | collective-permute-done | bytes 262176 | tf_op jit(solution)/shard_map/L_m2/ppermute | solution.py:34
  116.2 2.5 %attend.2 = bf16[512,256]{1,0:T(8,128)(2,1)S(1)} custom-call(s32[8]{0:T(128)S(1)} %copy-done.4, s32[1]{0:T(128)S(6)} %copy.9.length, bf16[512,256]{1,0:T(8,128)(2,1)S(1)} %get-tuple-element.80.queries, f32[512,256]{1,0:T(8,128)S(1)} %get-tuple-element.81.sums, f32[512,256]{1,0:T(8,128)S(1)} %get-tuple-element.82.largest, ...), custom_call_target="tpu_custom_call" | custom-call | flops 4000000000 | bytes 1000 | tf_op jit(solution)/shard_map/attend/pallas_call | solution.py:340
  118.7 0.4 collective-permute-start.21
  119.2 3.2 %attend_local.3 = (bf16[512,256]{1,0:T(8,128)(2,1)S(1)}, f32[512,256]{1,0:T(8,128)S(1)}, f32[512,256]{1,0:T(8,128)S(1)}, f32[512,256]{1,0:T(8,128)S(1)}) custom-call(s32[8]{0:T(128)S(1)} %copy-done.4, bf16[4096,256]{1,0:T(8,128)(2,1)S(1)} %get-tuple-element.86.refs_1_, bf16[4,1024,1024]{2,1,0:T(8,128)(2,1)S(1)} %get-tuple-element.78.refs_7_.refs_2_, ...), custom_call_target="tpu_custom_call" | custom-call | flops 4000000000 | bytes 1000 | tf_op jit(solution)/shard_map/attend_local/pallas_call | solution.py:279
  122.4 3.2 %attend.3 = bf16[512,512]{1,0:T(8,128)(2,1)} custom-call(s32[8]{0:T(128)S(1)} %copy-done.4, s32[1]{0:T(128)S(6)} %copy.9.length, bf16[512,256]{1,0:T(8,128)(2,1)S(1)} %get-tuple-element.87.queries, f32[512,256]{1,0:T(8,128)S(1)} %get-tuple-element.88.sums, f32[512,256]{1,0:T(8,128)S(1)} %get-tuple-element.89.largest, ...), custom_call_target="tpu_custom_call" | custom-call | flops 4000000000 | bytes 1000 | tf_op jit(solution)/shard_map/attend/pallas_call | solution.py:340
  125.6 0.1 collective-permute-done.21
  125.7 0.7 constant_dynamic-update-slice_fusion
  (10 shorter events, 0.0 us)
Async XLA Ops:
  0.0 37.7 %collective-permute-start = (bf16[512,1024]{1,0:T(8,128)(2,1)}, bf16[512,1024]{1,0:T(8,128)(2,1)}, u32[]{:S(2)}, u32[]{:S(2)}) collective-permute-start(bf16[512,1024]{1,0:T(8,128)(2,1)} %refs_0_.4), channel_id=1, source_target_pairs={{0,4},{4,0},{8,12},{12,8},{1,5},{5,1},{9,13},{13,9},{2,6},{6,2},{1... | collective-permute-start | bytes 3145736 | tf_op jit(solution)/shard_map/L_Xz/ppermute | solution.py:34
  3.0 34.7 %collective-permute-start.1 = (bf16[512,1024]{1,0:T(8,128)(2,1)}, bf16[512,1024]{1,0:T(8,128)(2,1)}, u32[]{:S(2)}, u32[]{:S(2)}) collective-permute-start(bf16[512,1024]{1,0:T(8,128)(2,1)} %refs_0_.4), channel_id=1, source_target_pairs={{0,2},{2,0},{1,3},{3,1},{4,6},{6,4},{5,7},{7,5},{8,10},{10,8},{9,1... | collective-permute-start | bytes 3145736 | tf_op jit(solution)/shard_map/L_Ax1/ppermute | solution.py:34
  4.5 33.2 %collective-permute-start.2 = (bf16[512,1024]{1,0:T(8,128)(2,1)}, bf16[512,1024]{1,0:T(8,128)(2,1)S(1)}, u32[]{:S(2)}, u32[]{:S(2)}) collective-permute-start(bf16[512,1024]{1,0:T(8,128)(2,1)} %refs_0_.4), channel_id=1, source_target_pairs={{0,1},{1,0},{2,3},{3,2},{4,5},{5,4},{6,7},{7,6},{8,9},{9,8},{10,11... | collective-permute-start | bytes 3145736 | tf_op jit(solution)/shard_map/L_A0c1/ppermute | solution.py:34
  7.4 29.6 %collective-permute-start.3 = (bf16[512,512]{1,0:T(8,128)(2,1)}, bf16[512,512]{1,0:T(8,128)(2,1)S(1)}, u32[]{:S(2)}, u32[]{:S(2)}) collective-permute-start(bf16[512,512]{1,0:T(8,128)(2,1)} %get-tuple-element.49), channel_id=1, source_target_pairs={{0,8},{4,12},{8,0},{12,4},{1,9},{5,13},{9,1},{13,5},{2,10},{6,14},... | collective-permute-start | bytes 1572872 | tf_op jit(solution)/shard_map/L_kv2/ppermute | solution.py:34
  37.7 27.6 %collective-permute-start.4 = (bf16[512,1024]{1,0:T(8,128)(2,1)}, bf16[512,1024]{1,0:T(8,128)(2,1)}, u32[]{:S(2)}, u32[]{:S(2)}) collective-permute-start(bf16[512,1024]{1,0:T(8,128)(2,1)} %collective-permute-done.partner_ref.refs_4_), channel_id=1, source_target_pairs={{0,2},{2,0},{1,3},{3,1},{4,6},{6,4},{5,7},{7,5},{8,10},{10,8},{9,1... | collective-permute-start | bytes 3145736 | tf_op jit(solution)/shard_map/L_Bx1/ppermute | solution.py:34
  39.4 16.9 %collective-permute-start.5 = (bf16[512,512]{1,0:T(8,128)(2,1)}, bf16[512,512]{1,0:T(8,128)(2,1)S(1)}, u32[]{:S(2)}, u32[]{:S(2)}) collective-permute-start(bf16[512,512]{1,0:T(8,128)(2,1)} %get-tuple-element.56), channel_id=1, source_target_pairs={{0,12},{4,8},{8,4},{12,0},{1,13},{5,9},{9,5},{13,1},{2,14},{6,10},... | collective-permute-start | bytes 1572872 | tf_op jit(solution)/shard_map/L_kv3/ppermute | solution.py:34
  43.0 22.3 %collective-permute-start.6 = (bf16[512,512]{1,0:T(8,128)(2,1)}, bf16[512,512]{1,0:T(8,128)(2,1)S(1)}, u32[]{:S(2)}, u32[]{:S(2)}) collective-permute-start(bf16[512,512]{1,0:T(8,128)(2,1)} %get-tuple-element.56), channel_id=1, source_target_pairs={{0,4},{4,0},{8,12},{12,8},{1,5},{5,1},{9,13},{13,9},{2,6},{6,2},{1... | collective-permute-start | bytes 1572872 | tf_op jit(solution)/shard_map/L_kv1/ppermute | solution.py:34
  43.0 22.3 %collective-permute-start.7 = (bf16[512,512]{1,0:T(8,128)(2,1)S(1)}, bf16[512,512]{1,0:T(8,128)(2,1)S(1)}, u32[]{:S(2)}, u32[]{:S(2)}) collective-permute-start(bf16[512,512]{1,0:T(8,128)(2,1)S(1)} %collective-permute-done.3.refs_3_), channel_id=1, source_target_pairs={{0,16},{16,0},{1,17},{17,1},{2,18},{18,2},{3,19},{19,3},{4,20},{20... | collective-permute-start | bytes 1572872 | tf_op jit(solution)/shard_map/L_ykv2/ppermute | solution.py:34
  49.0 18.0 %copy-start.7 = (bf16[1024,256]{1,0:T(8,128)(2,1)S(1)}, bf16[1024,256]{1,0:T(8,128)(2,1)}, u32[]{:S(2)}) copy-start(bf16[1024,256]{1,0:T(8,128)(2,1)} %get-tuple-element.66) | copy-start | bytes 1572868
  49.0 20.2 %copy-start.9 = (bf16[512,256]{1,0:T(8,128)(2,1)S(1)}, bf16[512,256]{1,0:T(8,128)(2,1)}, u32[]{:S(2)}) copy-start(bf16[512,256]{1,0:T(8,128)(2,1)} %get-tuple-element.62) | copy-start | bytes 786436
  49.0 20.7 %copy-start.8 = (bf16[512,256]{1,0:T(8,128)(2,1)S(1)}, bf16[512,256]{1,0:T(8,128)(2,1)}, u32[]{:S(2)}) copy-start(bf16[512,256]{1,0:T(8,128)(2,1)} %get-tuple-element.64) | copy-start | bytes 786436
  65.3 1.7 %copy-start.6 = (bf16[512,512]{1,0:T(8,128)(2,1)}, bf16[512,512]{1,0:T(8,128)(2,1)S(1)}, u32[]{:S(2)}) copy-start(bf16[512,512]{1,0:T(8,128)(2,1)S(1)} %collective-permute-done.7.refs_5_) | copy-start | bytes 1572868
  65.4 26.9 %collective-permute-start.11 = (bf16[1024,512]{1,0:T(8,128)(2,1)S(1)}, bf16[1024,512]{1,0:T(8,128)(2,1)S(1)}, u32[]{:S(2)}, u32[]{:S(2)}) collective-permute-start(bf16[1024,512]{1,0:T(8,128)(2,1)S(1)} %pad_maximum_fusion), channel_id=1, source_target_pairs={{0,16},{16,0},{1,17},{17,1},{2,18},{18,2},{3,19},{19,3},{4,20},{20... | collective-permute-start | bytes 3145736 | tf_op jit(solution)/shard_map/L_ykv/ppermute | solution.py:34
  67.0 24.8 %collective-permute-start.10 = (bf16[1024,256]{1,0:T(8,128)(2,1)S(1)}, bf16[1024,256]{1,0:T(8,128)(2,1)S(1)}, u32[]{:S(2)}, u32[]{:S(2)}) collective-permute-start(bf16[1024,256]{1,0:T(8,128)(2,1)S(1)} %copy-done.7), channel_id=1, source_target_pairs={{0,4},{4,0},{8,12},{12,8},{1,5},{5,1},{9,13},{13,9},{2,6},{6,2},{1... | collective-permute-start | bytes 1572872 | tf_op jit(solution)/shard_map/L_q1/ppermute | solution.py:34
  68.7 23.1 %collective-permute-start.12 = (bf16[256,1024]{1,0:T(8,128)(2,1)}, bf16[256,1024]{1,0:T(8,128)(2,1)}, u32[]{:S(2)}, u32[]{:S(2)}) collective-permute-start(bf16[256,1024]{1,0:T(8,128)(2,1)} %compress.1.refs_7_), channel_id=1, source_target_pairs={{0,2},{2,0},{1,3},{3,1},{4,6},{6,4},{5,7},{7,5},{8,10},{10,8},{9,1... | collective-permute-start | bytes 1572872 | tf_op jit(solution)/shard_map/L_Cx1/ppermute | solution.py:34
  69.2 17.5 %collective-permute-start.8 = (bf16[512,256]{1,0:T(8,128)(2,1)S(1)}, bf16[512,256]{1,0:T(8,128)(2,1)S(1)}, u32[]{:S(2)}, u32[]{:S(2)}) collective-permute-start(bf16[512,256]{1,0:T(8,128)(2,1)S(1)} %copy-done.9), channel_id=1, source_target_pairs={{0,8},{4,12},{8,0},{12,4},{1,9},{5,13},{9,1},{13,5},{2,10},{6,14},... | collective-permute-start | bytes 786440 | tf_op jit(solution)/shard_map/L_q2/ppermute | solution.py:34
  69.7 21.2 %collective-permute-start.9 = (bf16[512,256]{1,0:T(8,128)(2,1)S(1)}, bf16[512,256]{1,0:T(8,128)(2,1)S(1)}, u32[]{:S(2)}, u32[]{:S(2)}) collective-permute-start(bf16[512,256]{1,0:T(8,128)(2,1)S(1)} %copy-done.8), channel_id=1, source_target_pairs={{0,12},{4,8},{8,4},{12,0},{1,13},{5,9},{9,5},{13,1},{2,14},{6,10},... | collective-permute-start | bytes 786440 | tf_op jit(solution)/shard_map/L_q3/ppermute | solution.py:34
  86.7 15.1 %collective-permute-start.15 = (bf16[512,1024]{1,0:T(8,128)(2,1)}, bf16[512,1024]{1,0:T(8,128)(2,1)}, u32[]{:S(2)}, u32[]{:S(2)}) collective-permute-start(bf16[512,1024]{1,0:T(8,128)(2,1)} %collective-permute-done.1.refs_2_), channel_id=1, source_target_pairs={{0,1},{1,0},{2,3},{3,2},{4,5},{5,4},{6,7},{7,6},{8,9},{9,8},{10,11... | collective-permute-start | bytes 3145736 | tf_op jit(solution)/shard_map/L_A1c1/ppermute | solution.py:34
  91.0 0.8 copy-start.2
  91.0 13.5 %collective-permute-start.16 = (bf16[512,1024]{1,0:T(8,128)(2,1)}, bf16[512,1024]{1,0:T(8,128)(2,1)}, u32[]{:S(2)}, u32[]{:S(2)}) collective-permute-start(bf16[512,1024]{1,0:T(8,128)(2,1)} %collective-permute-done.partner_ref.refs_4_), channel_id=1, source_target_pairs={{0,1},{1,0},{2,3},{3,2},{4,5},{5,4},{6,7},{7,6},{8,9},{9,8},{10,11... | collective-permute-start | bytes 3145736 | tf_op jit(solution)/shard_map/L_B0c1/ppermute | solution.py:34
  91.8 12.7 %collective-permute-start.17 = (bf16[512,1024]{1,0:T(8,128)(2,1)}, bf16[512,1024]{1,0:T(8,128)(2,1)}, u32[]{:S(2)}, u32[]{:S(2)}) collective-permute-start(bf16[512,1024]{1,0:T(8,128)(2,1)} %collective-permute-done.4.refs_6_), channel_id=1, source_target_pairs={{0,1},{1,0},{2,3},{3,2},{4,5},{5,4},{6,7},{7,6},{8,9},{9,8},{10,11... | collective-permute-start | bytes 3145736 | tf_op jit(solution)/shard_map/L_B1c1/ppermute | solution.py:34
  91.8 4.4 %collective-permute-start.18 = (bf16[256,1024]{1,0:T(8,128)(2,1)}, bf16[256,1024]{1,0:T(8,128)(2,1)}, u32[]{:S(2)}, u32[]{:S(2)}) collective-permute-start(bf16[256,1024]{1,0:T(8,128)(2,1)} %compress.1.refs_7_), channel_id=1, source_target_pairs={{0,1},{1,0},{2,3},{3,2},{4,5},{5,4},{6,7},{7,6},{8,9},{9,8},{10,11... | collective-permute-start | bytes 1572872 | tf_op jit(solution)/shard_map/L_C0c1/ppermute | solution.py:34
  92.3 1.0 copy-start.5
  93.3 3.9 %collective-permute-start.19 = (bf16[256,1024]{1,0:T(8,128)(2,1)}, bf16[256,1024]{1,0:T(8,128)(2,1)}, u32[]{:S(2)}, u32[]{:S(2)}) collective-permute-start(bf16[256,1024]{1,0:T(8,128)(2,1)} %collective-permute-done.12.refs_9_), channel_id=1, source_target_pairs={{0,1},{1,0},{2,3},{3,2},{4,5},{5,4},{6,7},{7,6},{8,9},{9,8},{10,11... | collective-permute-start | bytes 1572872 | tf_op jit(solution)/shard_map/L_C1c1/ppermute | solution.py:34
  94.0 10.5 %copy-start = (bf16[512,1024]{1,0:T(8,128)(2,1)S(1)}, bf16[512,1024]{1,0:T(8,128)(2,1)}, u32[]{:S(2)}) copy-start(bf16[512,1024]{1,0:T(8,128)(2,1)} %refs_0_.4) | copy-start | bytes 3145732
  96.2 14.1 %collective-permute-start.13 = (bf16[512,256]{1,0:T(8,128)(2,1)S(1)}, bf16[512,256]{1,0:T(8,128)(2,1)S(1)}, u32[]{:S(2)}, u32[]{:S(2)}) collective-permute-start(bf16[512,256]{1,0:T(8,128)(2,1)S(1)} %collective-permute-done.8.refs_3_), channel_id=1, source_target_pairs={{0,16},{16,0},{1,17},{17,1},{2,18},{18,2},{3,19},{19,3},{4,20},{20... | collective-permute-start | bytes 786440 | tf_op jit(solution)/shard_map/L_yq2/ppermute | solution.py:34
  97.2 13.2 %collective-permute-start.14 = (bf16[512,256]{1,0:T(8,128)(2,1)}, bf16[512,256]{1,0:T(8,128)(2,1)S(1)}, u32[]{:S(2)}, u32[]{:S(2)}) collective-permute-start(bf16[512,256]{1,0:T(8,128)(2,1)} %copy-done.2), channel_id=1, source_target_pairs={{0,16},{16,0},{1,17},{17,1},{2,18},{18,2},{3,19},{19,3},{4,20},{20... | collective-permute-start | bytes 786440 | tf_op jit(solution)/shard_map/L_yq3/ppermute | solution.py:34
  101.8 14.4 %collective-permute-start.20 = (bf16[256,512]{1,0:T(8,128)(2,1)S(1)}, bf16[256,512]{1,0:T(8,128)(2,1)S(1)}, u32[]{:S(2)}, u32[]{:S(2)}) collective-permute-start(bf16[256,512]{1,0:T(8,128)(2,1)S(1)} %get-tuple-element.84.refs_0_), channel_id=1, source_target_pairs={{0,8},{4,12},{8,0},{12,4},{1,9},{5,13},{9,1},{13,5},{2,10},{6,14},... | collective-permute-start | bytes 786440 | tf_op jit(solution)/shard_map/L_m2/ppermute | solution.py:34
  104.5 5.9 %copy-start.1 = (bf16[1024,512]{1,0:T(8,128)(2,1)S(1)}, bf16[1024,512]{1,0:T(8,128)(2,1)}, u32[]{:S(2)}) copy-start(bf16[1024,512]{1,0:T(8,128)(2,1)} %refs_1_.3) | copy-start | bytes 3145732
  104.5 5.9 %copy-start.3 = (bf16[512,256]{1,0:T(8,128)(2,1)S(1)}, bf16[512,256]{1,0:T(8,128)(2,1)}, u32[]{:S(2)}) copy-start(bf16[512,256]{1,0:T(8,128)(2,1)} %copy-done.2) | copy-start | bytes 786436
  104.5 5.9 %copy-start.4 = (s32[8]{0:T(128)S(1)}, s32[8]{0:T(128)}, u32[]{:S(2)}) copy-start(s32[8]{0:T(128)} %segments.3) | copy-start | bytes 100
  118.7 6.9 %collective-permute-start.21 = (bf16[512,256]{1,0:T(8,128)(2,1)S(1)}, bf16[512,256]{1,0:T(8,128)(2,1)S(1)}, u32[]{:S(2)}, u32[]{:S(2)}) collective-permute-start(bf16[512,256]{1,0:T(8,128)(2,1)S(1)} %attend.2), channel_id=1, source_target_pairs={{0,4},{4,0},{8,12},{12,8},{1,5},{5,1},{9,13},{13,9},{2,6},{6,2},{1... | collective-permute-start | bytes 786440 | tf_op jit(solution)/shard_map/L_ctx/ppermute | solution.py:34

commit v6 on v5

--- a/solution.py
+++ b/solution.py
@@ -398,7 +398,10 @@
     )
     partner = got["Xz"]
     sends = across(partner, "B") | distant(second, "kv") | relayed(first, "kv")
-    (both,) = stage(sends, compress(activations, partner, conv_weight))
+    both = compress(activations, partner, conv_weight)
+    hops = {f"C0c{k}": swap(both, "sub", k, f"C0c{k}") for k in range(1, sub_size)}
+    both, *ended = stage(sends, both, *hops.values())
+    got.update(zip(hops, ended))
     far_planes = range(2, planes)
     second_kv = jnp.concatenate([got[f"kv{d}"] for d in second], axis=0)
     stage(
@@ -406,7 +409,7 @@
         | {"q1": (q_whole, "seq", 1), "ykv": (second_kv, "groups", 1)}
         | across(both, "C")
     )
-    sends = within(both, "C0") | within(partner, "B0") | relayed(far_planes, "q")
+    sends = within(partner, "B0") | relayed(far_planes, "q")
     for label in ("C", "B", "A"):
         for k in range(1, tensor_size):
             sends |= within(got[f"{label}x{k}"], f"{label}{k}")

time: 127 us -> 127 us (level)
  no operation moved by 1% of the time
where the time goes in v6:
time: 127 us; the launch traced here: 126 us
  waiting for transfers between devices  68.6 us (54%)
  Pallas kernels  29.1 us (23%)
  starting transfers between devices  25.2 us (20%)
  local copies, waits for them, and re-layouts  2.58 us (2%)
    ppermute x22, waiting for transfers between devices, swap(): return lax.ppermute(value, axis, [(i, i ^ distance) for i in range(size)])  68.6 us
    ppermute x22, starting transfers between devices, swap(): return lax.ppermute(value, axis, [(i, i ^ distance) for i in range(size)])  25.2 us
    pallas_call x2, Pallas kernels, attend_local(): pl.pallas_call(functools.partial(local_kernel, side, planes, tensor_size,...  6.56 us
    pallas_call x1, Pallas kernels, project_tokens(): pl.pallas_call(functools.partial(tokens_kernel, tensor_size, sub_size), o...  5.83 us
    pallas_call x2, Pallas kernels, attend(): pl.pallas_call(functools.partial(far_kernel, side, planes), out_shape=jax...  5.75 us
    pallas_call x1, Pallas kernels, compress(): pl.pallas_call(compress_kernel, out_shape=jax.ShapeDtypeStruct((2 * count...  4.52 us
    pallas_call x1, Pallas kernels, project_memory(): pl.pallas_call(functools.partial(memory_kernel, planes, tensor_size, sub_...  3.53 us
    pallas_call x1, Pallas kernels, split_weights(): pl.pallas_call(split_kernel, out_shape=[jax.ShapeDtypeStruct(s, BF) for s...  2.89 us
  transfers between devices with their start and end apart: 22, of which 10 were waited for; matrix products, arithmetic and copies ran while one was open for 0% of the time, Pallas kernels for 21%

profile of v6, /device:TPU:0, one launch (start us, length us, event | category | flops | bytes accessed | tf_op | source)
XLA Modules:
  0.0 126.4 jit_solution(2638918807965369590)
XLA Ops:
  0.0 3.0 %collective-permute-start = (bf16[512,1024]{1,0:T(8,128)(2,1)}, bf16[512,1024]{1,0:T(8,128)(2,1)}, u32[]{:S(2)}, u32[]{:S(2)}) collective-permute-start(bf16[512,1024]{1,0:T(8,128)(2,1)} %refs_0_.4), channel_id=1, source_target_pairs={{0,4},{4,0},{8,12},{12,8},{1,5},{5,1},{9,13},{13,9},{2,6},{6,2},{1... | collective-permute-start | bytes 3145736 | tf_op jit(solution)/shard_map/L_Xz/ppermute | solution.py:34
  3.0 1.5 %collective-permute-start.1 = (bf16[512,1024]{1,0:T(8,128)(2,1)}, bf16[512,1024]{1,0:T(8,128)(2,1)}, u32[]{:S(2)}, u32[]{:S(2)}) collective-permute-start(bf16[512,1024]{1,0:T(8,128)(2,1)} %refs_0_.4), channel_id=1, source_target_pairs={{0,2},{2,0},{1,3},{3,1},{4,6},{6,4},{5,7},{7,5},{8,10},{10,8},{9,1... | collective-permute-start | bytes 3145736 | tf_op jit(solution)/shard_map/L_Ax1/ppermute | solution.py:34
  4.5 0.0 collective-permute-start.2
  4.5 2.9 %split_weights.1 = (bf16[512,512]{1,0:T(8,128)(2,1)}, bf16[512,512]{1,0:T(8,128)(2,1)}, bf16[512,256]{1,0:T(8,128)(2,1)}, bf16[512,256]{1,0:T(8,128)(2,1)}, bf16[1024,256]{1,0:T(8,128)(2,1)}) custom-call(bf16[1024,512]{1,0:T(8,128)(2,1)} %refs_0_.3, bf16[1024,512]{1,0:T(8,128)(2,1)} %refs_1_.2, bf16[1024,512]{1,0:T(8,128)(2,1)} %refs_1_.3), custom_call_target="tpu_custom_call" | custom-call | flops 2000000000 | bytes 1000 | tf_op jit(solution)/shard_map/split_weights/pallas_call | solution.py:74
  7.4 2.7 %collective-permute-start.3 = (bf16[512,512]{1,0:T(8,128)(2,1)}, bf16[512,512]{1,0:T(8,128)(2,1)S(1)}, u32[]{:S(2)}, u32[]{:S(2)}) collective-permute-start(bf16[512,512]{1,0:T(8,128)(2,1)} %get-tuple-element.50), channel_id=1, source_target_pairs={{0,8},{4,12},{8,0},{12,4},{1,9},{5,13},{9,1},{13,5},{2,10},{6,14},... | collective-permute-start | bytes 1572872 | tf_op jit(solution)/shard_map/L_kv2/ppermute | solution.py:34
  10.1 26.9 %collective-permute-done.3.refs_3_ = bf16[512,512]{1,0:T(8,128)(2,1)S(1)} collective-permute-done((bf16[512,512]{1,0:T(8,128)(2,1)}, bf16[512,512]{1,0:T(8,128)(2,1)S(1)}, u32[]{:S(2)}, u32[]{:S(2)}) %collective-permute-start.3) | collective-permute-done | bytes 524320 | tf_op jit(solution)/shard_map/L_kv2/ppermute | solution.py:34
  37.0 0.7 collective-permute-done.partner_ref.refs_4_
  37.7 0.0 collective-permute-done.1.refs_2_
  37.7 0.0 collective-permute-done.2.refs_1_
  37.7 1.7 %collective-permute-start.4 = (bf16[512,1024]{1,0:T(8,128)(2,1)}, bf16[512,1024]{1,0:T(8,128)(2,1)}, u32[]{:S(2)}, u32[]{:S(2)}) collective-permute-start(bf16[512,1024]{1,0:T(8,128)(2,1)} %collective-permute-done.partner_ref.refs_4_), channel_id=1, source_target_pairs={{0,2},{2,0},{1,3},{3,1},{4,6},{6,4},{5,7},{7,5},{8,10},{10,8},{9,1... | collective-permute-start | bytes 3145736 | tf_op jit(solution)/shard_map/L_Bx1/ppermute | solution.py:34
  39.4 3.6 %collective-permute-start.5 = (bf16[512,512]{1,0:T(8,128)(2,1)}, bf16[512,512]{1,0:T(8,128)(2,1)S(1)}, u32[]{:S(2)}, u32[]{:S(2)}) collective-permute-start(bf16[512,512]{1,0:T(8,128)(2,1)} %get-tuple-element.57), channel_id=1, source_target_pairs={{0,12},{4,8},{8,4},{12,0},{1,13},{5,9},{9,5},{13,1},{2,14},{6,10},... | collective-permute-start | bytes 1572872 | tf_op jit(solution)/shard_map/L_kv3/ppermute | solution.py:34
  43.0 0.0 collective-permute-start.6
  43.0 1.5 %collective-permute-start.7 = (bf16[512,512]{1,0:T(8,128)(2,1)S(1)}, bf16[512,512]{1,0:T(8,128)(2,1)S(1)}, u32[]{:S(2)}, u32[]{:S(2)}) collective-permute-start(bf16[512,512]{1,0:T(8,128)(2,1)S(1)} %collective-permute-done.3.refs_3_), channel_id=1, source_target_pairs={{0,16},{16,0},{1,17},{17,1},{2,18},{18,2},{3,19},{19,3},{4,20},{20... | collective-permute-start | bytes 1572872 | tf_op jit(solution)/shard_map/L_ykv2/ppermute | solution.py:34
  44.5 4.5 %compress.1.refs_7_ = bf16[256,1024]{1,0:T(8,128)(2,1)} custom-call(bf16[512,1024]{1,0:T(8,128)(2,1)} %refs_0_.4, bf16[512,1024]{1,0:T(8,128)(2,1)} %collective-permute-done.partner_ref.refs_4_, bf16[512,1024]{1,0:T(8,128)(2,1)} %w_ref.1), custom_call_target="tpu_custom_call" | custom-call | flops 5000000000 | bytes 1000 | tf_op jit(solution)/shard_map/compress/pallas_call | solution.py:106
  49.1 0.1 collective-permute-start.8
  49.1 7.2 %collective-permute-done.5.refs_4_ = bf16[512,512]{1,0:T(8,128)(2,1)S(1)} collective-permute-done((bf16[512,512]{1,0:T(8,128)(2,1)}, bf16[512,512]{1,0:T(8,128)(2,1)S(1)}, u32[]{:S(2)}, u32[]{:S(2)}) %collective-permute-start.5) | collective-permute-done | bytes 524320 | tf_op jit(solution)/shard_map/L_kv3/ppermute | solution.py:34
  56.3 9.0 %collective-permute-done.6.refs_2_ = bf16[512,512]{1,0:T(8,128)(2,1)S(1)} collective-permute-done((bf16[512,512]{1,0:T(8,128)(2,1)}, bf16[512,512]{1,0:T(8,128)(2,1)S(1)}, u32[]{:S(2)}, u32[]{:S(2)}) %collective-permute-start.6) | collective-permute-done | bytes 524320 | tf_op jit(solution)/shard_map/L_kv1/ppermute | solution.py:34
  65.3 0.0 collective-permute-done.7.refs_5_
  65.3 0.0 collective-permute-done.8.refs_8_
  65.3 0.0 copy-start.8
  65.3 0.9 copy-done.8
  66.2 0.0 collective-permute-done.4.refs_6_
  66.2 0.1 pad_maximum_fusion
  66.3 1.6 %collective-permute-start.12 = (bf16[1024,512]{1,0:T(8,128)(2,1)S(1)}, bf16[1024,512]{1,0:T(8,128)(2,1)S(1)}, u32[]{:S(2)}, u32[]{:S(2)}) collective-permute-start(bf16[1024,512]{1,0:T(8,128)(2,1)S(1)} %pad_maximum_fusion), channel_id=1, source_target_pairs={{0,16},{16,0},{1,17},{17,1},{2,18},{18,2},{3,19},{19,3},{4,20},{20... | collective-permute-start | bytes 3145736 | tf_op jit(solution)/shard_map/L_ykv/ppermute | solution.py:34
  67.9 0.0 copy-done.9
  67.9 1.7 %collective-permute-start.11 = (bf16[1024,256]{1,0:T(8,128)(2,1)S(1)}, bf16[1024,256]{1,0:T(8,128)(2,1)S(1)}, u32[]{:S(2)}, u32[]{:S(2)}) collective-permute-start(bf16[1024,256]{1,0:T(8,128)(2,1)S(1)} %copy-done.9), channel_id=1, source_target_pairs={{0,4},{4,0},{8,12},{12,8},{1,5},{5,1},{9,13},{13,9},{2,6},{6,2},{1... | collective-permute-start | bytes 1572872 | tf_op jit(solution)/shard_map/L_q1/ppermute | solution.py:34
  69.6 0.5 collective-permute-start.13
  70.1 0.5 collective-permute-start.9
  70.6 2.2 %collective-permute-start.10 = (bf16[512,256]{1,0:T(8,128)(2,1)S(1)}, bf16[512,256]{1,0:T(8,128)(2,1)S(1)}, u32[]{:S(2)}, u32[]{:S(2)}) collective-permute-start(bf16[512,256]{1,0:T(8,128)(2,1)S(1)} %copy-done.10), channel_id=1, source_target_pairs={{0,12},{4,8},{8,4},{12,0},{1,13},{5,9},{9,5},{13,1},{2,14},{6,10},... | collective-permute-start | bytes 786440 | tf_op jit(solution)/shard_map/L_q3/ppermute | solution.py:34
  72.8 14.8 %collective-permute-done.9.refs_3_ = bf16[512,256]{1,0:T(8,128)(2,1)S(1)} collective-permute-done((bf16[512,256]{1,0:T(8,128)(2,1)S(1)}, bf16[512,256]{1,0:T(8,128)(2,1)S(1)}, u32[]{:S(2)}, u32[]{:S(2)}) %collective-permute-start.9) | collective-permute-done | bytes 262176 | tf_op jit(solution)/shard_map/L_q2/ppermute | solution.py:34
  87.6 0.0 collective-permute-start.16
  87.6 4.3 %collective-permute-done.10.refs_4_ = bf16[512,256]{1,0:T(8,128)(2,1)S(1)} collective-permute-done((bf16[512,256]{1,0:T(8,128)(2,1)S(1)}, bf16[512,256]{1,0:T(8,128)(2,1)S(1)}, u32[]{:S(2)}, u32[]{:S(2)}) %collective-permute-start.10) | collective-permute-done | bytes 262176 | tf_op jit(solution)/shard_map/L_q3/ppermute | solution.py:34
  91.9 0.0 collective-permute-start.17
  91.9 0.8 collective-permute-done.11.refs_2_
  92.7 0.0 collective-permute-start.18
  92.7 0.0 collective-permute-done.13.refs_9_
  92.7 0.0 collective-permute-done.12.refs_6_
  92.7 1.0 copy-done.5
  93.6 0.5 collective-permute-start.19
  94.8 0.0 copy-start
  94.8 0.6 collective-permute-start.14
  95.4 1.7 %collective-permute-done.19.refs_10_ = bf16[256,1024]{1,0:T(8,128)(2,1)} collective-permute-done((bf16[256,1024]{1,0:T(8,128)(2,1)}, bf16[256,1024]{1,0:T(8,128)(2,1)}, u32[]{:S(2)}, u32[]{:S(2)}) %collective-permute-start.19) | collective-permute-done | bytes 524320 | tf_op jit(solution)/shard_map/L_C1c1/ppermute | solution.py:34
  97.1 0.5 collective-permute-start.15
  97.6 3.5 %project_memory.1 = (bf16[256,512]{1,0:T(8,128)(2,1)S(1)}, bf16[4096,512]{1,0:T(8,128)(2,1)S(1)}) custom-call(bf16[1024,512]{1,0:T(8,128)(2,1)} %refs_0_.3, bf16[1024,512]{1,0:T(8,128)(2,1)} %refs_1_.2, bf16[512,512]{1,0:T(8,128)(2,1)S(1)} %collective-permute-done.6.refs_2_, bf16[512,512]{1,0:T(8,128)(2,1)S(1)} %collective-permute-done.3.refs_3_, ...), custom_call_target="tpu_custom_call" | custom-call | flops 4000000000 | bytes 1000 | tf_op jit(solution)/shard_map/project_memory/pallas_call | solution.py:178
  101.2 0.0 collective-permute-done.16.refs_3_
  101.2 2.7 %collective-permute-start.20 = (bf16[256,512]{1,0:T(8,128)(2,1)S(1)}, bf16[256,512]{1,0:T(8,128)(2,1)S(1)}, u32[]{:S(2)}, u32[]{:S(2)}) collective-permute-start(bf16[256,512]{1,0:T(8,128)(2,1)S(1)} %get-tuple-element.86.refs_0_), channel_id=1, source_target_pairs={{0,8},{4,12},{8,0},{12,4},{1,9},{5,13},{9,1},{13,5},{2,10},{6,14},... | collective-permute-start | bytes 786440 | tf_op jit(solution)/shard_map/L_m2/ppermute | solution.py:34
  103.9 0.0 collective-permute-done.17.refs_5_
  103.9 0.0 collective-permute-done.18.refs_7_
  103.9 0.0 copy-start.1
  103.9 0.0 copy-start.4
  103.9 5.8 %project_tokens.1 = (bf16[1024,512]{1,0:T(8,128)(2,1)S(1)}, bf16[4,1024,1024]{2,1,0:T(8,128)(2,1)S(1)}) custom-call(bf16[512,1024]{1,0:T(8,128)(2,1)S(1)} %copy-done, bf16[512,1024]{1,0:T(8,128)(2,1)S(1)} %collective-permute-done.2.refs_1_, bf16[512,1024]{1,0:T(8,128)(2,1)} %collective-permute-done.1.refs_2_, ...), custom_call_target="tpu_custom_call" | custom-call | flops 6000000000 | bytes 1000 | tf_op jit(solution)/shard_map/project_tokens/pallas_call | solution.py:222
  109.8 0.0 collective-permute-done.14.refs_5_
  109.8 0.0 collective-permute-done.15.refs_6_
  109.8 0.0 copy-done.1
  109.8 0.0 copy-done.3
  109.8 0.0 copy-done.4
  109.8 3.4 %attend_local.2 = (bf16[512,256]{1,0:T(8,128)(2,1)S(1)}, f32[512,256]{1,0:T(8,128)S(1)}, f32[512,256]{1,0:T(8,128)S(1)}, f32[512,256]{1,0:T(8,128)S(1)}, bf16[4096,256]{1,0:T(8,128)(2,1)S(1)}) custom-call(s32[8]{0:T(128)S(1)} %copy-done.4, bf16[1024,512]{1,0:T(8,128)(2,1)S(1)} %copy-done.1, bf16[1024,256]{1,0:T(8,128)(2,1)S(1)} %collective-permute-done.11.refs_2_, ...), custom_call_target="tpu_custom_call" | custom-call | flops 4000000000 | bytes 1000 | tf_op jit(solution)/shard_map/attend_local/pallas_call | solution.py:279
  113.2 2.6 %collective-permute-done.20.refs_1_ = bf16[256,512]{1,0:T(8,128)(2,1)S(1)} collective-permute-done((bf16[256,512]{1,0:T(8,128)(2,1)S(1)}, bf16[256,512]{1,0:T(8,128)(2,1)S(1)}, u32[]{:S(2)}, u32[]{:S(2)}) %collective-permute-start.20) | collective-permute-done | bytes 262176 | tf_op jit(solution)/shard_map/L_m2/ppermute | solution.py:34
  115.8 2.5 %attend.2 = bf16[512,256]{1,0:T(8,128)(2,1)S(1)} custom-call(s32[8]{0:T(128)S(1)} %copy-done.4, s32[1]{0:T(128)S(6)} %copy.9.length, bf16[512,256]{1,0:T(8,128)(2,1)S(1)} %get-tuple-element.82.queries, f32[512,256]{1,0:T(8,128)S(1)} %get-tuple-element.83.sums, f32[512,256]{1,0:T(8,128)S(1)} %get-tuple-element.84.largest, ...), custom_call_target="tpu_custom_call" | custom-call | flops 4000000000 | bytes 1000 | tf_op jit(solution)/shard_map/attend/pallas_call | solution.py:340
  118.4 0.4 collective-permute-start.21
  118.8 3.2 %attend_local.3 = (bf16[512,256]{1,0:T(8,128)(2,1)S(1)}, f32[512,256]{1,0:T(8,128)S(1)}, f32[512,256]{1,0:T(8,128)S(1)}, f32[512,256]{1,0:T(8,128)S(1)}) custom-call(s32[8]{0:T(128)S(1)} %copy-done.4, bf16[4096,256]{1,0:T(8,128)(2,1)S(1)} %get-tuple-element.88.refs_1_, bf16[4,1024,1024]{2,1,0:T(8,128)(2,1)S(1)} %get-tuple-element.80.refs_7_.refs_2_, ...), custom_call_target="tpu_custom_call" | custom-call | flops 4000000000 | bytes 1000 | tf_op jit(solution)/shard_map/attend_local/pallas_call | solution.py:279
  122.0 3.2 %attend.3 = bf16[512,512]{1,0:T(8,128)(2,1)} custom-call(s32[8]{0:T(128)S(1)} %copy-done.4, s32[1]{0:T(128)S(6)} %copy.9.length, bf16[512,256]{1,0:T(8,128)(2,1)S(1)} %get-tuple-element.89.queries, f32[512,256]{1,0:T(8,128)S(1)} %get-tuple-element.90.sums, f32[512,256]{1,0:T(8,128)S(1)} %get-tuple-element.91.largest, ...), custom_call_target="tpu_custom_call" | custom-call | flops 4000000000 | bytes 1000 | tf_op jit(solution)/shard_map/attend/pallas_call | solution.py:340
  125.2 0.5 collective-permute-done.21
  125.7 0.7 constant_dynamic-update-slice_fusion
  (14 shorter events, 0.0 us)
Async XLA Ops:
  0.0 37.7 %collective-permute-start = (bf16[512,1024]{1,0:T(8,128)(2,1)}, bf16[512,1024]{1,0:T(8,128)(2,1)}, u32[]{:S(2)}, u32[]{:S(2)}) collective-permute-start(bf16[512,1024]{1,0:T(8,128)(2,1)} %refs_0_.4), channel_id=1, source_target_pairs={{0,4},{4,0},{8,12},{12,8},{1,5},{5,1},{9,13},{13,9},{2,6},{6,2},{1... | collective-permute-start | bytes 3145736 | tf_op jit(solution)/shard_map/L_Xz/ppermute | solution.py:34
  3.0 34.7 %collective-permute-start.1 = (bf16[512,1024]{1,0:T(8,128)(2,1)}, bf16[512,1024]{1,0:T(8,128)(2,1)}, u32[]{:S(2)}, u32[]{:S(2)}) collective-permute-start(bf16[512,1024]{1,0:T(8,128)(2,1)} %refs_0_.4), channel_id=1, source_target_pairs={{0,2},{2,0},{1,3},{3,1},{4,6},{6,4},{5,7},{7,5},{8,10},{10,8},{9,1... | collective-permute-start | bytes 3145736 | tf_op jit(solution)/shard_map/L_Ax1/ppermute | solution.py:34
  4.5 33.2 %collective-permute-start.2 = (bf16[512,1024]{1,0:T(8,128)(2,1)}, bf16[512,1024]{1,0:T(8,128)(2,1)S(1)}, u32[]{:S(2)}, u32[]{:S(2)}) collective-permute-start(bf16[512,1024]{1,0:T(8,128)(2,1)} %refs_0_.4), channel_id=1, source_target_pairs={{0,1},{1,0},{2,3},{3,2},{4,5},{5,4},{6,7},{7,6},{8,9},{9,8},{10,11... | collective-permute-start | bytes 3145736 | tf_op jit(solution)/shard_map/L_A0c1/ppermute | solution.py:34
  7.4 29.6 %collective-permute-start.3 = (bf16[512,512]{1,0:T(8,128)(2,1)}, bf16[512,512]{1,0:T(8,128)(2,1)S(1)}, u32[]{:S(2)}, u32[]{:S(2)}) collective-permute-start(bf16[512,512]{1,0:T(8,128)(2,1)} %get-tuple-element.50), channel_id=1, source_target_pairs={{0,8},{4,12},{8,0},{12,4},{1,9},{5,13},{9,1},{13,5},{2,10},{6,14},... | collective-permute-start | bytes 1572872 | tf_op jit(solution)/shard_map/L_kv2/ppermute | solution.py:34
  37.7 28.5 %collective-permute-start.4 = (bf16[512,1024]{1,0:T(8,128)(2,1)}, bf16[512,1024]{1,0:T(8,128)(2,1)}, u32[]{:S(2)}, u32[]{:S(2)}) collective-permute-start(bf16[512,1024]{1,0:T(8,128)(2,1)} %collective-permute-done.partner_ref.refs_4_), channel_id=1, source_target_pairs={{0,2},{2,0},{1,3},{3,1},{4,6},{6,4},{5,7},{7,5},{8,10},{10,8},{9,1... | collective-permute-start | bytes 3145736 | tf_op jit(solution)/shard_map/L_Bx1/ppermute | solution.py:34
  39.4 16.9 %collective-permute-start.5 = (bf16[512,512]{1,0:T(8,128)(2,1)}, bf16[512,512]{1,0:T(8,128)(2,1)S(1)}, u32[]{:S(2)}, u32[]{:S(2)}) collective-permute-start(bf16[512,512]{1,0:T(8,128)(2,1)} %get-tuple-element.57), channel_id=1, source_target_pairs={{0,12},{4,8},{8,4},{12,0},{1,13},{5,9},{9,5},{13,1},{2,14},{6,10},... | collective-permute-start | bytes 1572872 | tf_op jit(solution)/shard_map/L_kv3/ppermute | solution.py:34
  43.0 22.3 %collective-permute-start.6 = (bf16[512,512]{1,0:T(8,128)(2,1)}, bf16[512,512]{1,0:T(8,128)(2,1)S(1)}, u32[]{:S(2)}, u32[]{:S(2)}) collective-permute-start(bf16[512,512]{1,0:T(8,128)(2,1)} %get-tuple-element.57), channel_id=1, source_target_pairs={{0,4},{4,0},{8,12},{12,8},{1,5},{5,1},{9,13},{13,9},{2,6},{6,2},{1... | collective-permute-start | bytes 1572872 | tf_op jit(solution)/shard_map/L_kv1/ppermute | solution.py:34
  43.0 22.3 %collective-permute-start.7 = (bf16[512,512]{1,0:T(8,128)(2,1)S(1)}, bf16[512,512]{1,0:T(8,128)(2,1)S(1)}, u32[]{:S(2)}, u32[]{:S(2)}) collective-permute-start(bf16[512,512]{1,0:T(8,128)(2,1)S(1)} %collective-permute-done.3.refs_3_), channel_id=1, source_target_pairs={{0,16},{16,0},{1,17},{17,1},{2,18},{18,2},{3,19},{19,3},{4,20},{20... | collective-permute-start | bytes 1572872 | tf_op jit(solution)/shard_map/L_ykv2/ppermute | solution.py:34
  49.0 18.8 %copy-start.9 = (bf16[1024,256]{1,0:T(8,128)(2,1)S(1)}, bf16[1024,256]{1,0:T(8,128)(2,1)}, u32[]{:S(2)}) copy-start(bf16[1024,256]{1,0:T(8,128)(2,1)} %get-tuple-element.67) | copy-start | bytes 1572868
  49.0 20.5 %copy-start.7 = (bf16[256,1024]{1,0:T(8,128)(2,1)S(1)}, bf16[256,1024]{1,0:T(8,128)(2,1)}, u32[]{:S(2)}) copy-start(bf16[256,1024]{1,0:T(8,128)(2,1)} %compress.1.refs_7_) | copy-start | bytes 1572868
  49.1 21.0 %copy-start.11 = (bf16[512,256]{1,0:T(8,128)(2,1)S(1)}, bf16[512,256]{1,0:T(8,128)(2,1)}, u32[]{:S(2)}) copy-start(bf16[512,256]{1,0:T(8,128)(2,1)} %get-tuple-element.63) | copy-start | bytes 786436
  49.1 21.6 %copy-start.10 = (bf16[512,256]{1,0:T(8,128)(2,1)S(1)}, bf16[512,256]{1,0:T(8,128)(2,1)}, u32[]{:S(2)}) copy-start(bf16[512,256]{1,0:T(8,128)(2,1)} %get-tuple-element.65) | copy-start | bytes 786436
  49.1 16.3 %collective-permute-start.8 = (bf16[256,1024]{1,0:T(8,128)(2,1)}, bf16[256,1024]{1,0:T(8,128)(2,1)S(1)}, u32[]{:S(2)}, u32[]{:S(2)}) collective-permute-start(bf16[256,1024]{1,0:T(8,128)(2,1)} %compress.1.refs_7_), channel_id=1, source_target_pairs={{0,1},{1,0},{2,3},{3,2},{4,5},{5,4},{6,7},{7,6},{8,9},{9,8},{10,11... | collective-permute-start | bytes 1572872 | tf_op jit(solution)/shard_map/L_C0c1/ppermute | solution.py:34
  65.3 2.5 %copy-start.6 = (bf16[512,512]{1,0:T(8,128)(2,1)}, bf16[512,512]{1,0:T(8,128)(2,1)S(1)}, u32[]{:S(2)}) copy-start(bf16[512,512]{1,0:T(8,128)(2,1)S(1)} %collective-permute-done.7.refs_5_) | copy-start | bytes 1572868
  65.3 0.9 copy-start.8
  66.3 26.4 %collective-permute-start.12 = (bf16[1024,512]{1,0:T(8,128)(2,1)S(1)}, bf16[1024,512]{1,0:T(8,128)(2,1)S(1)}, u32[]{:S(2)}, u32[]{:S(2)}) collective-permute-start(bf16[1024,512]{1,0:T(8,128)(2,1)S(1)} %pad_maximum_fusion), channel_id=1, source_target_pairs={{0,16},{16,0},{1,17},{17,1},{2,18},{18,2},{3,19},{19,3},{4,20},{20... | collective-permute-start | bytes 3145736 | tf_op jit(solution)/shard_map/L_ykv/ppermute | solution.py:34
  67.9 24.8 %collective-permute-start.11 = (bf16[1024,256]{1,0:T(8,128)(2,1)S(1)}, bf16[1024,256]{1,0:T(8,128)(2,1)S(1)}, u32[]{:S(2)}, u32[]{:S(2)}) collective-permute-start(bf16[1024,256]{1,0:T(8,128)(2,1)S(1)} %copy-done.9), channel_id=1, source_target_pairs={{0,4},{4,0},{8,12},{12,8},{1,5},{5,1},{9,13},{13,9},{2,6},{6,2},{1... | collective-permute-start | bytes 1572872 | tf_op jit(solution)/shard_map/L_q1/ppermute | solution.py:34
  69.6 23.1 %collective-permute-start.13 = (bf16[256,1024]{1,0:T(8,128)(2,1)S(1)}, bf16[256,1024]{1,0:T(8,128)(2,1)}, u32[]{:S(2)}, u32[]{:S(2)}) collective-permute-start(bf16[256,1024]{1,0:T(8,128)(2,1)S(1)} %copy-done.7), channel_id=1, source_target_pairs={{0,2},{2,0},{1,3},{3,1},{4,6},{6,4},{5,7},{7,5},{8,10},{10,8},{9,1... | collective-permute-start | bytes 1572872 | tf_op jit(solution)/shard_map/L_Cx1/ppermute | solution.py:34
  70.1 17.5 %collective-permute-start.9 = (bf16[512,256]{1,0:T(8,128)(2,1)S(1)}, bf16[512,256]{1,0:T(8,128)(2,1)S(1)}, u32[]{:S(2)}, u32[]{:S(2)}) collective-permute-start(bf16[512,256]{1,0:T(8,128)(2,1)S(1)} %copy-done.11), channel_id=1, source_target_pairs={{0,8},{4,12},{8,0},{12,4},{1,9},{5,13},{9,1},{13,5},{2,10},{6,14},... | collective-permute-start | bytes 786440 | tf_op jit(solution)/shard_map/L_q2/ppermute | solution.py:34
  70.6 21.2 %collective-permute-start.10 = (bf16[512,256]{1,0:T(8,128)(2,1)S(1)}, bf16[512,256]{1,0:T(8,128)(2,1)S(1)}, u32[]{:S(2)}, u32[]{:S(2)}) collective-permute-start(bf16[512,256]{1,0:T(8,128)(2,1)S(1)} %copy-done.10), channel_id=1, source_target_pairs={{0,12},{4,8},{8,4},{12,0},{1,13},{5,9},{9,5},{13,1},{2,14},{6,10},... | collective-permute-start | bytes 786440 | tf_op jit(solution)/shard_map/L_q3/ppermute | solution.py:34
  87.6 13.6 %collective-permute-start.16 = (bf16[512,1024]{1,0:T(8,128)(2,1)}, bf16[512,1024]{1,0:T(8,128)(2,1)}, u32[]{:S(2)}, u32[]{:S(2)}) collective-permute-start(bf16[512,1024]{1,0:T(8,128)(2,1)} %collective-permute-done.1.refs_2_), channel_id=1, source_target_pairs={{0,1},{1,0},{2,3},{3,2},{4,5},{5,4},{6,7},{7,6},{8,9},{9,8},{10,11... | collective-permute-start | bytes 3145736 | tf_op jit(solution)/shard_map/L_A1c1/ppermute | solution.py:34
  91.9 0.8 copy-start.2
  91.9 12.0 %collective-permute-start.17 = (bf16[512,1024]{1,0:T(8,128)(2,1)}, bf16[512,1024]{1,0:T(8,128)(2,1)}, u32[]{:S(2)}, u32[]{:S(2)}) collective-permute-start(bf16[512,1024]{1,0:T(8,128)(2,1)} %collective-permute-done.partner_ref.refs_4_), channel_id=1, source_target_pairs={{0,1},{1,0},{2,3},{3,2},{4,5},{5,4},{6,7},{7,6},{8,9},{9,8},{10,11... | collective-permute-start | bytes 3145736 | tf_op jit(solution)/shard_map/L_B0c1/ppermute | solution.py:34
  92.7 11.2 %collective-permute-start.18 = (bf16[512,1024]{1,0:T(8,128)(2,1)}, bf16[512,1024]{1,0:T(8,128)(2,1)}, u32[]{:S(2)}, u32[]{:S(2)}) collective-permute-start(bf16[512,1024]{1,0:T(8,128)(2,1)} %collective-permute-done.4.refs_6_), channel_id=1, source_target_pairs={{0,1},{1,0},{2,3},{3,2},{4,5},{5,4},{6,7},{7,6},{8,9},{9,8},{10,11... | collective-permute-start | bytes 3145736 | tf_op jit(solution)/shard_map/L_B1c1/ppermute | solution.py:34
  92.7 1.0 copy-start.5
  93.6 3.5 %collective-permute-start.19 = (bf16[256,1024]{1,0:T(8,128)(2,1)}, bf16[256,1024]{1,0:T(8,128)(2,1)}, u32[]{:S(2)}, u32[]{:S(2)}) collective-permute-start(bf16[256,1024]{1,0:T(8,128)(2,1)} %collective-permute-done.13.refs_9_), channel_id=1, source_target_pairs={{0,1},{1,0},{2,3},{3,2},{4,5},{5,4},{6,7},{7,6},{8,9},{9,8},{10,11... | collective-permute-start | bytes 1572872 | tf_op jit(solution)/shard_map/L_C1c1/ppermute | solution.py:34
  94.8 9.1 %copy-start = (bf16[512,1024]{1,0:T(8,128)(2,1)S(1)}, bf16[512,1024]{1,0:T(8,128)(2,1)}, u32[]{:S(2)}) copy-start(bf16[512,1024]{1,0:T(8,128)(2,1)} %refs_0_.4) | copy-start | bytes 3145732
  94.8 15.0 %collective-permute-start.14 = (bf16[512,256]{1,0:T(8,128)(2,1)S(1)}, bf16[512,256]{1,0:T(8,128)(2,1)S(1)}, u32[]{:S(2)}, u32[]{:S(2)}) collective-permute-start(bf16[512,256]{1,0:T(8,128)(2,1)S(1)} %collective-permute-done.9.refs_3_), channel_id=1, source_target_pairs={{0,16},{16,0},{1,17},{17,1},{2,18},{18,2},{3,19},{19,3},{4,20},{20... | collective-permute-start | bytes 786440 | tf_op jit(solution)/shard_map/L_yq2/ppermute | solution.py:34
  97.1 12.7 %collective-permute-start.15 = (bf16[512,256]{1,0:T(8,128)(2,1)}, bf16[512,256]{1,0:T(8,128)(2,1)S(1)}, u32[]{:S(2)}, u32[]{:S(2)}) collective-permute-start(bf16[512,256]{1,0:T(8,128)(2,1)} %copy-done.2), channel_id=1, source_target_pairs={{0,16},{16,0},{1,17},{17,1},{2,18},{18,2},{3,19},{19,3},{4,20},{20... | collective-permute-start | bytes 786440 | tf_op jit(solution)/shard_map/L_yq3/ppermute | solution.py:34
  101.2 14.7 %collective-permute-start.20 = (bf16[256,512]{1,0:T(8,128)(2,1)S(1)}, bf16[256,512]{1,0:T(8,128)(2,1)S(1)}, u32[]{:S(2)}, u32[]{:S(2)}) collective-permute-start(bf16[256,512]{1,0:T(8,128)(2,1)S(1)} %get-tuple-element.86.refs_0_), channel_id=1, source_target_pairs={{0,8},{4,12},{8,0},{12,4},{1,9},{5,13},{9,1},{13,5},{2,10},{6,14},... | collective-permute-start | bytes 786440 | tf_op jit(solution)/shard_map/L_m2/ppermute | solution.py:34
  103.9 5.9 %copy-start.1 = (bf16[1024,512]{1,0:T(8,128)(2,1)S(1)}, bf16[1024,512]{1,0:T(8,128)(2,1)}, u32[]{:S(2)}) copy-start(bf16[1024,512]{1,0:T(8,128)(2,1)} %refs_1_.3) | copy-start | bytes 3145732
  103.9 5.9 %copy-start.3 = (bf16[512,256]{1,0:T(8,128)(2,1)S(1)}, bf16[512,256]{1,0:T(8,128)(2,1)}, u32[]{:S(2)}) copy-start(bf16[512,256]{1,0:T(8,128)(2,1)} %copy-done.2) | copy-start | bytes 786436
  103.9 5.9 %copy-start.4 = (s32[8]{0:T(128)S(1)}, s32[8]{0:T(128)}, u32[]{:S(2)}) copy-start(s32[8]{0:T(128)} %segments.3) | copy-start | bytes 100
  118.4 7.3 %collective-permute-start.21 = (bf16[512,256]{1,0:T(8,128)(2,1)S(1)}, bf16[512,256]{1,0:T(8,128)(2,1)S(1)}, u32[]{:S(2)}, u32[]{:S(2)}) collective-permute-start(bf16[512,256]{1,0:T(8,128)(2,1)S(1)} %attend.2), channel_id=1, source_target_pairs={{0,4},{4,0},{8,12},{12,8},{1,5},{5,1},{9,13},{13,9},{2,6},{6,2},{1... | collective-permute-start | bytes 786440 | tf_op jit(solution)/shard_map/L_ctx/ppermute | solution.py:34

commit v7 on v6

--- a/solution.py
+++ b/solution.py
@@ -389,7 +389,7 @@
     fresh = []
     every = range(1, planes)
     first = [2] if planes > 2 else []
-    second = [d for d in every[::-1] if d not in first]
+    second = [d for d in every if d not in first]
     stage(
         {"Xz": (activations, "seq", 1)}
         | across(activations, "A")

time: 127 us -> 126 us (level)
  transfers between devices with their start and end apart: 22 -> 22, of which waited for: 10 -> 9; matrix products, arithmetic and copies ran while one was open for 0% -> 0% of each run, Pallas kernels for 21% -> 21%
where the time goes in v7:
time: 126 us
  waiting for transfers between devices  68.4 us (54%)
  Pallas kernels  29.1 us (23%)
  starting transfers between devices  24.6 us (20%)
  local copies, waits for them, and re-layouts  3.26 us (3%)
    ppermute x22, waiting for transfers between devices, swap(): return lax.ppermute(value, axis, [(i, i ^ distance) for i in range(size)])  68.4 us
    ppermute x22, starting transfers between devices, swap(): return lax.ppermute(value, axis, [(i, i ^ distance) for i in range(size)])  24.6 us
    pallas_call x2, Pallas kernels, attend_local(): pl.pallas_call(functools.partial(local_kernel, side, planes, tensor_size,...  6.57 us
    pallas_call x1, Pallas kernels, project_tokens(): pl.pallas_call(functools.partial(tokens_kernel, tensor_size, sub_size), o...  5.83 us
    pallas_call x2, Pallas kernels, attend(): pl.pallas_call(functools.partial(far_kernel, side, planes), out_shape=jax...  5.75 us
    pallas_call x1, Pallas kernels, compress(): pl.pallas_call(compress_kernel, out_shape=jax.ShapeDtypeStruct((2 * count...  4.51 us
    pallas_call x1, Pallas kernels, project_memory(): pl.pallas_call(functools.partial(memory_kernel, planes, tensor_size, sub_...  3.54 us
    pallas_call x1, Pallas kernels, split_weights(): pl.pallas_call(split_kernel, out_shape=[jax.ShapeDtypeStruct(s, BF) for s...  2.89 us
  transfers between devices with their start and end apart: 22, of which 9 were waited for; matrix products, arithmetic and copies ran while one was open for 0% of the time, Pallas kernels for 21%

profile of v7, /device:TPU:0, one launch (start us, length us, event | category | flops | bytes accessed | tf_op | source)
XLA Modules:
  0.0 126.2 jit_solution(14806884733961256934)
XLA Ops:
  0.0 3.0 %collective-permute-start = (bf16[512,1024]{1,0:T(8,128)(2,1)}, bf16[512,1024]{1,0:T(8,128)(2,1)}, u32[]{:S(2)}, u32[]{:S(2)}) collective-permute-start(bf16[512,1024]{1,0:T(8,128)(2,1)} %refs_0_.4), channel_id=1, source_target_pairs={{0,4},{4,0},{8,12},{12,8},{1,5},{5,1},{9,13},{13,9},{2,6},{6,2},{1... | collective-permute-start | bytes 3145736 | tf_op jit(solution)/shard_map/L_Xz/ppermute | solution.py:34
  3.0 1.5 %collective-permute-start.1 = (bf16[512,1024]{1,0:T(8,128)(2,1)}, bf16[512,1024]{1,0:T(8,128)(2,1)}, u32[]{:S(2)}, u32[]{:S(2)}) collective-permute-start(bf16[512,1024]{1,0:T(8,128)(2,1)} %refs_0_.4), channel_id=1, source_target_pairs={{0,2},{2,0},{1,3},{3,1},{4,6},{6,4},{5,7},{7,5},{8,10},{10,8},{9,1... | collective-permute-start | bytes 3145736 | tf_op jit(solution)/shard_map/L_Ax1/ppermute | solution.py:34
  4.5 0.0 collective-permute-start.2
  4.5 2.9 %split_weights.1 = (bf16[512,512]{1,0:T(8,128)(2,1)}, bf16[512,512]{1,0:T(8,128)(2,1)}, bf16[512,256]{1,0:T(8,128)(2,1)}, bf16[512,256]{1,0:T(8,128)(2,1)}, bf16[1024,256]{1,0:T(8,128)(2,1)}) custom-call(bf16[1024,512]{1,0:T(8,128)(2,1)} %refs_0_.3, bf16[1024,512]{1,0:T(8,128)(2,1)} %refs_1_.2, bf16[1024,512]{1,0:T(8,128)(2,1)} %refs_1_.3), custom_call_target="tpu_custom_call" | custom-call | flops 2000000000 | bytes 1000 | tf_op jit(solution)/shard_map/split_weights/pallas_call | solution.py:74
  7.4 2.7 %collective-permute-start.3 = (bf16[512,512]{1,0:T(8,128)(2,1)}, bf16[512,512]{1,0:T(8,128)(2,1)S(1)}, u32[]{:S(2)}, u32[]{:S(2)}) collective-permute-start(bf16[512,512]{1,0:T(8,128)(2,1)} %get-tuple-element.50), channel_id=1, source_target_pairs={{0,8},{4,12},{8,0},{12,4},{1,9},{5,13},{9,1},{13,5},{2,10},{6,14},... | collective-permute-start | bytes 1572872 | tf_op jit(solution)/shard_map/L_kv2/ppermute | solution.py:34
  10.1 26.9 %collective-permute-done.3.refs_3_ = bf16[512,512]{1,0:T(8,128)(2,1)S(1)} collective-permute-done((bf16[512,512]{1,0:T(8,128)(2,1)}, bf16[512,512]{1,0:T(8,128)(2,1)S(1)}, u32[]{:S(2)}, u32[]{:S(2)}) %collective-permute-start.3) | collective-permute-done | bytes 524320 | tf_op jit(solution)/shard_map/L_kv2/ppermute | solution.py:34
  37.0 0.7 collective-permute-done.partner_ref.refs_4_
  37.7 0.0 collective-permute-done.1.refs_2_
  37.7 0.0 collective-permute-done.2.refs_1_
  37.7 1.7 %collective-permute-start.4 = (bf16[512,1024]{1,0:T(8,128)(2,1)}, bf16[512,1024]{1,0:T(8,128)(2,1)}, u32[]{:S(2)}, u32[]{:S(2)}) collective-permute-start(bf16[512,1024]{1,0:T(8,128)(2,1)} %collective-permute-done.partner_ref.refs_4_), channel_id=1, source_target_pairs={{0,2},{2,0},{1,3},{3,1},{4,6},{6,4},{5,7},{7,5},{8,10},{10,8},{9,1... | collective-permute-start | bytes 3145736 | tf_op jit(solution)/shard_map/L_Bx1/ppermute | solution.py:34
  39.4 2.6 %collective-permute-start.5 = (bf16[512,512]{1,0:T(8,128)(2,1)}, bf16[512,512]{1,0:T(8,128)(2,1)S(1)}, u32[]{:S(2)}, u32[]{:S(2)}) collective-permute-start(bf16[512,512]{1,0:T(8,128)(2,1)} %get-tuple-element.57), channel_id=1, source_target_pairs={{0,4},{4,0},{8,12},{12,8},{1,5},{5,1},{9,13},{13,9},{2,6},{6,2},{1... | collective-permute-start | bytes 1572872 | tf_op jit(solution)/shard_map/L_kv1/ppermute | solution.py:34
  42.0 1.3 %collective-permute-start.6 = (bf16[512,512]{1,0:T(8,128)(2,1)}, bf16[512,512]{1,0:T(8,128)(2,1)S(1)}, u32[]{:S(2)}, u32[]{:S(2)}) collective-permute-start(bf16[512,512]{1,0:T(8,128)(2,1)} %get-tuple-element.57), channel_id=1, source_target_pairs={{0,12},{4,8},{8,4},{12,0},{1,13},{5,9},{9,5},{13,1},{2,14},{6,10},... | collective-permute-start | bytes 1572872 | tf_op jit(solution)/shard_map/L_kv3/ppermute | solution.py:34
  43.3 1.5 %collective-permute-start.7 = (bf16[512,512]{1,0:T(8,128)(2,1)S(1)}, bf16[512,512]{1,0:T(8,128)(2,1)S(1)}, u32[]{:S(2)}, u32[]{:S(2)}) collective-permute-start(bf16[512,512]{1,0:T(8,128)(2,1)S(1)} %collective-permute-done.3.refs_3_), channel_id=1, source_target_pairs={{0,16},{16,0},{1,17},{17,1},{2,18},{18,2},{3,19},{19,3},{4,20},{20... | collective-permute-start | bytes 1572872 | tf_op jit(solution)/shard_map/L_ykv2/ppermute | solution.py:34
  44.8 4.5 %compress.1.refs_7_ = bf16[256,1024]{1,0:T(8,128)(2,1)} custom-call(bf16[512,1024]{1,0:T(8,128)(2,1)} %refs_0_.4, bf16[512,1024]{1,0:T(8,128)(2,1)} %collective-permute-done.partner_ref.refs_4_, bf16[512,1024]{1,0:T(8,128)(2,1)} %w_ref.1), custom_call_target="tpu_custom_call" | custom-call | flops 5000000000 | bytes 1000 | tf_op jit(solution)/shard_map/compress/pallas_call | solution.py:106
  49.3 0.1 collective-permute-start.8
  49.4 5.2 %collective-permute-done.5.refs_2_ = bf16[512,512]{1,0:T(8,128)(2,1)S(1)} collective-permute-done((bf16[512,512]{1,0:T(8,128)(2,1)}, bf16[512,512]{1,0:T(8,128)(2,1)S(1)}, u32[]{:S(2)}, u32[]{:S(2)}) %collective-permute-start.5) | collective-permute-done | bytes 524320 | tf_op jit(solution)/shard_map/L_kv1/ppermute | solution.py:34
  54.6 10.7 %collective-permute-done.6.refs_4_ = bf16[512,512]{1,0:T(8,128)(2,1)S(1)} collective-permute-done((bf16[512,512]{1,0:T(8,128)(2,1)}, bf16[512,512]{1,0:T(8,128)(2,1)S(1)}, u32[]{:S(2)}, u32[]{:S(2)}) %collective-permute-start.6) | collective-permute-done | bytes 524320 | tf_op jit(solution)/shard_map/L_kv3/ppermute | solution.py:34
  65.3 0.0 collective-permute-done.7.refs_5_
  65.3 0.0 collective-permute-done.8.refs_8_
  65.4 0.0 copy-start.8
  65.4 0.9 copy-done.8
  66.2 0.0 collective-permute-done.4.refs_6_
  66.2 0.1 pad_maximum_fusion
  66.3 1.6 %collective-permute-start.12 = (bf16[1024,512]{1,0:T(8,128)(2,1)S(1)}, bf16[1024,512]{1,0:T(8,128)(2,1)S(1)}, u32[]{:S(2)}, u32[]{:S(2)}) collective-permute-start(bf16[1024,512]{1,0:T(8,128)(2,1)S(1)} %pad_maximum_fusion), channel_id=1, source_target_pairs={{0,16},{16,0},{1,17},{17,1},{2,18},{18,2},{3,19},{19,3},{4,20},{20... | collective-permute-start | bytes 3145736 | tf_op jit(solution)/shard_map/L_ykv/ppermute | solution.py:34
  67.9 0.0 copy-done.6
  67.9 0.8 collective-permute-start.11
  68.6 0.5 collective-permute-start.13
  69.2 0.0 copy-done.11
  69.2 2.3 %collective-permute-start.9 = (bf16[512,256]{1,0:T(8,128)(2,1)S(1)}, bf16[512,256]{1,0:T(8,128)(2,1)S(1)}, u32[]{:S(2)}, u32[]{:S(2)}) collective-permute-start(bf16[512,256]{1,0:T(8,128)(2,1)S(1)} %copy-done.11), channel_id=1, source_target_pairs={{0,8},{4,12},{8,0},{12,4},{1,9},{5,13},{9,1},{13,5},{2,10},{6,14},... | collective-permute-start | bytes 786440 | tf_op jit(solution)/shard_map/L_q2/ppermute | solution.py:34
  71.5 1.4 %collective-permute-start.10 = (bf16[512,256]{1,0:T(8,128)(2,1)S(1)}, bf16[512,256]{1,0:T(8,128)(2,1)S(1)}, u32[]{:S(2)}, u32[]{:S(2)}) collective-permute-start(bf16[512,256]{1,0:T(8,128)(2,1)S(1)} %copy-done.10), channel_id=1, source_target_pairs={{0,12},{4,8},{8,4},{12,0},{1,13},{5,9},{9,5},{13,1},{2,14},{6,10},... | collective-permute-start | bytes 786440 | tf_op jit(solution)/shard_map/L_q3/ppermute | solution.py:34
  72.8 12.6 %collective-permute-done.9.refs_3_ = bf16[512,256]{1,0:T(8,128)(2,1)S(1)} collective-permute-done((bf16[512,256]{1,0:T(8,128)(2,1)S(1)}, bf16[512,256]{1,0:T(8,128)(2,1)S(1)}, u32[]{:S(2)}, u32[]{:S(2)}) %collective-permute-start.9) | collective-permute-done | bytes 262176 | tf_op jit(solution)/shard_map/L_q2/ppermute | solution.py:34
  85.4 0.0 collective-permute-start.16
  85.4 5.8 %collective-permute-done.10.refs_4_ = bf16[512,256]{1,0:T(8,128)(2,1)S(1)} collective-permute-done((bf16[512,256]{1,0:T(8,128)(2,1)S(1)}, bf16[512,256]{1,0:T(8,128)(2,1)S(1)}, u32[]{:S(2)}, u32[]{:S(2)}) %collective-permute-start.10) | collective-permute-done | bytes 262176 | tf_op jit(solution)/shard_map/L_q3/ppermute | solution.py:34
  91.2 0.0 collective-permute-start.17
  91.2 0.0 collective-permute-done.11.refs_2_
  91.2 0.7 copy-done.2
  91.9 0.0 collective-permute-start.18
  91.9 0.0 collective-permute-done.13.refs_9_
  91.9 0.0 collective-permute-done.12.refs_6_
  91.9 1.0 copy-done.5
  92.9 0.5 collective-permute-start.19
  94.0 0.0 copy-start
  94.1 0.6 collective-permute-start.14
  94.6 1.8 %collective-permute-done.19.refs_10_ = bf16[256,1024]{1,0:T(8,128)(2,1)} collective-permute-done((bf16[256,1024]{1,0:T(8,128)(2,1)}, bf16[256,1024]{1,0:T(8,128)(2,1)}, u32[]{:S(2)}, u32[]{:S(2)}) %collective-permute-start.19) | collective-permute-done | bytes 524320 | tf_op jit(solution)/shard_map/L_C1c1/ppermute | solution.py:34
  96.5 0.5 collective-permute-start.15
  97.0 3.5 %project_memory.1 = (bf16[256,512]{1,0:T(8,128)(2,1)S(1)}, bf16[4096,512]{1,0:T(8,128)(2,1)S(1)}) custom-call(bf16[1024,512]{1,0:T(8,128)(2,1)} %refs_0_.3, bf16[1024,512]{1,0:T(8,128)(2,1)} %refs_1_.2, bf16[512,512]{1,0:T(8,128)(2,1)S(1)} %collective-permute-done.5.refs_2_, bf16[512,512]{1,0:T(8,128)(2,1)S(1)} %collective-permute-done.3.refs_3_, ...), custom_call_target="tpu_custom_call" | custom-call | flops 4000000000 | bytes 1000 | tf_op jit(solution)/shard_map/project_memory/pallas_call | solution.py:178
  100.5 0.0 collective-permute-done.16.refs_3_
  100.5 2.1 %collective-permute-start.20 = (bf16[256,512]{1,0:T(8,128)(2,1)S(1)}, bf16[256,512]{1,0:T(8,128)(2,1)S(1)}, u32[]{:S(2)}, u32[]{:S(2)}) collective-permute-start(bf16[256,512]{1,0:T(8,128)(2,1)S(1)} %get-tuple-element.86.refs_0_), channel_id=1, source_target_pairs={{0,8},{4,12},{8,0},{12,4},{1,9},{5,13},{9,1},{13,5},{2,10},{6,14},... | collective-permute-start | bytes 786440 | tf_op jit(solution)/shard_map/L_m2/ppermute | solution.py:34
  102.6 0.0 collective-permute-done.17.refs_5_
  102.6 0.0 collective-permute-done.18.refs_7_
  102.6 0.0 copy-done
  102.6 0.0 copy-start.1
  102.6 0.0 copy-start.4
  102.7 5.8 %project_tokens.1 = (bf16[1024,512]{1,0:T(8,128)(2,1)S(1)}, bf16[4,1024,1024]{2,1,0:T(8,128)(2,1)S(1)}) custom-call(bf16[512,1024]{1,0:T(8,128)(2,1)S(1)} %copy-done, bf16[512,1024]{1,0:T(8,128)(2,1)S(1)} %collective-permute-done.2.refs_1_, bf16[512,1024]{1,0:T(8,128)(2,1)} %collective-permute-done.1.refs_2_, ...), custom_call_target="tpu_custom_call" | custom-call | flops 6000000000 | bytes 1000 | tf_op jit(solution)/shard_map/project_tokens/pallas_call | solution.py:222
  108.5 0.0 collective-permute-done.14.refs_5_
  108.5 0.0 collective-permute-done.15.refs_6_
  108.5 3.4 %attend_local.2 = (bf16[512,256]{1,0:T(8,128)(2,1)S(1)}, f32[512,256]{1,0:T(8,128)S(1)}, f32[512,256]{1,0:T(8,128)S(1)}, f32[512,256]{1,0:T(8,128)S(1)}, bf16[4096,256]{1,0:T(8,128)(2,1)S(1)}) custom-call(s32[8]{0:T(128)S(1)} %copy-done.4, bf16[1024,512]{1,0:T(8,128)(2,1)S(1)} %copy-done.1, bf16[1024,256]{1,0:T(8,128)(2,1)S(1)} %collective-permute-done.11.refs_2_, ...), custom_call_target="tpu_custom_call" | custom-call | flops 4000000000 | bytes 1000 | tf_op jit(solution)/shard_map/attend_local/pallas_call | solution.py:279
  112.0 3.2 %collective-permute-done.20.refs_1_ = bf16[256,512]{1,0:T(8,128)(2,1)S(1)} collective-permute-done((bf16[256,512]{1,0:T(8,128)(2,1)S(1)}, bf16[256,512]{1,0:T(8,128)(2,1)S(1)}, u32[]{:S(2)}, u32[]{:S(2)}) %collective-permute-start.20) | collective-permute-done | bytes 262176 | tf_op jit(solution)/shard_map/L_m2/ppermute | solution.py:34
  115.2 2.5 %attend.2 = bf16[512,256]{1,0:T(8,128)(2,1)S(1)} custom-call(s32[8]{0:T(128)S(1)} %copy-done.4, s32[1]{0:T(128)S(6)} %copy.9.length, bf16[512,256]{1,0:T(8,128)(2,1)S(1)} %get-tuple-element.82.queries, f32[512,256]{1,0:T(8,128)S(1)} %get-tuple-element.83.sums, f32[512,256]{1,0:T(8,128)S(1)} %get-tuple-element.84.largest, ...), custom_call_target="tpu_custom_call" | custom-call | flops 4000000000 | bytes 1000 | tf_op jit(solution)/shard_map/attend/pallas_call | solution.py:340
  117.7 0.1 collective-permute-start.21
  117.8 3.2 %attend_local.3 = (bf16[512,256]{1,0:T(8,128)(2,1)S(1)}, f32[512,256]{1,0:T(8,128)S(1)}, f32[512,256]{1,0:T(8,128)S(1)}, f32[512,256]{1,0:T(8,128)S(1)}) custom-call(s32[8]{0:T(128)S(1)} %copy-done.4, bf16[4096,256]{1,0:T(8,128)(2,1)S(1)} %get-tuple-element.88.refs_1_, bf16[4,1024,1024]{2,1,0:T(8,128)(2,1)S(1)} %get-tuple-element.80.refs_7_.refs_2_, ...), custom_call_target="tpu_custom_call" | custom-call | flops 4000000000 | bytes 1000 | tf_op jit(solution)/shard_map/attend_local/pallas_call | solution.py:279
  121.0 3.2 %attend.3 = bf16[512,512]{1,0:T(8,128)(2,1)} custom-call(s32[8]{0:T(128)S(1)} %copy-done.4, s32[1]{0:T(128)S(6)} %copy.9.length, bf16[512,256]{1,0:T(8,128)(2,1)S(1)} %get-tuple-element.89.queries, f32[512,256]{1,0:T(8,128)S(1)} %get-tuple-element.90.sums, f32[512,256]{1,0:T(8,128)S(1)} %get-tuple-element.91.largest, ...), custom_call_target="tpu_custom_call" | custom-call | flops 4000000000 | bytes 1000 | tf_op jit(solution)/shard_map/attend/pallas_call | solution.py:340
  124.2 1.3 %collective-permute-done.21 = bf16[512,256]{1,0:T(8,128)(2,1)S(1)} collective-permute-done((bf16[512,256]{1,0:T(8,128)(2,1)S(1)}, bf16[512,256]{1,0:T(8,128)(2,1)S(1)}, u32[]{:S(2)}, u32[]{:S(2)}) %collective-permute-start.21) | collective-permute-done | bytes 262176 | tf_op jit(solution)/shard_map/L_ctx/ppermute | solution.py:34
  125.5 0.7 constant_dynamic-update-slice_fusion
  (14 shorter events, 0.0 us)
Async XLA Ops:
  0.0 37.7 %collective-permute-start = (bf16[512,1024]{1,0:T(8,128)(2,1)}, bf16[512,1024]{1,0:T(8,128)(2,1)}, u32[]{:S(2)}, u32[]{:S(2)}) collective-permute-start(bf16[512,1024]{1,0:T(8,128)(2,1)} %refs_0_.4), channel_id=1, source_target_pairs={{0,4},{4,0},{8,12},{12,8},{1,5},{5,1},{9,13},{13,9},{2,6},{6,2},{1... | collective-permute-start | bytes 3145736 | tf_op jit(solution)/shard_map/L_Xz/ppermute | solution.py:34
  3.0 34.7 %collective-permute-start.1 = (bf16[512,1024]{1,0:T(8,128)(2,1)}, bf16[512,1024]{1,0:T(8,128)(2,1)}, u32[]{:S(2)}, u32[]{:S(2)}) collective-permute-start(bf16[512,1024]{1,0:T(8,128)(2,1)} %refs_0_.4), channel_id=1, source_target_pairs={{0,2},{2,0},{1,3},{3,1},{4,6},{6,4},{5,7},{7,5},{8,10},{10,8},{9,1... | collective-permute-start | bytes 3145736 | tf_op jit(solution)/shard_map/L_Ax1/ppermute | solution.py:34
  4.5 33.2 %collective-permute-start.2 = (bf16[512,1024]{1,0:T(8,128)(2,1)}, bf16[512,1024]{1,0:T(8,128)(2,1)S(1)}, u32[]{:S(2)}, u32[]{:S(2)}) collective-permute-start(bf16[512,1024]{1,0:T(8,128)(2,1)} %refs_0_.4), channel_id=1, source_target_pairs={{0,1},{1,0},{2,3},{3,2},{4,5},{5,4},{6,7},{7,6},{8,9},{9,8},{10,11... | collective-permute-start | bytes 3145736 | tf_op jit(solution)/shard_map/L_A0c1/ppermute | solution.py:34
  7.4 29.6 %collective-permute-start.3 = (bf16[512,512]{1,0:T(8,128)(2,1)}, bf16[512,512]{1,0:T(8,128)(2,1)S(1)}, u32[]{:S(2)}, u32[]{:S(2)}) collective-permute-start(bf16[512,512]{1,0:T(8,128)(2,1)} %get-tuple-element.50), channel_id=1, source_target_pairs={{0,8},{4,12},{8,0},{12,4},{1,9},{5,13},{9,1},{13,5},{2,10},{6,14},... | collective-permute-start | bytes 1572872 | tf_op jit(solution)/shard_map/L_kv2/ppermute | solution.py:34
  37.7 28.5 %collective-permute-start.4 = (bf16[512,1024]{1,0:T(8,128)(2,1)}, bf16[512,1024]{1,0:T(8,128)(2,1)}, u32[]{:S(2)}, u32[]{:S(2)}) collective-permute-start(bf16[512,1024]{1,0:T(8,128)(2,1)} %collective-permute-done.partner_ref.refs_4_), channel_id=1, source_target_pairs={{0,2},{2,0},{1,3},{3,1},{4,6},{6,4},{5,7},{7,5},{8,10},{10,8},{9,1... | collective-permute-start | bytes 3145736 | tf_op jit(solution)/shard_map/L_Bx1/ppermute | solution.py:34
  39.4 15.2 %collective-permute-start.5 = (bf16[512,512]{1,0:T(8,128)(2,1)}, bf16[512,512]{1,0:T(8,128)(2,1)S(1)}, u32[]{:S(2)}, u32[]{:S(2)}) collective-permute-start(bf16[512,512]{1,0:T(8,128)(2,1)} %get-tuple-element.57), channel_id=1, source_target_pairs={{0,4},{4,0},{8,12},{12,8},{1,5},{5,1},{9,13},{13,9},{2,6},{6,2},{1... | collective-permute-start | bytes 1572872 | tf_op jit(solution)/shard_map/L_kv1/ppermute | solution.py:34
  42.0 23.4 %collective-permute-start.6 = (bf16[512,512]{1,0:T(8,128)(2,1)}, bf16[512,512]{1,0:T(8,128)(2,1)S(1)}, u32[]{:S(2)}, u32[]{:S(2)}) collective-permute-start(bf16[512,512]{1,0:T(8,128)(2,1)} %get-tuple-element.57), channel_id=1, source_target_pairs={{0,12},{4,8},{8,4},{12,0},{1,13},{5,9},{9,5},{13,1},{2,14},{6,10},... | collective-permute-start | bytes 1572872 | tf_op jit(solution)/shard_map/L_kv3/ppermute | solution.py:34
  43.3 22.0 %collective-permute-start.7 = (bf16[512,512]{1,0:T(8,128)(2,1)S(1)}, bf16[512,512]{1,0:T(8,128)(2,1)S(1)}, u32[]{:S(2)}, u32[]{:S(2)}) collective-permute-start(bf16[512,512]{1,0:T(8,128)(2,1)S(1)} %collective-permute-done.3.refs_3_), channel_id=1, source_target_pairs={{0,16},{16,0},{1,17},{17,1},{2,18},{18,2},{3,19},{19,3},{4,20},{20... | collective-permute-start | bytes 1572872 | tf_op jit(solution)/shard_map/L_ykv2/ppermute | solution.py:34
  49.3 18.5 %copy-start.9 = (bf16[1024,256]{1,0:T(8,128)(2,1)S(1)}, bf16[1024,256]{1,0:T(8,128)(2,1)}, u32[]{:S(2)}) copy-start(bf16[1024,256]{1,0:T(8,128)(2,1)} %get-tuple-element.67) | copy-start | bytes 1572868
  49.3 19.3 %copy-start.7 = (bf16[256,1024]{1,0:T(8,128)(2,1)S(1)}, bf16[256,1024]{1,0:T(8,128)(2,1)}, u32[]{:S(2)}) copy-start(bf16[256,1024]{1,0:T(8,128)(2,1)} %compress.1.refs_7_) | copy-start | bytes 1572868
  49.3 19.8 %copy-start.11 = (bf16[512,256]{1,0:T(8,128)(2,1)S(1)}, bf16[512,256]{1,0:T(8,128)(2,1)}, u32[]{:S(2)}) copy-start(bf16[512,256]{1,0:T(8,128)(2,1)} %get-tuple-element.63) | copy-start | bytes 786436
  49.3 22.1 %copy-start.10 = (bf16[512,256]{1,0:T(8,128)(2,1)S(1)}, bf16[512,256]{1,0:T(8,128)(2,1)}, u32[]{:S(2)}) copy-start(bf16[512,256]{1,0:T(8,128)(2,1)} %get-tuple-element.65) | copy-start | bytes 786436
  49.3 16.0 %collective-permute-start.8 = (bf16[256,1024]{1,0:T(8,128)(2,1)}, bf16[256,1024]{1,0:T(8,128)(2,1)S(1)}, u32[]{:S(2)}, u32[]{:S(2)}) collective-permute-start(bf16[256,1024]{1,0:T(8,128)(2,1)} %compress.1.refs_7_), channel_id=1, source_target_pairs={{0,1},{1,0},{2,3},{3,2},{4,5},{5,4},{6,7},{7,6},{8,9},{9,8},{10,11... | collective-permute-start | bytes 1572872 | tf_op jit(solution)/shard_map/L_C0c1/ppermute | solution.py:34
  65.3 2.5 %copy-start.6 = (bf16[512,512]{1,0:T(8,128)(2,1)}, bf16[512,512]{1,0:T(8,128)(2,1)S(1)}, u32[]{:S(2)}) copy-start(bf16[512,512]{1,0:T(8,128)(2,1)S(1)} %collective-permute-done.7.refs_5_) | copy-start | bytes 1572868
  65.4 0.9 copy-start.8
  66.3 25.6 %collective-permute-start.12 = (bf16[1024,512]{1,0:T(8,128)(2,1)S(1)}, bf16[1024,512]{1,0:T(8,128)(2,1)S(1)}, u32[]{:S(2)}, u32[]{:S(2)}) collective-permute-start(bf16[1024,512]{1,0:T(8,128)(2,1)S(1)} %pad_maximum_fusion), channel_id=1, source_target_pairs={{0,16},{16,0},{1,17},{17,1},{2,18},{18,2},{3,19},{19,3},{4,20},{20... | collective-permute-start | bytes 3145736 | tf_op jit(solution)/shard_map/L_ykv/ppermute | solution.py:34
  67.9 23.3 %collective-permute-start.11 = (bf16[1024,256]{1,0:T(8,128)(2,1)S(1)}, bf16[1024,256]{1,0:T(8,128)(2,1)S(1)}, u32[]{:S(2)}, u32[]{:S(2)}) collective-permute-start(bf16[1024,256]{1,0:T(8,128)(2,1)S(1)} %copy-done.9), channel_id=1, source_target_pairs={{0,4},{4,0},{8,12},{12,8},{1,5},{5,1},{9,13},{13,9},{2,6},{6,2},{1... | collective-permute-start | bytes 1572872 | tf_op jit(solution)/shard_map/L_q1/ppermute | solution.py:34
  68.6 23.3 %collective-permute-start.13 = (bf16[256,1024]{1,0:T(8,128)(2,1)S(1)}, bf16[256,1024]{1,0:T(8,128)(2,1)}, u32[]{:S(2)}, u32[]{:S(2)}) collective-permute-start(bf16[256,1024]{1,0:T(8,128)(2,1)S(1)} %copy-done.7), channel_id=1, source_target_pairs={{0,2},{2,0},{1,3},{3,1},{4,6},{6,4},{5,7},{7,5},{8,10},{10,8},{9,1... | collective-permute-start | bytes 1572872 | tf_op jit(solution)/shard_map/L_Cx1/ppermute | solution.py:34
  69.2 16.2 %collective-permute-start.9 = (bf16[512,256]{1,0:T(8,128)(2,1)S(1)}, bf16[512,256]{1,0:T(8,128)(2,1)S(1)}, u32[]{:S(2)}, u32[]{:S(2)}) collective-permute-start(bf16[512,256]{1,0:T(8,128)(2,1)S(1)} %copy-done.11), channel_id=1, source_target_pairs={{0,8},{4,12},{8,0},{12,4},{1,9},{5,13},{9,1},{13,5},{2,10},{6,14},... | collective-permute-start | bytes 786440 | tf_op jit(solution)/shard_map/L_q2/ppermute | solution.py:34
  71.5 19.7 %collective-permute-start.10 = (bf16[512,256]{1,0:T(8,128)(2,1)S(1)}, bf16[512,256]{1,0:T(8,128)(2,1)S(1)}, u32[]{:S(2)}, u32[]{:S(2)}) collective-permute-start(bf16[512,256]{1,0:T(8,128)(2,1)S(1)} %copy-done.10), channel_id=1, source_target_pairs={{0,12},{4,8},{8,4},{12,0},{1,13},{5,9},{9,5},{13,1},{2,14},{6,10},... | collective-permute-start | bytes 786440 | tf_op jit(solution)/shard_map/L_q3/ppermute | solution.py:34
  85.4 15.1 %collective-permute-start.16 = (bf16[512,1024]{1,0:T(8,128)(2,1)}, bf16[512,1024]{1,0:T(8,128)(2,1)}, u32[]{:S(2)}, u32[]{:S(2)}) collective-permute-start(bf16[512,1024]{1,0:T(8,128)(2,1)} %collective-permute-done.1.refs_2_), channel_id=1, source_target_pairs={{0,1},{1,0},{2,3},{3,2},{4,5},{5,4},{6,7},{7,6},{8,9},{9,8},{10,11... | collective-permute-start | bytes 3145736 | tf_op jit(solution)/shard_map/L_A1c1/ppermute | solution.py:34
  91.2 0.7 copy-start.2
  91.2 11.4 %collective-permute-start.17 = (bf16[512,1024]{1,0:T(8,128)(2,1)}, bf16[512,1024]{1,0:T(8,128)(2,1)}, u32[]{:S(2)}, u32[]{:S(2)}) collective-permute-start(bf16[512,1024]{1,0:T(8,128)(2,1)} %collective-permute-done.partner_ref.refs_4_), channel_id=1, source_target_pairs={{0,1},{1,0},{2,3},{3,2},{4,5},{5,4},{6,7},{7,6},{8,9},{9,8},{10,11... | collective-permute-start | bytes 3145736 | tf_op jit(solution)/shard_map/L_B0c1/ppermute | solution.py:34
  91.9 10.7 %collective-permute-start.18 = (bf16[512,1024]{1,0:T(8,128)(2,1)}, bf16[512,1024]{1,0:T(8,128)(2,1)}, u32[]{:S(2)}, u32[]{:S(2)}) collective-permute-start(bf16[512,1024]{1,0:T(8,128)(2,1)} %collective-permute-done.4.refs_6_), channel_id=1, source_target_pairs={{0,1},{1,0},{2,3},{3,2},{4,5},{5,4},{6,7},{7,6},{8,9},{9,8},{10,11... | collective-permute-start | bytes 3145736 | tf_op jit(solution)/shard_map/L_B1c1/ppermute | solution.py:34
  91.9 1.0 copy-start.5
  92.9 3.6 %collective-permute-start.19 = (bf16[256,1024]{1,0:T(8,128)(2,1)}, bf16[256,1024]{1,0:T(8,128)(2,1)}, u32[]{:S(2)}, u32[]{:S(2)}) collective-permute-start(bf16[256,1024]{1,0:T(8,128)(2,1)} %collective-permute-done.13.refs_9_), channel_id=1, source_target_pairs={{0,1},{1,0},{2,3},{3,2},{4,5},{5,4},{6,7},{7,6},{8,9},{9,8},{10,11... | collective-permute-start | bytes 1572872 | tf_op jit(solution)/shard_map/L_C1c1/ppermute | solution.py:34
  94.0 8.6 %copy-start = (bf16[512,1024]{1,0:T(8,128)(2,1)S(1)}, bf16[512,1024]{1,0:T(8,128)(2,1)}, u32[]{:S(2)}) copy-start(bf16[512,1024]{1,0:T(8,128)(2,1)} %refs_0_.4) | copy-start | bytes 3145732
  94.1 14.4 %collective-permute-start.14 = (bf16[512,256]{1,0:T(8,128)(2,1)S(1)}, bf16[512,256]{1,0:T(8,128)(2,1)S(1)}, u32[]{:S(2)}, u32[]{:S(2)}) collective-permute-start(bf16[512,256]{1,0:T(8,128)(2,1)S(1)} %collective-permute-done.9.refs_3_), channel_id=1, source_target_pairs={{0,16},{16,0},{1,17},{17,1},{2,18},{18,2},{3,19},{19,3},{4,20},{20... | collective-permute-start | bytes 786440 | tf_op jit(solution)/shard_map/L_yq2/ppermute | solution.py:34
  96.5 12.0 %collective-permute-start.15 = (bf16[512,256]{1,0:T(8,128)(2,1)}, bf16[512,256]{1,0:T(8,128)(2,1)S(1)}, u32[]{:S(2)}, u32[]{:S(2)}) collective-permute-start(bf16[512,256]{1,0:T(8,128)(2,1)} %copy-done.2), channel_id=1, source_target_pairs={{0,16},{16,0},{1,17},{17,1},{2,18},{18,2},{3,19},{19,3},{4,20},{20... | collective-permute-start | bytes 786440 | tf_op jit(solution)/shard_map/L_yq3/ppermute | solution.py:34
  100.5 14.7 %collective-permute-start.20 = (bf16[256,512]{1,0:T(8,128)(2,1)S(1)}, bf16[256,512]{1,0:T(8,128)(2,1)S(1)}, u32[]{:S(2)}, u32[]{:S(2)}) collective-permute-start(bf16[256,512]{1,0:T(8,128)(2,1)S(1)} %get-tuple-element.86.refs_0_), channel_id=1, source_target_pairs={{0,8},{4,12},{8,0},{12,4},{1,9},{5,13},{9,1},{13,5},{2,10},{6,14},... | collective-permute-start | bytes 786440 | tf_op jit(solution)/shard_map/L_m2/ppermute | solution.py:34
  102.6 5.9 %copy-start.1 = (bf16[1024,512]{1,0:T(8,128)(2,1)S(1)}, bf16[1024,512]{1,0:T(8,128)(2,1)}, u32[]{:S(2)}) copy-start(bf16[1024,512]{1,0:T(8,128)(2,1)} %refs_1_.3) | copy-start | bytes 3145732
  102.6 5.9 %copy-start.3 = (bf16[512,256]{1,0:T(8,128)(2,1)S(1)}, bf16[512,256]{1,0:T(8,128)(2,1)}, u32[]{:S(2)}) copy-start(bf16[512,256]{1,0:T(8,128)(2,1)} %copy-done.2) | copy-start | bytes 786436
  102.6 5.9 %copy-start.4 = (s32[8]{0:T(128)S(1)}, s32[8]{0:T(128)}, u32[]{:S(2)}) copy-start(s32[8]{0:T(128)} %segments.3) | copy-start | bytes 100
  117.7 7.8 %collective-permute-start.21 = (bf16[512,256]{1,0:T(8,128)(2,1)S(1)}, bf16[512,256]{1,0:T(8,128)(2,1)S(1)}, u32[]{:S(2)}, u32[]{:S(2)}) collective-permute-start(bf16[512,256]{1,0:T(8,128)(2,1)S(1)} %attend.2), channel_id=1, source_target_pairs={{0,4},{4,0},{8,12},{12,8},{1,5},{5,1},{9,13},{13,9},{2,6},{6,2},{1... | collective-permute-start | bytes 786440 | tf_op jit(solution)/shard_map/L_ctx/ppermute | solution.py:34

commit v8 on v6

--- a/solution.py
+++ b/solution.py
@@ -294,9 +294,9 @@
     rows_here, width = obuf.shape
     slots = rows_here // SEG
     count = mems[0].shape[0]
-    copies = []
+    copies, leaving = [], []
     for i, mem in enumerate(mems):
-        copies.append(pltpu.make_async_copy(mem, membuf.at[pl.ds(i * count, count), :], sems.at[1 + i]))
+        copies.append(pltpu.make_async_copy(mem, membuf.at[pl.ds(i * count, count), :], sems.at[i]))
         copies[-1].start()
     per_plane = count // 2
     mem_total = membuf.shape[0]
@@ -327,10 +327,11 @@
             numerator = sums[rows, ks] * factor
             numerator += jnp.dot(weights.astype(BF), membuf[:, vs], preferred_element_type=F32)
             obuf[rows, ks] = jnp.where(valid, numerator / denominator, 0.0).astype(BF)
-    dest = out if side else out.at[:, aligned(plane & 1, width)]
-    copy = pltpu.make_async_copy(obuf, dest, sems.at[0])
-    copy.start()
-    copy.wait()
+        dest = out.at[rows, :] if side else out.at[rows, aligned(plane & 1, width)]
+        leaving.append(pltpu.make_async_copy(obuf.at[rows, :], dest, sems.at[len(mems) + a]))
+        leaving[-1].start()
+    for copy in leaving:
+        copy.wait()
 
 
 def attend(side, planes, segments, length, state, mems):
@@ -345,7 +346,7 @@
         scratch_shapes=[
             pltpu.VMEM((mem_total, 2 * width), BF),
             pltpu.VMEM((rows, width), BF),
-            pltpu.SemaphoreType.DMA((1 + len(mems),)),
+            pltpu.SemaphoreType.DMA((rows // SEG + len(mems),)),
         ],
         compiler_params=pltpu.CompilerParams(vmem_limit_bytes=VMEM_LIMIT),
         cost_estimate=cost(4),

time: 127 us -> 127 us (level)
  no operation moved by 1% of the time
where the time goes in v8:
time: 127 us
  waiting for transfers between devices  68.6 us (54%)
  Pallas kernels  29.5 us (23%)
  starting transfers between devices  25.2 us (20%)
  local copies, waits for them, and re-layouts  2.58 us (2%)
    ppermute x22, waiting for transfers between devices, swap(): return lax.ppermute(value, axis, [(i, i ^ distance) for i in range(size)])  68.6 us
    ppermute x22, starting transfers between devices, swap(): return lax.ppermute(value, axis, [(i, i ^ distance) for i in range(size)])  25.2 us
    pallas_call x2, Pallas kernels, attend_local(): pl.pallas_call(functools.partial(local_kernel, side, planes, tensor_size,...  6.56 us
    pallas_call x2, Pallas kernels, attend(): pl.pallas_call(functools.partial(far_kernel, side, planes), out_shape=jax...  6.15 us
    pallas_call x1, Pallas kernels, project_tokens(): pl.pallas_call(functools.partial(tokens_kernel, tensor_size, sub_size), o...  5.83 us
    pallas_call x1, Pallas kernels, compress(): pl.pallas_call(compress_kernel, out_shape=jax.ShapeDtypeStruct((2 * count...  4.52 us
    pallas_call x1, Pallas kernels, project_memory(): pl.pallas_call(functools.partial(memory_kernel, planes, tensor_size, sub_...  3.53 us
    pallas_call x1, Pallas kernels, split_weights(): pl.pallas_call(split_kernel, out_shape=[jax.ShapeDtypeStruct(s, BF) for s...  2.89 us
  transfers between devices with their start and end apart: 22, of which 10 were waited for; matrix products, arithmetic and copies ran while one was open for 0% of the time, Pallas kernels for 21%

profile of v8, /device:TPU:0, one launch (start us, length us, event | category | flops | bytes accessed | tf_op | source)
XLA Modules:
  0.0 126.8 jit_solution(743467097017433428)
XLA Ops:
  0.0 3.0 %collective-permute-start = (bf16[512,1024]{1,0:T(8,128)(2,1)}, bf16[512,1024]{1,0:T(8,128)(2,1)}, u32[]{:S(2)}, u32[]{:S(2)}) collective-permute-start(bf16[512,1024]{1,0:T(8,128)(2,1)} %refs_0_.4), channel_id=1, source_target_pairs={{0,4},{4,0},{8,12},{12,8},{1,5},{5,1},{9,13},{13,9},{2,6},{6,2},{1... | collective-permute-start | bytes 3145736 | tf_op jit(solution)/shard_map/L_Xz/ppermute | solution.py:34
  3.0 1.5 %collective-permute-start.1 = (bf16[512,1024]{1,0:T(8,128)(2,1)}, bf16[512,1024]{1,0:T(8,128)(2,1)}, u32[]{:S(2)}, u32[]{:S(2)}) collective-permute-start(bf16[512,1024]{1,0:T(8,128)(2,1)} %refs_0_.4), channel_id=1, source_target_pairs={{0,2},{2,0},{1,3},{3,1},{4,6},{6,4},{5,7},{7,5},{8,10},{10,8},{9,1... | collective-permute-start | bytes 3145736 | tf_op jit(solution)/shard_map/L_Ax1/ppermute | solution.py:34
  4.5 0.0 collective-permute-start.2
  4.5 2.9 %split_weights.1 = (bf16[512,512]{1,0:T(8,128)(2,1)}, bf16[512,512]{1,0:T(8,128)(2,1)}, bf16[512,256]{1,0:T(8,128)(2,1)}, bf16[512,256]{1,0:T(8,128)(2,1)}, bf16[1024,256]{1,0:T(8,128)(2,1)}) custom-call(bf16[1024,512]{1,0:T(8,128)(2,1)} %refs_0_.3, bf16[1024,512]{1,0:T(8,128)(2,1)} %refs_1_.2, bf16[1024,512]{1,0:T(8,128)(2,1)} %refs_1_.3), custom_call_target="tpu_custom_call" | custom-call | flops 2000000000 | bytes 1000 | tf_op jit(solution)/shard_map/split_weights/pallas_call | solution.py:74
  7.4 2.7 %collective-permute-start.3 = (bf16[512,512]{1,0:T(8,128)(2,1)}, bf16[512,512]{1,0:T(8,128)(2,1)S(1)}, u32[]{:S(2)}, u32[]{:S(2)}) collective-permute-start(bf16[512,512]{1,0:T(8,128)(2,1)} %get-tuple-element.50), channel_id=1, source_target_pairs={{0,8},{4,12},{8,0},{12,4},{1,9},{5,13},{9,1},{13,5},{2,10},{6,14},... | collective-permute-start | bytes 1572872 | tf_op jit(solution)/shard_map/L_kv2/ppermute | solution.py:34
  10.1 26.9 %collective-permute-done.3.refs_3_ = bf16[512,512]{1,0:T(8,128)(2,1)S(1)} collective-permute-done((bf16[512,512]{1,0:T(8,128)(2,1)}, bf16[512,512]{1,0:T(8,128)(2,1)S(1)}, u32[]{:S(2)}, u32[]{:S(2)}) %collective-permute-start.3) | collective-permute-done | bytes 524320 | tf_op jit(solution)/shard_map/L_kv2/ppermute | solution.py:34
  37.0 0.7 collective-permute-done.partner_ref.refs_4_
  37.7 0.0 collective-permute-done.1.refs_2_
  37.7 0.0 collective-permute-done.2.refs_1_
  37.7 1.7 %collective-permute-start.4 = (bf16[512,1024]{1,0:T(8,128)(2,1)}, bf16[512,1024]{1,0:T(8,128)(2,1)}, u32[]{:S(2)}, u32[]{:S(2)}) collective-permute-start(bf16[512,1024]{1,0:T(8,128)(2,1)} %collective-permute-done.partner_ref.refs_4_), channel_id=1, source_target_pairs={{0,2},{2,0},{1,3},{3,1},{4,6},{6,4},{5,7},{7,5},{8,10},{10,8},{9,1... | collective-permute-start | bytes 3145736 | tf_op jit(solution)/shard_map/L_Bx1/ppermute | solution.py:34
  39.4 3.6 %collective-permute-start.5 = (bf16[512,512]{1,0:T(8,128)(2,1)}, bf16[512,512]{1,0:T(8,128)(2,1)S(1)}, u32[]{:S(2)}, u32[]{:S(2)}) collective-permute-start(bf16[512,512]{1,0:T(8,128)(2,1)} %get-tuple-element.57), channel_id=1, source_target_pairs={{0,12},{4,8},{8,4},{12,0},{1,13},{5,9},{9,5},{13,1},{2,14},{6,10},... | collective-permute-start | bytes 1572872 | tf_op jit(solution)/shard_map/L_kv3/ppermute | solution.py:34
  43.0 0.0 collective-permute-start.6
  43.0 1.5 %collective-permute-start.7 = (bf16[512,512]{1,0:T(8,128)(2,1)S(1)}, bf16[512,512]{1,0:T(8,128)(2,1)S(1)}, u32[]{:S(2)}, u32[]{:S(2)}) collective-permute-start(bf16[512,512]{1,0:T(8,128)(2,1)S(1)} %collective-permute-done.3.refs_3_), channel_id=1, source_target_pairs={{0,16},{16,0},{1,17},{17,1},{2,18},{18,2},{3,19},{19,3},{4,20},{20... | collective-permute-start | bytes 1572872 | tf_op jit(solution)/shard_map/L_ykv2/ppermute | solution.py:34
  44.5 4.5 %compress.1.refs_7_ = bf16[256,1024]{1,0:T(8,128)(2,1)} custom-call(bf16[512,1024]{1,0:T(8,128)(2,1)} %refs_0_.4, bf16[512,1024]{1,0:T(8,128)(2,1)} %collective-permute-done.partner_ref.refs_4_, bf16[512,1024]{1,0:T(8,128)(2,1)} %w_ref.1), custom_call_target="tpu_custom_call" | custom-call | flops 5000000000 | bytes 1000 | tf_op jit(solution)/shard_map/compress/pallas_call | solution.py:106
  49.1 0.1 collective-permute-start.8
  49.1 7.2 %collective-permute-done.5.refs_4_ = bf16[512,512]{1,0:T(8,128)(2,1)S(1)} collective-permute-done((bf16[512,512]{1,0:T(8,128)(2,1)}, bf16[512,512]{1,0:T(8,128)(2,1)S(1)}, u32[]{:S(2)}, u32[]{:S(2)}) %collective-permute-start.5) | collective-permute-done | bytes 524320 | tf_op jit(solution)/shard_map/L_kv3/ppermute | solution.py:34
  56.3 9.0 %collective-permute-done.6.refs_2_ = bf16[512,512]{1,0:T(8,128)(2,1)S(1)} collective-permute-done((bf16[512,512]{1,0:T(8,128)(2,1)}, bf16[512,512]{1,0:T(8,128)(2,1)S(1)}, u32[]{:S(2)}, u32[]{:S(2)}) %collective-permute-start.6) | collective-permute-done | bytes 524320 | tf_op jit(solution)/shard_map/L_kv1/ppermute | solution.py:34
  65.3 0.0 collective-permute-done.7.refs_5_
  65.3 0.0 collective-permute-done.8.refs_8_
  65.3 0.0 copy-start.8
  65.3 0.9 copy-done.8
  66.2 0.0 collective-permute-done.4.refs_6_
  66.2 0.1 pad_maximum_fusion
  66.3 1.6 %collective-permute-start.12 = (bf16[1024,512]{1,0:T(8,128)(2,1)S(1)}, bf16[1024,512]{1,0:T(8,128)(2,1)S(1)}, u32[]{:S(2)}, u32[]{:S(2)}) collective-permute-start(bf16[1024,512]{1,0:T(8,128)(2,1)S(1)} %pad_maximum_fusion), channel_id=1, source_target_pairs={{0,16},{16,0},{1,17},{17,1},{2,18},{18,2},{3,19},{19,3},{4,20},{20... | collective-permute-start | bytes 3145736 | tf_op jit(solution)/shard_map/L_ykv/ppermute | solution.py:34
  67.9 0.0 copy-done.9
  67.9 1.7 %collective-permute-start.11 = (bf16[1024,256]{1,0:T(8,128)(2,1)S(1)}, bf16[1024,256]{1,0:T(8,128)(2,1)S(1)}, u32[]{:S(2)}, u32[]{:S(2)}) collective-permute-start(bf16[1024,256]{1,0:T(8,128)(2,1)S(1)} %copy-done.9), channel_id=1, source_target_pairs={{0,4},{4,0},{8,12},{12,8},{1,5},{5,1},{9,13},{13,9},{2,6},{6,2},{1... | collective-permute-start | bytes 1572872 | tf_op jit(solution)/shard_map/L_q1/ppermute | solution.py:34
  69.6 0.5 collective-permute-start.13
  70.1 0.5 collective-permute-start.9
  70.6 2.2 %collective-permute-start.10 = (bf16[512,256]{1,0:T(8,128)(2,1)S(1)}, bf16[512,256]{1,0:T(8,128)(2,1)S(1)}, u32[]{:S(2)}, u32[]{:S(2)}) collective-permute-start(bf16[512,256]{1,0:T(8,128)(2,1)S(1)} %copy-done.10), channel_id=1, source_target_pairs={{0,12},{4,8},{8,4},{12,0},{1,13},{5,9},{9,5},{13,1},{2,14},{6,10},... | collective-permute-start | bytes 786440 | tf_op jit(solution)/shard_map/L_q3/ppermute | solution.py:34
  72.8 14.8 %collective-permute-done.9.refs_3_ = bf16[512,256]{1,0:T(8,128)(2,1)S(1)} collective-permute-done((bf16[512,256]{1,0:T(8,128)(2,1)S(1)}, bf16[512,256]{1,0:T(8,128)(2,1)S(1)}, u32[]{:S(2)}, u32[]{:S(2)}) %collective-permute-start.9) | collective-permute-done | bytes 262176 | tf_op jit(solution)/shard_map/L_q2/ppermute | solution.py:34
  87.6 0.0 collective-permute-start.16
  87.6 4.3 %collective-permute-done.10.refs_4_ = bf16[512,256]{1,0:T(8,128)(2,1)S(1)} collective-permute-done((bf16[512,256]{1,0:T(8,128)(2,1)S(1)}, bf16[512,256]{1,0:T(8,128)(2,1)S(1)}, u32[]{:S(2)}, u32[]{:S(2)}) %collective-permute-start.10) | collective-permute-done | bytes 262176 | tf_op jit(solution)/shard_map/L_q3/ppermute | solution.py:34
  91.9 0.0 collective-permute-start.17
  91.9 0.8 collective-permute-done.11.refs_2_
  92.7 0.0 collective-permute-start.18
  92.7 0.0 collective-permute-done.13.refs_9_
  92.7 0.0 collective-permute-done.12.refs_6_
  92.7 1.0 copy-done.5
  93.6 0.5 collective-permute-start.19
  94.8 0.0 copy-start
  94.8 0.6 collective-permute-start.14
  95.4 1.7 %collective-permute-done.19.refs_10_ = bf16[256,1024]{1,0:T(8,128)(2,1)} collective-permute-done((bf16[256,1024]{1,0:T(8,128)(2,1)}, bf16[256,1024]{1,0:T(8,128)(2,1)}, u32[]{:S(2)}, u32[]{:S(2)}) %collective-permute-start.19) | collective-permute-done | bytes 524320 | tf_op jit(solution)/shard_map/L_C1c1/ppermute | solution.py:34
  97.1 0.5 collective-permute-start.15
  97.6 3.5 %project_memory.1 = (bf16[256,512]{1,0:T(8,128)(2,1)S(1)}, bf16[4096,512]{1,0:T(8,128)(2,1)S(1)}) custom-call(bf16[1024,512]{1,0:T(8,128)(2,1)} %refs_0_.3, bf16[1024,512]{1,0:T(8,128)(2,1)} %refs_1_.2, bf16[512,512]{1,0:T(8,128)(2,1)S(1)} %collective-permute-done.6.refs_2_, bf16[512,512]{1,0:T(8,128)(2,1)S(1)} %collective-permute-done.3.refs_3_, ...), custom_call_target="tpu_custom_call" | custom-call | flops 4000000000 | bytes 1000 | tf_op jit(solution)/shard_map/project_memory/pallas_call | solution.py:178
  101.2 0.0 collective-permute-done.16.refs_3_
  101.2 2.7 %collective-permute-start.20 = (bf16[256,512]{1,0:T(8,128)(2,1)S(1)}, bf16[256,512]{1,0:T(8,128)(2,1)S(1)}, u32[]{:S(2)}, u32[]{:S(2)}) collective-permute-start(bf16[256,512]{1,0:T(8,128)(2,1)S(1)} %get-tuple-element.86.refs_0_), channel_id=1, source_target_pairs={{0,8},{4,12},{8,0},{12,4},{1,9},{5,13},{9,1},{13,5},{2,10},{6,14},... | collective-permute-start | bytes 786440 | tf_op jit(solution)/shard_map/L_m2/ppermute | solution.py:34
  103.9 0.0 collective-permute-done.17.refs_5_
  103.9 0.0 collective-permute-done.18.refs_7_
  103.9 0.0 copy-start.1
  103.9 0.0 copy-start.4
  103.9 5.8 %project_tokens.1 = (bf16[1024,512]{1,0:T(8,128)(2,1)S(1)}, bf16[4,1024,1024]{2,1,0:T(8,128)(2,1)S(1)}) custom-call(bf16[512,1024]{1,0:T(8,128)(2,1)S(1)} %copy-done, bf16[512,1024]{1,0:T(8,128)(2,1)S(1)} %collective-permute-done.2.refs_1_, bf16[512,1024]{1,0:T(8,128)(2,1)} %collective-permute-done.1.refs_2_, ...), custom_call_target="tpu_custom_call" | custom-call | flops 6000000000 | bytes 1000 | tf_op jit(solution)/shard_map/project_tokens/pallas_call | solution.py:222
  109.8 0.0 collective-permute-done.14.refs_5_
  109.8 0.0 collective-permute-done.15.refs_6_
  109.8 0.0 copy-done.1
  109.8 0.0 copy-done.3
  109.8 0.0 copy-done.4
  109.8 3.4 %attend_local.2 = (bf16[512,256]{1,0:T(8,128)(2,1)S(1)}, f32[512,256]{1,0:T(8,128)S(1)}, f32[512,256]{1,0:T(8,128)S(1)}, f32[512,256]{1,0:T(8,128)S(1)}, bf16[4096,256]{1,0:T(8,128)(2,1)S(1)}) custom-call(s32[8]{0:T(128)S(1)} %copy-done.4, bf16[1024,512]{1,0:T(8,128)(2,1)S(1)} %copy-done.1, bf16[1024,256]{1,0:T(8,128)(2,1)S(1)} %collective-permute-done.11.refs_2_, ...), custom_call_target="tpu_custom_call" | custom-call | flops 4000000000 | bytes 1000 | tf_op jit(solution)/shard_map/attend_local/pallas_call | solution.py:279
  113.2 2.6 %collective-permute-done.20.refs_1_ = bf16[256,512]{1,0:T(8,128)(2,1)S(1)} collective-permute-done((bf16[256,512]{1,0:T(8,128)(2,1)S(1)}, bf16[256,512]{1,0:T(8,128)(2,1)S(1)}, u32[]{:S(2)}, u32[]{:S(2)}) %collective-permute-start.20) | collective-permute-done | bytes 262176 | tf_op jit(solution)/shard_map/L_m2/ppermute | solution.py:34
  115.8 3.0 %attend.2 = bf16[512,256]{1,0:T(8,128)(2,1)S(1)} custom-call(s32[8]{0:T(128)S(1)} %copy-done.4, s32[1]{0:T(128)S(6)} %copy.9.length, bf16[512,256]{1,0:T(8,128)(2,1)S(1)} %get-tuple-element.82.queries, f32[512,256]{1,0:T(8,128)S(1)} %get-tuple-element.83.sums, f32[512,256]{1,0:T(8,128)S(1)} %get-tuple-element.84.largest, ...), custom_call_target="tpu_custom_call" | custom-call | flops 4000000000 | bytes 1000 | tf_op jit(solution)/shard_map/attend/pallas_call | solution.py:341
  118.8 0.4 collective-permute-start.21
  119.2 3.2 %attend_local.3 = (bf16[512,256]{1,0:T(8,128)(2,1)S(1)}, f32[512,256]{1,0:T(8,128)S(1)}, f32[512,256]{1,0:T(8,128)S(1)}, f32[512,256]{1,0:T(8,128)S(1)}) custom-call(s32[8]{0:T(128)S(1)} %copy-done.4, bf16[4096,256]{1,0:T(8,128)(2,1)S(1)} %get-tuple-element.88.refs_1_, bf16[4,1024,1024]{2,1,0:T(8,128)(2,1)S(1)} %get-tuple-element.80.refs_7_.refs_2_, ...), custom_call_target="tpu_custom_call" | custom-call | flops 4000000000 | bytes 1000 | tf_op jit(solution)/shard_map/attend_local/pallas_call | solution.py:279
  122.4 3.2 %attend.3 = bf16[512,512]{1,0:T(8,128)(2,1)} custom-call(s32[8]{0:T(128)S(1)} %copy-done.4, s32[1]{0:T(128)S(6)} %copy.9.length, bf16[512,256]{1,0:T(8,128)(2,1)S(1)} %get-tuple-element.89.queries, f32[512,256]{1,0:T(8,128)S(1)} %get-tuple-element.90.sums, f32[512,256]{1,0:T(8,128)S(1)} %get-tuple-element.91.largest, ...), custom_call_target="tpu_custom_call" | custom-call | flops 4000000000 | bytes 1000 | tf_op jit(solution)/shard_map/attend/pallas_call | solution.py:341
  125.6 0.5 collective-permute-done.21
  126.1 0.7 constant_dynamic-update-slice_fusion
  (14 shorter events, 0.0 us)
Async XLA Ops:
  0.0 37.7 %collective-permute-start = (bf16[512,1024]{1,0:T(8,128)(2,1)}, bf16[512,1024]{1,0:T(8,128)(2,1)}, u32[]{:S(2)}, u32[]{:S(2)}) collective-permute-start(bf16[512,1024]{1,0:T(8,128)(2,1)} %refs_0_.4), channel_id=1, source_target_pairs={{0,4},{4,0},{8,12},{12,8},{1,5},{5,1},{9,13},{13,9},{2,6},{6,2},{1... | collective-permute-start | bytes 3145736 | tf_op jit(solution)/shard_map/L_Xz/ppermute | solution.py:34
  3.0 34.7 %collective-permute-start.1 = (bf16[512,1024]{1,0:T(8,128)(2,1)}, bf16[512,1024]{1,0:T(8,128)(2,1)}, u32[]{:S(2)}, u32[]{:S(2)}) collective-permute-start(bf16[512,1024]{1,0:T(8,128)(2,1)} %refs_0_.4), channel_id=1, source_target_pairs={{0,2},{2,0},{1,3},{3,1},{4,6},{6,4},{5,7},{7,5},{8,10},{10,8},{9,1... | collective-permute-start | bytes 3145736 | tf_op jit(solution)/shard_map/L_Ax1/ppermute | solution.py:34
  4.5 33.2 %collective-permute-start.2 = (bf16[512,1024]{1,0:T(8,128)(2,1)}, bf16[512,1024]{1,0:T(8,128)(2,1)S(1)}, u32[]{:S(2)}, u32[]{:S(2)}) collective-permute-start(bf16[512,1024]{1,0:T(8,128)(2,1)} %refs_0_.4), channel_id=1, source_target_pairs={{0,1},{1,0},{2,3},{3,2},{4,5},{5,4},{6,7},{7,6},{8,9},{9,8},{10,11... | collective-permute-start | bytes 3145736 | tf_op jit(solution)/shard_map/L_A0c1/ppermute | solution.py:34
  7.4 29.6 %collective-permute-start.3 = (bf16[512,512]{1,0:T(8,128)(2,1)}, bf16[512,512]{1,0:T(8,128)(2,1)S(1)}, u32[]{:S(2)}, u32[]{:S(2)}) collective-permute-start(bf16[512,512]{1,0:T(8,128)(2,1)} %get-tuple-element.50), channel_id=1, source_target_pairs={{0,8},{4,12},{8,0},{12,4},{1,9},{5,13},{9,1},{13,5},{2,10},{6,14},... | collective-permute-start | bytes 1572872 | tf_op jit(solution)/shard_map/L_kv2/ppermute | solution.py:34
  37.7 28.5 %collective-permute-start.4 = (bf16[512,1024]{1,0:T(8,128)(2,1)}, bf16[512,1024]{1,0:T(8,128)(2,1)}, u32[]{:S(2)}, u32[]{:S(2)}) collective-permute-start(bf16[512,1024]{1,0:T(8,128)(2,1)} %collective-permute-done.partner_ref.refs_4_), channel_id=1, source_target_pairs={{0,2},{2,0},{1,3},{3,1},{4,6},{6,4},{5,7},{7,5},{8,10},{10,8},{9,1... | collective-permute-start | bytes 3145736 | tf_op jit(solution)/shard_map/L_Bx1/ppermute | solution.py:34
  39.4 16.9 %collective-permute-start.5 = (bf16[512,512]{1,0:T(8,128)(2,1)}, bf16[512,512]{1,0:T(8,128)(2,1)S(1)}, u32[]{:S(2)}, u32[]{:S(2)}) collective-permute-start(bf16[512,512]{1,0:T(8,128)(2,1)} %get-tuple-element.57), channel_id=1, source_target_pairs={{0,12},{4,8},{8,4},{12,0},{1,13},{5,9},{9,5},{13,1},{2,14},{6,10},... | collective-permute-start | bytes 1572872 | tf_op jit(solution)/shard_map/L_kv3/ppermute | solution.py:34
  43.0 22.3 %collective-permute-start.6 = (bf16[512,512]{1,0:T(8,128)(2,1)}, bf16[512,512]{1,0:T(8,128)(2,1)S(1)}, u32[]{:S(2)}, u32[]{:S(2)}) collective-permute-start(bf16[512,512]{1,0:T(8,128)(2,1)} %get-tuple-element.57), channel_id=1, source_target_pairs={{0,4},{4,0},{8,12},{12,8},{1,5},{5,1},{9,13},{13,9},{2,6},{6,2},{1... | collective-permute-start | bytes 1572872 | tf_op jit(solution)/shard_map/L_kv1/ppermute | solution.py:34
  43.0 22.3 %collective-permute-start.7 = (bf16[512,512]{1,0:T(8,128)(2,1)S(1)}, bf16[512,512]{1,0:T(8,128)(2,1)S(1)}, u32[]{:S(2)}, u32[]{:S(2)}) collective-permute-start(bf16[512,512]{1,0:T(8,128)(2,1)S(1)} %collective-permute-done.3.refs_3_), channel_id=1, source_target_pairs={{0,16},{16,0},{1,17},{17,1},{2,18},{18,2},{3,19},{19,3},{4,20},{20... | collective-permute-start | bytes 1572872 | tf_op jit(solution)/shard_map/L_ykv2/ppermute | solution.py:34
  49.0 18.8 %copy-start.9 = (bf16[1024,256]{1,0:T(8,128)(2,1)S(1)}, bf16[1024,256]{1,0:T(8,128)(2,1)}, u32[]{:S(2)}) copy-start(bf16[1024,256]{1,0:T(8,128)(2,1)} %get-tuple-element.67) | copy-start | bytes 1572868
  49.0 20.5 %copy-start.7 = (bf16[256,1024]{1,0:T(8,128)(2,1)S(1)}, bf16[256,1024]{1,0:T(8,128)(2,1)}, u32[]{:S(2)}) copy-start(bf16[256,1024]{1,0:T(8,128)(2,1)} %compress.1.refs_7_) | copy-start | bytes 1572868
  49.1 21.0 %copy-start.11 = (bf16[512,256]{1,0:T(8,128)(2,1)S(1)}, bf16[512,256]{1,0:T(8,128)(2,1)}, u32[]{:S(2)}) copy-start(bf16[512,256]{1,0:T(8,128)(2,1)} %get-tuple-element.63) | copy-start | bytes 786436
  49.1 21.6 %copy-start.10 = (bf16[512,256]{1,0:T(8,128)(2,1)S(1)}, bf16[512,256]{1,0:T(8,128)(2,1)}, u32[]{:S(2)}) copy-start(bf16[512,256]{1,0:T(8,128)(2,1)} %get-tuple-element.65) | copy-start | bytes 786436
  49.1 16.3 %collective-permute-start.8 = (bf16[256,1024]{1,0:T(8,128)(2,1)}, bf16[256,1024]{1,0:T(8,128)(2,1)S(1)}, u32[]{:S(2)}, u32[]{:S(2)}) collective-permute-start(bf16[256,1024]{1,0:T(8,128)(2,1)} %compress.1.refs_7_), channel_id=1, source_target_pairs={{0,1},{1,0},{2,3},{3,2},{4,5},{5,4},{6,7},{7,6},{8,9},{9,8},{10,11... | collective-permute-start | bytes 1572872 | tf_op jit(solution)/shard_map/L_C0c1/ppermute | solution.py:34
  65.3 2.5 %copy-start.6 = (bf16[512,512]{1,0:T(8,128)(2,1)}, bf16[512,512]{1,0:T(8,128)(2,1)S(1)}, u32[]{:S(2)}) copy-start(bf16[512,512]{1,0:T(8,128)(2,1)S(1)} %collective-permute-done.7.refs_5_) | copy-start | bytes 1572868
  65.3 0.9 copy-start.8
  66.3 26.4 %collective-permute-start.12 = (bf16[1024,512]{1,0:T(8,128)(2,1)S(1)}, bf16[1024,512]{1,0:T(8,128)(2,1)S(1)}, u32[]{:S(2)}, u32[]{:S(2)}) collective-permute-start(bf16[1024,512]{1,0:T(8,128)(2,1)S(1)} %pad_maximum_fusion), channel_id=1, source_target_pairs={{0,16},{16,0},{1,17},{17,1},{2,18},{18,2},{3,19},{19,3},{4,20},{20... | collective-permute-start | bytes 3145736 | tf_op jit(solution)/shard_map/L_ykv/ppermute | solution.py:34
  67.9 24.8 %collective-permute-start.11 = (bf16[1024,256]{1,0:T(8,128)(2,1)S(1)}, bf16[1024,256]{1,0:T(8,128)(2,1)S(1)}, u32[]{:S(2)}, u32[]{:S(2)}) collective-permute-start(bf16[1024,256]{1,0:T(8,128)(2,1)S(1)} %copy-done.9), channel_id=1, source_target_pairs={{0,4},{4,0},{8,12},{12,8},{1,5},{5,1},{9,13},{13,9},{2,6},{6,2},{1... | collective-permute-start | bytes 1572872 | tf_op jit(solution)/shard_map/L_q1/ppermute | solution.py:34
  69.6 23.1 %collective-permute-start.13 = (bf16[256,1024]{1,0:T(8,128)(2,1)S(1)}, bf16[256,1024]{1,0:T(8,128)(2,1)}, u32[]{:S(2)}, u32[]{:S(2)}) collective-permute-start(bf16[256,1024]{1,0:T(8,128)(2,1)S(1)} %copy-done.7), channel_id=1, source_target_pairs={{0,2},{2,0},{1,3},{3,1},{4,6},{6,4},{5,7},{7,5},{8,10},{10,8},{9,1... | collective-permute-start | bytes 1572872 | tf_op jit(solution)/shard_map/L_Cx1/ppermute | solution.py:34
  70.1 17.5 %collective-permute-start.9 = (bf16[512,256]{1,0:T(8,128)(2,1)S(1)}, bf16[512,256]{1,0:T(8,128)(2,1)S(1)}, u32[]{:S(2)}, u32[]{:S(2)}) collective-permute-start(bf16[512,256]{1,0:T(8,128)(2,1)S(1)} %copy-done.11), channel_id=1, source_target_pairs={{0,8},{4,12},{8,0},{12,4},{1,9},{5,13},{9,1},{13,5},{2,10},{6,14},... | collective-permute-start | bytes 786440 | tf_op jit(solution)/shard_map/L_q2/ppermute | solution.py:34
  70.6 21.2 %collective-permute-start.10 = (bf16[512,256]{1,0:T(8,128)(2,1)S(1)}, bf16[512,256]{1,0:T(8,128)(2,1)S(1)}, u32[]{:S(2)}, u32[]{:S(2)}) collective-permute-start(bf16[512,256]{1,0:T(8,128)(2,1)S(1)} %copy-done.10), channel_id=1, source_target_pairs={{0,12},{4,8},{8,4},{12,0},{1,13},{5,9},{9,5},{13,1},{2,14},{6,10},... | collective-permute-start | bytes 786440 | tf_op jit(solution)/shard_map/L_q3/ppermute | solution.py:34
  87.6 13.6 %collective-permute-start.16 = (bf16[512,1024]{1,0:T(8,128)(2,1)}, bf16[512,1024]{1,0:T(8,128)(2,1)}, u32[]{:S(2)}, u32[]{:S(2)}) collective-permute-start(bf16[512,1024]{1,0:T(8,128)(2,1)} %collective-permute-done.1.refs_2_), channel_id=1, source_target_pairs={{0,1},{1,0},{2,3},{3,2},{4,5},{5,4},{6,7},{7,6},{8,9},{9,8},{10,11... | collective-permute-start | bytes 3145736 | tf_op jit(solution)/shard_map/L_A1c1/ppermute | solution.py:34
  91.9 0.8 copy-start.2
  91.9 12.0 %collective-permute-start.17 = (bf16[512,1024]{1,0:T(8,128)(2,1)}, bf16[512,1024]{1,0:T(8,128)(2,1)}, u32[]{:S(2)}, u32[]{:S(2)}) collective-permute-start(bf16[512,1024]{1,0:T(8,128)(2,1)} %collective-permute-done.partner_ref.refs_4_), channel_id=1, source_target_pairs={{0,1},{1,0},{2,3},{3,2},{4,5},{5,4},{6,7},{7,6},{8,9},{9,8},{10,11... | collective-permute-start | bytes 3145736 | tf_op jit(solution)/shard_map/L_B0c1/ppermute | solution.py:34
  92.7 11.2 %collective-permute-start.18 = (bf16[512,1024]{1,0:T(8,128)(2,1)}, bf16[512,1024]{1,0:T(8,128)(2,1)}, u32[]{:S(2)}, u32[]{:S(2)}) collective-permute-start(bf16[512,1024]{1,0:T(8,128)(2,1)} %collective-permute-done.4.refs_6_), channel_id=1, source_target_pairs={{0,1},{1,0},{2,3},{3,2},{4,5},{5,4},{6,7},{7,6},{8,9},{9,8},{10,11... | collective-permute-start | bytes 3145736 | tf_op jit(solution)/shard_map/L_B1c1/ppermute | solution.py:34
  92.7 1.0 copy-start.5
  93.6 3.5 %collective-permute-start.19 = (bf16[256,1024]{1,0:T(8,128)(2,1)}, bf16[256,1024]{1,0:T(8,128)(2,1)}, u32[]{:S(2)}, u32[]{:S(2)}) collective-permute-start(bf16[256,1024]{1,0:T(8,128)(2,1)} %collective-permute-done.13.refs_9_), channel_id=1, source_target_pairs={{0,1},{1,0},{2,3},{3,2},{4,5},{5,4},{6,7},{7,6},{8,9},{9,8},{10,11... | collective-permute-start | bytes 1572872 | tf_op jit(solution)/shard_map/L_C1c1/ppermute | solution.py:34
  94.8 9.1 %copy-start = (bf16[512,1024]{1,0:T(8,128)(2,1)S(1)}, bf16[512,1024]{1,0:T(8,128)(2,1)}, u32[]{:S(2)}) copy-start(bf16[512,1024]{1,0:T(8,128)(2,1)} %refs_0_.4) | copy-start | bytes 3145732
  94.8 15.0 %collective-permute-start.14 = (bf16[512,256]{1,0:T(8,128)(2,1)S(1)}, bf16[512,256]{1,0:T(8,128)(2,1)S(1)}, u32[]{:S(2)}, u32[]{:S(2)}) collective-permute-start(bf16[512,256]{1,0:T(8,128)(2,1)S(1)} %collective-permute-done.9.refs_3_), channel_id=1, source_target_pairs={{0,16},{16,0},{1,17},{17,1},{2,18},{18,2},{3,19},{19,3},{4,20},{20... | collective-permute-start | bytes 786440 | tf_op jit(solution)/shard_map/L_yq2/ppermute | solution.py:34
  97.1 12.7 %collective-permute-start.15 = (bf16[512,256]{1,0:T(8,128)(2,1)}, bf16[512,256]{1,0:T(8,128)(2,1)S(1)}, u32[]{:S(2)}, u32[]{:S(2)}) collective-permute-start(bf16[512,256]{1,0:T(8,128)(2,1)} %copy-done.2), channel_id=1, source_target_pairs={{0,16},{16,0},{1,17},{17,1},{2,18},{18,2},{3,19},{19,3},{4,20},{20... | collective-permute-start | bytes 786440 | tf_op jit(solution)/shard_map/L_yq3/ppermute | solution.py:34
  101.2 14.7 %collective-permute-start.20 = (bf16[256,512]{1,0:T(8,128)(2,1)S(1)}, bf16[256,512]{1,0:T(8,128)(2,1)S(1)}, u32[]{:S(2)}, u32[]{:S(2)}) collective-permute-start(bf16[256,512]{1,0:T(8,128)(2,1)S(1)} %get-tuple-element.86.refs_0_), channel_id=1, source_target_pairs={{0,8},{4,12},{8,0},{12,4},{1,9},{5,13},{9,1},{13,5},{2,10},{6,14},... | collective-permute-start | bytes 786440 | tf_op jit(solution)/shard_map/L_m2/ppermute | solution.py:34
  103.9 5.9 %copy-start.1 = (bf16[1024,512]{1,0:T(8,128)(2,1)S(1)}, bf16[1024,512]{1,0:T(8,128)(2,1)}, u32[]{:S(2)}) copy-start(bf16[1024,512]{1,0:T(8,128)(2,1)} %refs_1_.3) | copy-start | bytes 3145732
  103.9 5.9 %copy-start.3 = (bf16[512,256]{1,0:T(8,128)(2,1)S(1)}, bf16[512,256]{1,0:T(8,128)(2,1)}, u32[]{:S(2)}) copy-start(bf16[512,256]{1,0:T(8,128)(2,1)} %copy-done.2) | copy-start | bytes 786436
  103.9 5.9 %copy-start.4 = (s32[8]{0:T(128)S(1)}, s32[8]{0:T(128)}, u32[]{:S(2)}) copy-start(s32[8]{0:T(128)} %segments.3) | copy-start | bytes 100
  118.8 7.3 %collective-permute-start.21 = (bf16[512,256]{1,0:T(8,128)(2,1)S(1)}, bf16[512,256]{1,0:T(8,128)(2,1)S(1)}, u32[]{:S(2)}, u32[]{:S(2)}) collective-permute-start(bf16[512,256]{1,0:T(8,128)(2,1)S(1)} %attend.2), channel_id=1, source_target_pairs={{0,4},{4,0},{8,12},{12,8},{1,5},{5,1},{9,13},{13,9},{2,6},{6,2},{1... | collective-permute-start | bytes 786440 | tf_op jit(solution)/shard_map/L_ctx/ppermute | solution.py:34
